TPU v7x, 32 devices: a whole 2x2x4 slice. The times are simulated.
32 devices in a mesh: ctx: 16 (over z, y, x), fsdp: 2 (over core).
Axes of the slice: x: 2, y: 2, z: 4, core: 2. Of those that a mesh axis runs over, the one named last changes fastest.
Arguments:
- layer_input: bfloat16 [2, 2048, 2048], P('fsdp', 'ctx'), may hold values from -6 to 6
- block_table: int32 [2, 16, 2], P('fsdp'), may hold values from 0 to 31, as said below
- attn_gain: bfloat16 [2048], P(('ctx', 'fsdp')), may hold values from 0.25 to 1.75
- query_weight: bfloat16 [2048, 2048], P(('ctx', 'fsdp')), may hold values from -0.125 to 0.125
- key_weight: bfloat16 [2048, 2048], P(('ctx', 'fsdp')), may hold values from -0.125 to 0.125
- value_weight: bfloat16 [2048, 2048], P(('ctx', 'fsdp')), may hold values from -0.125 to 0.125
- out_weight: bfloat16 [2048, 2048], P(('ctx', 'fsdp')), may hold values from -3 to 3
- mlp_gain: bfloat16 [2048], P(('ctx', 'fsdp')), may hold values from 0.25 to 1.75
- gate_weight: bfloat16 [2048, 8192], P(('ctx', 'fsdp')), may hold values from -0.125 to 0.125
- up_weight: bfloat16 [2048, 8192], P(('ctx', 'fsdp')), may hold values from -0.125 to 0.125
- down_weight: bfloat16 [2048, 8192], P(('ctx', 'fsdp')), may hold values from -0.0625 to 0.0625
- cotangent: bfloat16 [2, 2048, 2048], P('fsdp', 'ctx'), may hold values from -6 to 6
Outputs:
- layer_output: bfloat16 [2, 2048, 2048], P('fsdp', 'ctx')
- input_grad: float32 [2, 2048, 2048], P('fsdp', 'ctx')
- attn_gain_grad: float32 [2048], P(('ctx', 'fsdp'))
- query_weight_grad: float32 [2048, 2048], P(('ctx', 'fsdp'))
- key_weight_grad: float32 [2048, 2048], P(('ctx', 'fsdp'))
- value_weight_grad: float32 [2048, 2048], P(('ctx', 'fsdp'))
- out_weight_grad: float32 [2048, 2048], P(('ctx', 'fsdp'))
- mlp_gain_grad: float32 [2048], P(('ctx', 'fsdp'))
- gate_weight_grad: float32 [2048, 8192], P(('ctx', 'fsdp'))
- up_weight_grad: float32 [2048, 8192], P(('ctx', 'fsdp'))
- down_weight_grad: float32 [2048, 8192], P(('ctx', 'fsdp'))
Inputs may be any that keep to these rules, and one draw needn't show every extreme that they name: For each sequence s and ctx index c, block_table[s, c] holds two block numbers b and 31 - b, in either order; each block number appears exactly once in a sequence's table. Rows of layer_input and cotangent follow the table: ctx index c holds the 64 positions of its first block, then those of its second.
All inputs are finite; a program needn't handle non-finite values.
Results may differ from a plain program's by a relative error of at most 0.035.
Values may be sent and summed in bfloat16 or wider, within the bound.
A program may use at most 704 MiB of HBM per device.

v0:
```python
import jax
import jax.numpy as jnp
from jax import lax
from jax.sharding import PartitionSpec as P

HEADS = 32
HD = 64


EPSILON = 1e-05
THETA_BASE = 130000.0
MASKED = -1e30


def rope_tables(positions):
    inv_freq = THETA_BASE ** (-(jnp.arange(HD // 2, dtype=jnp.float32) * 2.0 / HD))
    angles = positions.astype(jnp.float32)[:, None] * inv_freq[None, :]
    cosine = jnp.cos(angles)
    sine_tab = jnp.sin(angles)
    return (jnp.concatenate([cosine, cosine], -1), jnp.concatenate([sine_tab, sine_tab], -1))


def rotate(values, cosine, sine_tab):
    middle = values.shape[-1] // 2
    turned = jnp.concatenate([-values[..., middle:], values[..., :middle]], -1)
    return values * cosine[:, None, :] + turned * sine_tab[:, None, :]


def rotate_back(grads_in, cosine, sine_tab):
    middle = grads_in.shape[-1] // 2
    shifted = grads_in * sine_tab[:, None, :]
    turned = jnp.concatenate([shifted[..., middle:], -shifted[..., :middle]], -1)
    return grads_in * cosine[:, None, :] + turned


def inverse_rms(rows_in):
    return lax.rsqrt(jnp.mean(rows_in * rows_in, -1, keepdims=True) + EPSILON)


def norm_back(grad_normed, rows_in, inverse, gain_vec):
    scaled = grad_normed * gain_vec
    inner_sum = jnp.sum(scaled * rows_in, -1, keepdims=True)
    return inverse * scaled - inverse * inverse * inverse / rows_in.shape[-1] * rows_in * inner_sum


def score_rows(query_rows, key_rows, query_pos, key_pos):
    scores = jnp.einsum(
        "qhd,khd->hqk", query_rows, key_rows, preferred_element_type=jnp.float32
    ) * HD ** (-0.5)
    visible = key_pos[None, None, :] <= query_pos[None, :, None]
    return (scores, visible)


def softmax_rows(scores, visible, log_total):
    return jnp.where(
        visible, jnp.exp(jnp.where(visible, scores - log_total[..., None], MASKED)), 0.0
    )


def walk_keys(kv_steps, top_pos, width, step_fn, initial):
    step_rows = kv_steps.shape[1]
    offsets = jnp.arange(step_rows, dtype=jnp.int32)

    def advance(carried, step_item):
        step_index, kv_block = step_item
        first_key = step_index * step_rows
        key_rows = kv_block[:, :width].reshape(step_rows, HEADS, HD)
        value_rows = kv_block[:, width:].reshape(step_rows, HEADS, HD)
        key_pos = first_key + offsets
        updated = lax.cond(
            first_key <= top_pos,
            lambda state: step_fn(state, key_rows, value_rows, key_pos),
            lambda state: state,
            carried,
        )
        return (updated, None)

    indices = jnp.arange(kv_steps.shape[0], dtype=jnp.int32)
    final_state, ignored = lax.scan(advance, initial, (indices, kv_steps))
    return final_state


def body(
    layer_input,
    block_table,
    attn_gain,
    query_weight,
    key_weight,
    value_weight,
    out_weight,
    mlp_gain,
    gate_weight,
    up_weight,
    down_weight,
    cotangent,
):
    tokens = layer_input.shape[1]
    width = layer_input.shape[2]
    half_rows = tokens // 2
    ranks = lax.axis_size("ctx")
    length = tokens * ranks
    score_scale = HD ** (-0.5)
    block_ids = block_table[0].reshape(2 * ranks)
    own_blocks = lax.dynamic_slice_in_dim(block_ids, lax.axis_index("ctx") * 2, 2)
    inner = jnp.arange(half_rows, dtype=jnp.int32)
    query_pos = (own_blocks[:, None] * half_rows + inner[None, :]).reshape(tokens)
    cosine, sine_tab = rope_tables(query_pos)
    full_query, full_key, full_value, full_out, full_attn_gain = (
        lax.all_gather(query_weight, ("ctx", "fsdp"), axis=0, tiled=True),
        lax.all_gather(key_weight, ("ctx", "fsdp"), axis=0, tiled=True),
        lax.all_gather(value_weight, ("ctx", "fsdp"), axis=0, tiled=True),
        lax.all_gather(out_weight, ("ctx", "fsdp"), axis=0, tiled=True),
        lax.all_gather(attn_gain, ("ctx", "fsdp"), axis=0, tiled=True),
    )
    source = layer_input[0].astype(jnp.float32)
    inverse_in = inverse_rms(source)
    normed = (source * inverse_in * full_attn_gain.astype(jnp.float32)).astype(jnp.bfloat16)
    query_pre = jnp.dot(normed, full_query, preferred_element_type=jnp.float32).reshape(
        tokens, HEADS, HD
    )
    key_pre = jnp.dot(normed, full_key, preferred_element_type=jnp.float32).reshape(
        tokens, HEADS, HD
    )
    value_low = jnp.dot(normed, full_value, preferred_element_type=jnp.float32).astype(jnp.bfloat16)
    queries = rotate(query_pre, cosine, sine_tab).astype(jnp.bfloat16)
    keys_low = rotate(key_pre, cosine, sine_tab).astype(jnp.bfloat16).reshape(tokens, width)
    kv_dev = lax.all_gather(jnp.concatenate([keys_low, value_low], 1), "ctx", axis=0, tiled=True)
    slot_ids = jnp.arange(2 * ranks, dtype=jnp.int32)
    holder = jnp.sum(jnp.where(block_ids[None, :] == slot_ids[:, None], slot_ids[None, :], 0), 1)
    kv_seq = jnp.take(kv_dev.reshape(2 * ranks, half_rows, 2 * width), holder, axis=0).reshape(
        length, 2 * width
    )
    step_rows = min(512, length)
    kv_steps = kv_seq.reshape(length // step_rows, step_rows, 2 * width)
    log_totals = []
    attended_parts = []
    top_list = []
    for slot_index in range(2):
        slot_queries = queries[slot_index * half_rows : (slot_index + 1) * half_rows]
        slot_pos = query_pos[slot_index * half_rows : (slot_index + 1) * half_rows]
        top_pos = own_blocks[slot_index] * half_rows + half_rows - 1
        top_list.append(top_pos)

        def stat_step(state, key_rows, value_rows, key_pos):
            running, running_sum = state
            scores, visible = score_rows(slot_queries, key_rows, slot_pos, key_pos)
            scores = jnp.where(visible, scores, MASKED)
            newest = jnp.maximum(running, jnp.max(scores, -1))
            running_sum = running_sum * jnp.exp(running - newest) + jnp.sum(
                jnp.where(visible, jnp.exp(scores - newest[..., None]), 0.0), -1
            )
            return (newest, running_sum)

        start_state = (
            jnp.full((HEADS, half_rows), MASKED, jnp.float32),
            jnp.zeros((HEADS, half_rows), jnp.float32),
        )
        running, running_sum = walk_keys(kv_steps, top_pos, width, stat_step, start_state)
        log_total = running + jnp.log(running_sum)

        def value_step(accumulated, key_rows, value_rows, key_pos):
            scores, visible = score_rows(slot_queries, key_rows, slot_pos, key_pos)
            weights_low = softmax_rows(scores, visible, log_total).astype(jnp.bfloat16)
            return accumulated + jnp.einsum(
                "hqk,khd->qhd", weights_low, value_rows, preferred_element_type=jnp.float32
            )

        attended_parts.append(
            walk_keys(
                kv_steps, top_pos, width, value_step, jnp.zeros((half_rows, HEADS, HD), jnp.float32)
            )
        )
        log_totals.append(log_total)
    attended = jnp.concatenate(attended_parts, 0)
    log_all = jnp.concatenate(log_totals, 1)
    attn_low = attended.reshape(tokens, width).astype(jnp.bfloat16)
    hidden = source + jnp.dot(attn_low, full_out, preferred_element_type=jnp.float32)
    full_gate, full_up, full_down, full_mlp_gain = (
        lax.all_gather(gate_weight, ("ctx", "fsdp"), axis=0, tiled=True),
        lax.all_gather(up_weight, ("ctx", "fsdp"), axis=0, tiled=True),
        lax.all_gather(down_weight, ("ctx", "fsdp"), axis=0, tiled=True),
        lax.all_gather(mlp_gain, ("ctx", "fsdp"), axis=0, tiled=True),
    )
    inverse_mid = inverse_rms(hidden)
    mlp_in = (hidden * inverse_mid * full_mlp_gain.astype(jnp.float32)).astype(jnp.bfloat16)
    gate_pre = jnp.dot(mlp_in, full_gate, preferred_element_type=jnp.float32)
    up_pre = jnp.dot(mlp_in, full_up, preferred_element_type=jnp.float32)
    activation = (jax.nn.silu(gate_pre) * up_pre).astype(jnp.bfloat16)
    branch_mlp = jnp.einsum("tf,df->td", activation, full_down, preferred_element_type=jnp.float32)
    layer_output = (hidden + branch_mlp).astype(jnp.bfloat16)
    back_gate, back_up, back_down, back_mlp_gain = (
        lax.all_gather(gate_weight, ("ctx", "fsdp"), axis=0, tiled=True),
        lax.all_gather(up_weight, ("ctx", "fsdp"), axis=0, tiled=True),
        lax.all_gather(down_weight, ("ctx", "fsdp"), axis=0, tiled=True),
        lax.all_gather(mlp_gain, ("ctx", "fsdp"), axis=0, tiled=True),
    )
    grad_out_low = cotangent[0]
    grad_act = jnp.dot(grad_out_low, back_down, preferred_element_type=jnp.float32)
    sigmoid_gate = jax.nn.sigmoid(gate_pre)
    grad_gate = (grad_act * up_pre * sigmoid_gate * (1.0 + gate_pre * (1.0 - sigmoid_gate))).astype(
        jnp.bfloat16
    )
    grad_up = (grad_act * gate_pre * sigmoid_gate).astype(jnp.bfloat16)
    grad_mlp_in = jnp.einsum(
        "tf,df->td", grad_gate, back_gate, preferred_element_type=jnp.float32
    ) + jnp.einsum("tf,df->td", grad_up, back_up, preferred_element_type=jnp.float32)
    mlp_gain_term = jnp.sum(grad_mlp_in * hidden * inverse_mid, 0)
    grad_hidden = grad_out_low.astype(jnp.float32) + norm_back(
        grad_mlp_in, hidden, inverse_mid, back_mlp_gain.astype(jnp.float32)
    )
    grad_branch = grad_hidden.astype(jnp.bfloat16)
    back_query, back_key, back_value, back_out, back_attn_gain = (
        lax.all_gather(query_weight, ("ctx", "fsdp"), axis=0, tiled=True),
        lax.all_gather(key_weight, ("ctx", "fsdp"), axis=0, tiled=True),
        lax.all_gather(value_weight, ("ctx", "fsdp"), axis=0, tiled=True),
        lax.all_gather(out_weight, ("ctx", "fsdp"), axis=0, tiled=True),
        lax.all_gather(attn_gain, ("ctx", "fsdp"), axis=0, tiled=True),
    )
    grad_attended = (
        jnp.einsum("te,de->td", grad_branch, back_out, preferred_element_type=jnp.float32)
        .astype(jnp.bfloat16)
        .reshape(tokens, HEADS, HD)
    )
    delta_all = jnp.sum(grad_attended.astype(jnp.float32) * attended, -1).T
    grad_query_parts = []
    for slot_index in range(2):
        slot_queries = queries[slot_index * half_rows : (slot_index + 1) * half_rows]
        slot_pos = query_pos[slot_index * half_rows : (slot_index + 1) * half_rows]
        slot_grad_out = grad_attended[slot_index * half_rows : (slot_index + 1) * half_rows]
        slot_delta = delta_all[:, slot_index * half_rows : (slot_index + 1) * half_rows]
        slot_log = log_totals[slot_index]

        def query_step(accumulated, key_rows, value_rows, key_pos):
            scores, visible = score_rows(slot_queries, key_rows, slot_pos, key_pos)
            weights_full = softmax_rows(scores, visible, slot_log)
            grad_weights = jnp.einsum(
                "qhd,khd->hqk", slot_grad_out, value_rows, preferred_element_type=jnp.float32
            )
            grad_scores = (weights_full * (grad_weights - slot_delta[..., None])).astype(
                jnp.bfloat16
            )
            return accumulated + jnp.einsum(
                "hqk,khd->qhd", grad_scores, key_rows, preferred_element_type=jnp.float32
            )

        grad_query_parts.append(
            walk_keys(
                kv_steps,
                top_list[slot_index],
                width,
                query_step,
                jnp.zeros((half_rows, HEADS, HD), jnp.float32),
            )
        )
    grad_queries = jnp.concatenate(grad_query_parts, 0) * score_scale
    grad_query_low = (
        rotate_back(grad_queries, cosine, sine_tab).reshape(tokens, width).astype(jnp.bfloat16)
    )
    bottom_key = jnp.min(query_pos)
    query_both = lax.all_gather(
        jnp.concatenate([queries.reshape(tokens, width), grad_attended.reshape(tokens, width)], 1),
        "ctx",
        axis=0,
        tiled=True,
    )
    stats_both = lax.all_gather(
        jnp.stack([log_all.T, delta_all.T], 1).astype(jnp.bfloat16), "ctx", axis=0, tiled=True
    ).astype(jnp.float32)
    all_rows = jnp.arange(length, dtype=jnp.int32)
    all_pos = jnp.take(block_ids, all_rows // half_rows) * half_rows + all_rows % half_rows
    own_keys = keys_low.reshape(tokens, HEADS, HD)
    own_values = value_low.reshape(tokens, HEADS, HD)

    def gather_step(carried, piece_index):
        first = piece_index * step_rows
        piece_pos = lax.dynamic_slice_in_dim(all_pos, first, step_rows)

        def live_piece(state):
            rows_here = lax.dynamic_slice_in_dim(query_both, first, step_rows, 0)
            stats_here = lax.dynamic_slice_in_dim(stats_both, first, step_rows, 0)
            piece_queries = rows_here[:, :width].reshape(step_rows, HEADS, HD)
            piece_grads = rows_here[:, width:].reshape(step_rows, HEADS, HD)
            piece_log = stats_here[:, 0, :].T
            piece_delta = stats_here[:, 1, :].T
            scores, visible = score_rows(piece_queries, own_keys, piece_pos, query_pos)
            weights_full = softmax_rows(scores, visible, piece_log)
            grad_weights = jnp.einsum(
                "qhd,khd->hqk", piece_grads, own_values, preferred_element_type=jnp.float32
            )
            grad_scores = (weights_full * (grad_weights - piece_delta[..., None])).astype(
                jnp.bfloat16
            )
            grad_keys = (
                jnp.einsum(
                    "hqk,qhd->khd", grad_scores, piece_queries, preferred_element_type=jnp.float32
                )
                * score_scale
            )
            grad_values = jnp.einsum(
                "hqk,qhd->khd",
                weights_full.astype(jnp.bfloat16),
                piece_grads,
                preferred_element_type=jnp.float32,
            )
            return (state[0] + grad_keys, state[1] + grad_values)

        updated = lax.cond(
            jnp.max(piece_pos) >= bottom_key, live_piece, lambda state: state, carried
        )
        return (updated, None)

    start_grads = (
        jnp.zeros((tokens, HEADS, HD), jnp.float32),
        jnp.zeros((tokens, HEADS, HD), jnp.float32),
    )
    summed, ignored = lax.scan(
        gather_step, start_grads, jnp.arange(length // step_rows, dtype=jnp.int32)
    )
    kv_grads = jnp.concatenate(
        [summed[0].reshape(tokens, width), summed[1].reshape(tokens, width)], 1
    )
    grad_key_low = (
        rotate_back(kv_grads[:, :width].reshape(tokens, HEADS, HD), cosine, sine_tab)
        .reshape(tokens, width)
        .astype(jnp.bfloat16)
    )
    grad_value_low = kv_grads[:, width:].astype(jnp.bfloat16)
    grad_normed = jnp.einsum(
        "te,de->td", grad_query_low, back_query, preferred_element_type=jnp.float32
    )
    grad_normed = grad_normed + jnp.einsum(
        "te,de->td", grad_key_low, back_key, preferred_element_type=jnp.float32
    )
    grad_normed = grad_normed + jnp.einsum(
        "te,de->td", grad_value_low, back_value, preferred_element_type=jnp.float32
    )
    attn_gain_term = jnp.sum(grad_normed * source * inverse_in, 0)
    input_grad = grad_hidden + norm_back(
        grad_normed, source, inverse_in, back_attn_gain.astype(jnp.float32)
    )

    def outer_sum(left_side, right_side):
        return jnp.einsum("tc,te->ce", left_side, right_side, preferred_element_type=jnp.float32)

    weight_grads = lax.psum_scatter(
        jnp.concatenate(
            [
                outer_sum(normed, grad_query_low),
                outer_sum(normed, grad_key_low),
                outer_sum(normed, grad_value_low),
                outer_sum(attn_low, grad_branch),
                outer_sum(mlp_in, grad_gate),
                outer_sum(mlp_in, grad_up),
                outer_sum(grad_out_low, activation),
            ],
            1,
        ),
        ("ctx", "fsdp"),
        scatter_dimension=0,
        tiled=True,
    )
    gain_grads = lax.psum_scatter(
        jnp.stack([attn_gain_term, mlp_gain_term], 1),
        ("ctx", "fsdp"),
        scatter_dimension=0,
        tiled=True,
    )
    hidden_units = gate_weight.shape[1]
    edge_attn = 4 * width
    return (
        layer_output[None],
        input_grad[None],
        gain_grads[:, 0],
        weight_grads[:, 0:width],
        weight_grads[:, width : 2 * width],
        weight_grads[:, 2 * width : 3 * width],
        weight_grads[:, 3 * width : edge_attn],
        gain_grads[:, 1],
        weight_grads[:, edge_attn : edge_attn + hidden_units],
        weight_grads[:, edge_attn + hidden_units : edge_attn + 2 * hidden_units],
        weight_grads[:, edge_attn + 2 * hidden_units : edge_attn + 3 * hidden_units],
    )


def solution(mesh):
    return jax.shard_map(
        body,
        mesh=mesh,
        in_specs=(
            P("fsdp", "ctx", None),
            P("fsdp", None, None),
            P(("ctx", "fsdp")),
            P(("ctx", "fsdp"), None),
            P(("ctx", "fsdp"), None),
            P(("ctx", "fsdp"), None),
            P(("ctx", "fsdp"), None),
            P(("ctx", "fsdp")),
            P(("ctx", "fsdp"), None),
            P(("ctx", "fsdp"), None),
            P(("ctx", "fsdp"), None),
            P("fsdp", "ctx", None),
        ),
        out_specs=(
            P("fsdp", "ctx", None),
            P("fsdp", "ctx", None),
            P(("ctx", "fsdp")),
            P(("ctx", "fsdp"), None),
            P(("ctx", "fsdp"), None),
            P(("ctx", "fsdp"), None),
            P(("ctx", "fsdp"), None),
            P(("ctx", "fsdp")),
            P(("ctx", "fsdp"), None),
            P(("ctx", "fsdp"), None),
            P(("ctx", "fsdp"), None),
        ),
        check_vma=False,
    )
```

profile of v0, /device:TPU:9, one launch (start us, length us, event | category | flops | bytes accessed | tf_op | source)
XLA Modules:
  0.0 4484.4 jit_solution(11830913646299219411)
XLA Ops:
  11.2 40.8 all-reduce.2
  56.9 33.2 all-gather.10.cloned.1.call-done
  102.4 66.6 %all-gather.16.cloned.1.call-done = bf16[2048,2048]{1,0:T(8,128)(2,1)} async-done(((bf16[64,2048]{1,0:T(8,128)(2,1)}), bf16[2048,2048]{1,0:T(8,128)(2,1)}) %all-gather.16.cloned.1.call-update) | async-done | bytes 8388624 | tf_op jit(solution)/shard_map/all_gather | solution.py:109
  191.0 57.0 %all-gather.12.cloned.1.call-done = bf16[2048,2048]{1,0:T(8,128)(2,1)} async-done(((bf16[64,2048]{1,0:T(8,128)(2,1)}), bf16[2048,2048]{1,0:T(8,128)(2,1)}) %all-gather.12.cloned.1.call-update) | async-done | bytes 8388624 | tf_op jit(solution)/shard_map/all_gather | solution.py:111
  262.0 180.3 %all-gather.14.cloned.1.call-done = bf16[2048,4096]{1,0:T(8,128)(2,1)} async-done(((bf16[128,4096]{1,0:T(8,128)(2,1)}), bf16[2048,4096]{1,0:T(8,128)(2,1)}) %all-gather.14.cloned.1.call-update) | async-done | bytes 16777232 | tf_op jit(solution)/shard_map/all_gather | solution.py:127
  469.8 21.3 copy.118
  491.1 15.8 while.95
  507.6 23.4 while.96
  532.5 20.1 while.97
  553.7 32.5 while.98
  594.9 122.6 %all-gather.22.cloned.1.call-done = bf16[2048,8192]{1,0:T(8,128)(2,1)} async-done(((bf16[64,8192]{1,0:T(8,128)(2,1)}), bf16[2048,8192]{1,0:T(8,128)(2,1)}) %all-gather.22.cloned.1.call-update) | async-done | bytes 33554448 | tf_op jit(solution)/shard_map/all_gather | solution.py:180
  717.6 17.1 fusion.157
  734.6 178.8 %all-gather.20.cloned.1.call-done = bf16[2048,8192]{1,0:T(8,128)(2,1)} async-done(((bf16[64,8192]{1,0:T(8,128)(2,1)}), bf16[2048,8192]{1,0:T(8,128)(2,1)}) %all-gather.20.cloned.1.call-update) | async-done | bytes 33554448 | tf_op jit(solution)/shard_map/all_gather | solution.py:179
  913.4 17.1 fusion.156
  930.5 178.7 %all-gather.24.cloned.1.call-done = bf16[2048,8192]{1,0:T(8,128)(2,1)} async-done(((bf16[64,8192]{1,0:T(8,128)(2,1)}), bf16[2048,8192]{1,0:T(8,128)(2,1)}) %all-gather.24.cloned.1.call-update) | async-done | bytes 33554448 | tf_op jit(solution)/shard_map/all_gather | solution.py:181
  1109.2 19.5 multiply_convert_fusion.8
  1128.7 17.4 fusion.158
  1146.1 18.0 multiply_reduce_fusion
  1209.6 44.3 while.100
  1261.1 32.7 while.99
  1298.4 34.3 all_gather.56
  1367.7 22.7 copy.141
  1391.7 130.7 %while.101 = (s32[]{:T(128)}, f32[128,32,64]{0,2,1:T(8,128)S(1)}, f32[128,32,64]{0,2,1:T(8,128)}, s32[4]{0:T(128)S(1)}, s32[2048]{0:T(1024)S(1)}, /*index=5*/s32...) while((s32[]{:T(128)}, f32[128,32,64]{0,2,1:T(8,128)S(1)}, ...), condition=%wide.region_38.39_spmd.clone, body=%wide.region_34.38_spmd.clone.sunk | while | flops 1099760256 | bytes 56239592 | solution.py:316
  1395.0 29.4 conditional.27
  1427.7 29.4 conditional.27
  1460.4 29.4 conditional.27
  1493.1 29.0 conditional.27
  1562.8 24.1 convolution_dynamic-update-slice_fusion.1
  1587.0 23.5 convolution_dynamic-update-slice_fusion
  1610.5 23.4 bitcast_dynamic-update-slice_fusion
  1635.2 17.0 fusion.68
  1655.7 2813.1 %reduce-scatter.5.cloned.1.call-done = f32[64,32768]{1,0:T(8,128)} async-done(((f32[2048,32768]{1,0:T(8,128)}), f32[64,32768]{1,0:T(8,128)}) %reduce-scatter.5.cloned.1.call-update) | async-done | bytes 8388624 | tf_op jit(solution)/shard_map/reduce_scatter | solution.py:345
  (521 shorter events, 653.2 us)
Async XLA Ops:
  7.2 82.9 %all-gather.10.cloned.1.call-start = ((), (), s32[]{:S(2)}) async-start(), calls=%async_computation.2 | async-start | bytes 8650752 | tf_op jit(solution)/shard_map/all_gather | solution.py:110
  7.9 161.1 %all-gather.16.cloned.1.call-start = ((), (), s32[]{:S(2)}) async-start(), calls=%async_computation.5 | async-start | bytes 8650752 | tf_op jit(solution)/shard_map/all_gather | solution.py:109
  8.7 239.3 %all-gather.12.cloned.1.call-start = ((), (), s32[]{:S(2)}) async-start(), calls=%async_computation.3 | async-start | bytes 8650752 | tf_op jit(solution)/shard_map/all_gather | solution.py:111
  9.4 432.8 %all-gather.14.cloned.1.call-start = ((), (), s32[]{:S(2)}) async-start(), calls=%async_computation.4 | async-start | bytes 17825792 | tf_op jit(solution)/shard_map/all_gather | solution.py:127
  52.0 196.0 %copy-start.36 = (f32[2048]{0:T(1024)}, f32[2048]{0:T(1024)S(1)}, u32[]{:S(2)}) copy-start(f32[2048]{0:T(1024)S(1)} %convert_element_type.166) | copy-start | bytes 24580
  52.8 206.9 %copy-start.39 = (s32[32]{0:T(128)}, s32[32]{0:T(128)S(1)}, u32[]{:S(2)}) copy-start(s32[32]{0:T(128)S(1)} %eq.17) | copy-start | bytes 388
  55.1 135.1 %copy-start.42 = (f32[128,64]{0,1:T(8,128)}, f32[128,64]{0,1:T(8,128)S(1)}, u32[]{:S(2)}) copy-start(f32[128,64]{0,1:T(8,128)S(1)} %get-tuple-element.1349) | copy-start | bytes 98308
  55.1 135.1 %copy-start.44 = (f32[128,64]{0,1:T(8,128)}, f32[128,64]{0,1:T(8,128)S(1)}, u32[]{:S(2)}) copy-start(f32[128,64]{0,1:T(8,128)S(1)} %get-tuple-element.1399) | copy-start | bytes 98308
  56.9 191.1 %copy-start.50 = (f32[128]{0:T(128)}, f32[128]{0:T(128)S(1)}, u32[]{:S(2)}) copy-start(f32[128]{0:T(128)S(1)} %get-tuple-element.1355) | copy-start | bytes 1540
  190.7 61.9 %copy-start.9 = (bf16[128,32,64]{0,2,1:T(8,128)(2,1)}, bf16[128,32,64]{0,2,1:T(8,128)(2,1)S(1)}, u32[]{:S(2)}) copy-start(bf16[128,32,64]{0,2,1:T(8,128)(2,1)S(1)} %get-tuple-element.2015) | copy-start | bytes 1572868
  254.5 335.2 %all-gather.18.cloned.1.call-start = ((), (), s32[]{:S(2)}) async-start(), calls=%async_computation.6 | async-start | bytes 8650752 | tf_op jit(solution)/shard_map/all_gather | solution.py:112
  255.1 462.4 %all-gather.22.cloned.1.call-start = ((), (), s32[]{:S(2)}) async-start(), calls=%async_computation.8 | async-start | bytes 34603008 | tf_op jit(solution)/shard_map/all_gather | solution.py:180
  255.7 657.7 %all-gather.20.cloned.1.call-start = ((), (), s32[]{:S(2)}) async-start(), calls=%async_computation.7 | async-start | bytes 34603008 | tf_op jit(solution)/shard_map/all_gather | solution.py:179
  256.4 852.8 %all-gather.24.cloned.1.call-start = ((), (), s32[]{:S(2)}) async-start(), calls=%async_computation.9 | async-start | bytes 34603008 | tf_op jit(solution)/shard_map/all_gather | solution.py:181
  257.2 1110.5 %all-gather.26.cloned.1.call-start = ((), (), s32[]{:S(2)}) async-start(), calls=%async_computation.10 | async-start | bytes 17825792 | tf_op jit(solution)/shard_map/all_gather | solution.py:260
  594.7 569.4 %copy-start.7 = (f32[128,2048]{1,0:T(8,128)}, f32[128,2048]{1,0:T(8,128)S(1)}, u32[]{:S(2)}) copy-start(f32[128,2048]{1,0:T(8,128)S(1)} %get-tuple-element.1396) | copy-start | bytes 3145732
  594.9 318.5 %copy-start.14 = (bf16[128,2048]{1,0:T(8,128)(2,1)}, bf16[128,2048]{1,0:T(8,128)(2,1)S(1)}, u32[]{:S(2)}) copy-start(bf16[128,2048]{1,0:T(8,128)(2,1)S(1)} %multiply_convert_fusion.11) | copy-start | bytes 1572868
  734.6 374.6 %copy-start.32 = (bf16[1,128,2048]{2,1,0:T(8,128)(2,1)S(1)}, bf16[1,128,2048]{2,1,0:T(8,128)(2,1)}, u32[]{:S(2)}) copy-start(bf16[1,128,2048]{2,1,0:T(8,128)(2,1)} %param.51) | copy-start | bytes 1572868
  1172.4 29.9 copy-start.53
  1173.5 480.2 %reduce-scatter.7.cloned.1.call-start = ((), (), s32[]{:S(2)}) async-start(), calls=%async_computation.12 | async-start | bytes 1081344
  1174.6 32.1 copy-start.20
  1174.6 32.1 copy-start.22
  1293.8 39.7 copy-start.30
  1293.8 43.2 copy-start.23
  1293.9 43.2 copy-start.48
  1355.5 36.2 copy-start.10
  1355.5 36.2 copy-start.56
  1391.7 132.1 %copy-start.43 = (f32[128,64]{0,1:T(8,128)S(1)}, f32[128,64]{0,1:T(8,128)}, u32[]{:S(2)}) copy-start(f32[128,64]{0,1:T(8,128)} %copy-done.42) | copy-start | bytes 98308
  1536.6 2932.2 %reduce-scatter.5.cloned.1.call-start = ((), (), s32[]{:S(2)}) async-start(), calls=%async_computation.11 | async-start | bytes 276824064 | tf_op jit(solution)/shard_map/reduce_scatter | solution.py:345
  1562.8 24.1 copy-start.19
  1587.0 23.5 copy-start.16
  1587.0 23.5 copy-start.33
  (48 other events, 345.8 us)
Sparse Core Ops, SparseCore 0:
  10.9 79.1 all-gather.9
  92.9 76.0 all-gather.15
  171.9 76.0 all-gather.11
  254.7 187.5 all-gather.13
  444.9 78.3 all-gather.17
  526.1 191.4 all-gather.21
  720.4 192.9 all-gather.19
  916.3 192.9 all-gather.23
  1173.6 194.0 all-gather.25
  1536.8 111.5 reduce-scatter.6
  1650.9 2817.9 reduce-scatter.4
where the time goes:
time: 4500 us; the launch traced here: 4480 us
  waiting for transfers between devices  3650 us (81%)
  matrix products  410 us (9%)
  local copies, waits for them, and re-layouts  243 us (5%)
  blocking collectives  75.2 us (2%)
  other arithmetic  65.9 us (1%)
    reduce_scatter x1, waiting for transfers between devices, body(): lax.psum_scatter(jnp.concatenate([outer_sum(normed, grad_query_low), oute...  2810 us
    all_gather x1, waiting for transfers between devices, body(): lax.all_gather(jnp.concatenate([keys_low, value_low], 1), 'ctx', axis=0,...  180 us
    all_gather x1, waiting for transfers between devices, body(): lax.all_gather(gate_weight, ('ctx', 'fsdp'), axis=0, tiled=True)  179 us
    all_gather x1, waiting for transfers between devices, body(): lax.all_gather(down_weight, ('ctx', 'fsdp'), axis=0, tiled=True)  179 us
    all_gather x1, waiting for transfers between devices, body(): lax.all_gather(up_weight, ('ctx', 'fsdp'), axis=0, tiled=True)  123 us
    dot_general x7, matrix products, outer_sum(): jnp.einsum('tc,te->ce', left_side, right_side, preferred_element_type=jnp...  105 us
  transfers between devices with their start and end apart: 11, of which 9 were waited for; matrix products, arithmetic and copies ran while one was open for 11% of the time, Pallas kernels for 0%

commit v1 on v0

--- a/solution.py
+++ b/solution.py
@@ -1,18 +1,765 @@
-import jax
-import jax.numpy as jnp
+import functools
+import jax, jax.numpy as jnp
 from jax import lax
+from jax.experimental import pallas as pl
+from jax.experimental.pallas import tpu as pltpu
+
+MESH = pl.DeviceIdType.MESH
+DMA = pltpu.SemaphoreType.DMA
+BF = jnp.bfloat16
+F32 = jnp.float32
+
+
+class Plan:
+    def __init__(self):
+        self.steps = []
+
+    def at(self, when, step):
+        self.steps.append((when, len(self.steps), step))
+
+    def run(self):
+        for _, _, step in sorted(self.steps, key=lambda s: s[:2]):
+            step()
+
+
+class Here:
+    def __init__(self):
+        self.me = lax.axis_index("ctx")
+        self.core = lax.axis_index("fsdp")
+        self.z = self.me // 4
+        self.y = lax.rem(self.me // 2, 2)
+        self.x = lax.rem(self.me, 2)
+        self.xy = lax.rem(self.me, 4)
+        self.xn = self.me + 1 - 2 * self.x
+        self.yn = self.me + 2 - 4 * self.y
+
+
+def remote(src, dst, send_sem, recv_sem, **device):
+    return pltpu.make_async_remote_copy(
+        src_ref=src, dst_ref=dst, send_sem=send_sem, recv_sem=recv_sem, device_id=device, device_id_type=MESH
+    )
+
+
+def greet_all(h):
+    barrier = pltpu.get_barrier_semaphore()
+    for step in range(1, 16):
+        pl.semaphore_signal(barrier, inc=1, device_id={"ctx": jnp.bitwise_xor(h.me, step)}, device_id_type=MESH)
+    pl.semaphore_signal(barrier, inc=1, device_id={"fsdp": 1 - h.core}, device_id_type=MESH)
+    pl.semaphore_wait(barrier, 16)
+
+
+GATHER_SEMS = [DMA((4,))] * 12 + [DMA]
+
+
+def gather16(plan, h, src, out, sems, t0, tz, tx):
+    us, ur, ds, dr, xs, xr, ys, yr, xfs, xfr, yfs, yfr, own = sems
+    half = src.shape[0] // 2
+
+    def plane(zz, source=None):
+        s = zz * 4 + h.xy
+        source = out.at[s] if source is None else source
+        return (
+            remote(source, out.at[s], xs.at[zz], xr.at[zz], ctx=h.xn),
+            remote(source, out.at[s], ys.at[zz], yr.at[zz], ctx=h.yn),
+        )
+
+    def across(zz):
+        sx = zz * 4 + lax.rem(h.xn, 4)
+        sy = zz * 4 + lax.rem(h.yn, 4)
+        top, low = pl.ds(0, half), pl.ds(half, half)
+        return (
+            remote(out.at[sx, top], out.at[sx, top], yfs.at[zz], yfr.at[zz], ctx=h.yn),
+            remote(out.at[sy, low], out.at[sy, low], xfs.at[zz], xfr.at[zz], ctx=h.xn),
+        )
+
+    def arrived(zz):
+        sx = zz * 4 + lax.rem(h.xn, 4)
+        sy = zz * 4 + lax.rem(h.yn, 4)
+        return (
+            remote(out.at[sx], out.at[sx], xs.at[zz], xr.at[zz], ctx=h.xn),
+            remote(out.at[sy], out.at[sy], ys.at[zz], yr.at[zz], ctx=h.yn),
+        )
+
+    def hop(k, up, source=None):
+        it = (h.z - k if up else h.z + k) * 4 + h.xy
+        send, recv = (us, ur) if up else (ds, dr)
+        source = out.at[it] if source is None else source
+        to = h.me + 4 if up else h.me - 4
+        return remote(source, out.at[it], send.at[k], recv.at[k + 1], ctx=to)
+
+    def landed(k, up):
+        it = (h.z - k if up else h.z + k) * 4 + h.xy
+        send, recv = (us, ur) if up else (ds, dr)
+        return remote(out.at[it], out.at[it], send.at[k - 1], recv.at[k], ctx=h.me)
+
+    local = pltpu.make_async_copy(src, out.at[h.me], own)
+
+    def first():
+        pl.when(h.z < 3)(lambda: hop(0, True, src).start())
+        pl.when(h.z > 0)(lambda: hop(0, False, src).start())
+        for c in plane(h.z, src):
+            c.start()
+        local.start()
+
+    plan.at(t0, first)
+
+    def step(k, up):
+        def go():
+            landed(k, up).wait_recv()
+            if k < 3:
+                pl.when((h.z < 3) if up else (h.z > 0))(lambda: hop(k, up).start())
+            for c in plane(h.z - k if up else h.z + k):
+                c.start()
+
+        pl.when((h.z >= k) if up else (h.z + k <= 3))(go)
+
+    def forward(zz):
+        got, on = arrived(zz), across(zz)
+        for g, c in zip(got, on):
+            g.wait_recv()
+            c.start()
+
+    def finish(zz):
+        sx = zz * 4 + 3 - h.xy
+        top, low = pl.ds(0, half), pl.ds(half, half)
+        remote(out.at[sx, top], out.at[sx, top], yfs.at[zz], yfr.at[zz], ctx=h.yn).wait_recv()
+        remote(out.at[sx, low], out.at[sx, low], xfs.at[zz], xfr.at[zz], ctx=h.xn).wait_recv()
+
+    plan.at(t0 + 0.8 * tx, lambda: forward(h.z))
+    for k in (1, 2, 3):
+        for up in (True, False):
+            valid = (lambda k=k, up=up: (h.z >= k) if up else (h.z + k <= 3))
+            plan.at(t0 + k * tz, functools.partial(step, k, up))
+            zz = (lambda k=k, up=up: h.z - k if up else h.z + k)
+            plan.at(t0 + (k + 0.8) * tx, lambda v=valid, q=zz: pl.when(v())(lambda: forward(q())))
+
+    def drain():
+        for zz in range(4):
+            finish(zz)
+        for k in range(3):
+            pl.when((h.z >= k) & (h.z < 3))(lambda: hop(k, True).wait_send())
+            pl.when((h.z + k <= 3) & (h.z > 0))(lambda: hop(k, False).wait_send())
+        for zz in range(4):
+            for c in plane(zz) + across(zz):
+                c.wait_send()
+        local.wait()
+
+    plan.at(t0 + 4.5 * tx, drain)
+
+
+SCATTER_SEMS = [DMA((4,))] * 8 + [DMA((4,))] * 2
+
+
+def scatter_scratch(rows, width):
+    half = width // 2
+    return [
+        pltpu.VMEM((4, 2, rows, half), BF),
+        pltpu.VMEM((4, 2, rows, half), BF),
+        pltpu.VMEM((4, rows, half), BF),
+        pltpu.VMEM((4, rows, half), BF),
+        pltpu.VMEM((4, rows, half), BF),
+        pltpu.VMEM((4, rows, half), BF),
+        pltpu.VMEM((3, rows, width), BF),
+        pltpu.VMEM((3, rows, width), BF),
+    ] + SCATTER_SEMS
+
+
+N_SCATTER = 18
+AHEAD = 2
+
+
+def scatter16(plan, h, part, out, scratch, t0, tx):
+    ra, rb, sa, sb, qa, qb, sz, rz = scratch[:8]
+    as_, ar, bs, br, cs, cr, es, er, zs, zr = scratch[8:]
+    rows, width = part.shape[3:]
+    half = width // 2
+    lo, hi = pl.ds(0, half), pl.ds(half, half)
+    xo, yo = 1 - h.x, 1 - h.y
+
+    def place(k):
+        return lax.rem(h.z + k, 4)
+
+    def first(i, k):
+        return (
+            remote(part.at[place(k), :, xo, :, lo], ra.at[i], as_.at[i], ar.at[i], ctx=h.xn),
+            remote(part.at[place(k), yo, :, :, hi], rb.at[i], bs.at[i], br.at[i], ctx=h.yn),
+        )
+
+    def second(i):
+        return (
+            remote(sa.at[i], qa.at[i], cs.at[i], cr.at[i], ctx=h.yn),
+            remote(sb.at[i], qb.at[i], es.at[i], er.at[i], ctx=h.xn),
+        )
+
+    def third(k):
+        return remote(sz.at[k - 1], rz.at[k - 1], zs.at[k], zr.at[k], ctx=place(k) * 4 + h.xy)
+
+    def start(i, k):
+        for c in first(i, k):
+            c.start()
+
+    def middle(i, k):
+        a, b = first(i, k)
+        c, e = second(i)
+        a.wait_recv()
+        sa[i] = (part[place(k), yo, h.x, :, lo].astype(F32) + ra[i, yo].astype(F32)).astype(BF)
+        c.start()
+        b.wait_recv()
+        sb[i] = (part[place(k), h.y, xo, :, hi].astype(F32) + rb[i, xo].astype(F32)).astype(BF)
+        e.start()
+
+    def total(i, k):
+        c, e = second(i)
+        c.wait_recv()
+        e.wait_recv()
+        left = part[place(k), h.y, h.x, :, lo].astype(F32) + ra[i, h.y].astype(F32) + qa[i].astype(F32)
+        right = part[place(k), h.y, h.x, :, hi].astype(F32) + rb[i, h.x].astype(F32) + qb[i].astype(F32)
+        if k:
+            sz[k - 1, :, lo] = left.astype(BF)
+            sz[k - 1, :, hi] = right.astype(BF)
+            third(k).start()
+        else:
+            out[:, lo] = left
+            out[:, hi] = right
+
+    def last():
+        for k in (1, 2, 3):
+            third(k).wait_recv()
+        out[...] += rz[0].astype(F32) + rz[1].astype(F32) + rz[2].astype(F32)
+        for k in (1, 2, 3):
+            third(k).wait_send()
+        for i, k in enumerate((2, 1, 3, 0)):
+            for c in first(i, k) + second(i):
+                c.wait_send()
+
+    for i, k in enumerate((2, 1, 3, 0)):
+        plan.at(t0 + max(0, i - AHEAD + 0.71) * tx if i >= AHEAD else t0 + 0.01 * i, functools.partial(start, i, k))
+        plan.at(t0 + i * tx + 0.7 * tx, functools.partial(middle, i, k))
+        plan.at(t0 + i * tx + 1.35 * tx, functools.partial(total, i, k))
+    plan.at(t0 + 5 * tx, last)
+
+
+DEAL_SEMS = [DMA((16,))] * 4 + [DMA]
+
+
+def deal16(plan, h, piece, put, passed, sems, t0, t1, both=True):
+    ss, sr, fs, fr, own = sems
+
+    def send(step):
+        to = jnp.bitwise_xor(h.me, step)
+        return remote(piece(to), put(h.me), ss.at[step], sr.at[step], ctx=to)
+
+    def got(step):
+        at = jnp.bitwise_xor(h.me, step)
+        return remote(put(at), put(at), ss.at[step], sr.at[step], ctx=at)
+
+    def hand(step):
+        at = jnp.bitwise_xor(h.me, step)
+        return remote(put(at) if step else piece(h.me), passed(at, h.core), fs.at[step], fr.at[step], fsdp=1 - h.core)
+
+    def taken(step):
+        at = jnp.bitwise_xor(h.me, step)
+        return remote(passed(at, 1 - h.core), passed(at, 1 - h.core), fs.at[step], fr.at[step], fsdp=1 - h.core)
+
+    local = pltpu.make_async_copy(piece(h.me), put(h.me), own)
+
+    def first():
+        for step in ORDER:
+            send(step).start()
+        local.start()
+        if both:
+            hand(0).start()
+
+    plan.at(t0, first)
+    for i, step in enumerate(ORDER):
+
+        def relay(step=step):
+            got(step).wait_recv()
+            if both:
+                hand(step).start()
+
+        plan.at(t0 + (t1 - t0) * (i + 1) / 15, relay)
+
+    def drain():
+        if both:
+            for step in range(16):
+                taken(step).wait_recv()
+                hand(step).wait_send()
+        for step in ORDER:
+            send(step).wait_send()
+        local.wait()
+
+    plan.at(t1 + 2, drain)
+
+
+ORDER = (1, 2, 3, 4, 5, 6, 7, 8, 9, 10, 11, 12, 13, 14, 15)
+
+ROWS = 256
+
+
+def _tri():
+    i = lax.broadcasted_iota(jnp.int32, (ROWS, ROWS), 0)
+    j = lax.broadcasted_iota(jnp.int32, (ROWS, ROWS), 1)
+    return i <= j
+
+
+def _heads(value):
+    lane = lax.broadcasted_iota(jnp.int32, value.shape, 1)
+    zero = jnp.zeros_like(value)
+    return jnp.where(lane < 64, value, zero), jnp.where(lane >= 64, value, zero)
+
+
+def _nt(a, b):
+    return lax.dot_general(a, b, (((1,), (1,)), ((), ())), preferred_element_type=F32)
+
+
+def _tn(a, b):
+    return lax.dot_general(a, b, (((0,), (0,)), ((), ())), preferred_element_type=F32)
+
+
+def _nn(a, b):
+    return jnp.dot(a, b, preferred_element_type=F32)
+
+
+def _scores(keys, query, tri):
+    scores = _nt(keys, query)
+    n = keys.shape[0]
+    low = jnp.where(tri, scores[n - ROWS :], -1e30)
+    return low if n == ROWS else jnp.concatenate([scores[: n - ROWS], low], 0)
+
+
+def sort_rows(order_ref, src, dst, blk=64):
+    for b in range(src.shape[0] // blk):
+        at = pl.multiple_of(order_ref[b] * blk, blk)
+        dst[b * blk : (b + 1) * blk, :] = src[pl.ds(at, blk), :]
+
+
+def attend(qs, ks, vs, os, lse):
+    tri = _tri()
+    for i in range(qs.shape[0] // ROWS):
+        n = (i + 1) * ROWS
+        mine = slice(i * ROWS, n)
+        total = None
+        for head, query in enumerate(_heads(qs[mine, :] * BF(0.125))):
+            scores = _scores(ks[:n, :], query, tri)
+            top = jnp.max(scores, 0, keepdims=True)
+            raw = jnp.exp(scores - top)
+            size = jnp.sum(raw, 0, keepdims=True)
+            lse[head : head + 1, mine] = top + jnp.log(size)
+            probs = (raw * (1.0 / size)).astype(BF)
+            part = _tn(probs, _heads(vs[:n, :])[head])
+            total = part if total is None else total + part
+        os[mine, :] = total.astype(BF)
+
+
+def attend_back(qs, ks, vs, gs, lse, dq, dk, dv):
+    tri = _tri()
+    dk[...] = jnp.zeros_like(dk)
+    dv[...] = jnp.zeros_like(dv)
+    for i in range(qs.shape[0] // ROWS):
+        n = (i + 1) * ROWS
+        mine = slice(i * ROWS, n)
+        total = None
+        queries = _heads(qs[mine, :] * BF(0.125))
+        grads = _heads(gs[mine, :])
+        for head in range(2):
+            scores = _scores(ks[:n, :], queries[head], tri)
+            probs = jnp.exp(scores - lse[head : head + 1, mine])
+            gp = _nt(vs[:n, :], grads[head])
+            delta = jnp.sum(probs * gp, 0, keepdims=True)
+            ds = (probs * (gp - delta)).astype(BF)
+            dv[:n, :] += _nn(probs.astype(BF), grads[head])
+            dk[:n, :] += _nn(ds, queries[head])
+            part = _tn(ds, _heads(ks[:n, :])[head])
+            total = part if total is None else total + part
+        dq[mine, :] = total * 0.125
+
+
+def fwd_kernel(order, table, q, k, v, o, lse, qs, ks, vs, os):
+    for a, b in ((q, qs), (k, ks), (v, vs)):
+        sort_rows(order, a, b)
+    attend(qs, ks, vs, os, lse)
+    sort_rows(table, os, o)
+
+
+def bwd_kernel(order, table, qs, ks, vs, g, lse, dq, dk, dv, gs, dqs, dks, dvs):
+    sort_rows(order, g, gs)
+    attend_back(qs, ks, vs, gs, lse, dqs, dks, dvs)
+    for a, b in ((dqs, dq), (dks, dk), (dvs, dv)):
+        sort_rows(table, a, b)
+
+
+def attention(order, table, q, k, v):
+    n = q.shape[0]
+    rows = jax.ShapeDtypeStruct((n, 128), BF)
+    return pl.pallas_call(
+        fwd_kernel,
+        out_shape=(rows, jax.ShapeDtypeStruct((2, n), F32), rows, rows, rows),
+        grid_spec=pltpu.PrefetchScalarGridSpec(
+            num_scalar_prefetch=2, grid=(),
+            in_specs=[pl.BlockSpec(memory_space=pltpu.VMEM)] * 3,
+            out_specs=[pl.BlockSpec(memory_space=pltpu.VMEM)] * 5,
+            scratch_shapes=[pltpu.VMEM((n, 128), BF)],
+        ),
+        compiler_params=pltpu.CompilerParams(vmem_limit_bytes=48 << 20),
+        name="attention",
+    )(order, table, q, k, v)
+
+
+def attention_back(order, table, qs, ks, vs, g, lse):
+    n = qs.shape[0]
+    rows = jax.ShapeDtypeStruct((n, 128), F32)
+    return pl.pallas_call(
+        bwd_kernel,
+        out_shape=(rows, rows, rows),
+        grid_spec=pltpu.PrefetchScalarGridSpec(
+            num_scalar_prefetch=2, grid=(),
+            in_specs=[pl.BlockSpec(memory_space=pltpu.VMEM)] * 5,
+            out_specs=[pl.BlockSpec(memory_space=pltpu.VMEM)] * 3,
+            scratch_shapes=[pltpu.VMEM((n, 128), BF)] + [pltpu.VMEM((n, 128), F32)] * 3,
+        ),
+        compiler_params=pltpu.CompilerParams(vmem_limit_bytes=48 << 20),
+        name="attention_back",
+    )(order, table, qs, ks, vs, g, lse)
+
+
 from jax.sharding import PartitionSpec as P
 
 HEADS = 32
 HD = 64
-
-
 EPSILON = 1e-05
 THETA_BASE = 130000.0
+ANY = pl.BlockSpec(memory_space=pl.ANY)
+INNER = pl.BlockSpec(memory_space=pltpu.VMEM)
+
+
+def comm_call(kernel, outs, out_specs, in_specs, scratch, cid, name, vmem=40):
+    return pl.pallas_call(
+        kernel,
+        out_shape=outs,
+        in_specs=in_specs,
+        out_specs=out_specs,
+        scratch_shapes=scratch,
+        compiler_params=pltpu.CompilerParams(
+            collective_id=cid, has_side_effects=True, vmem_limit_bytes=vmem << 20
+        ),
+        name=name,
+    )
+
+
+def take(refs, n):
+    head, refs[:] = refs[:n], refs[n:]
+    return head
+
+
+def columns(src, width):
+    return lambda c: src.at[:, pl.ds(pl.multiple_of(c * width, 128), width)]
+
+
+def deal_columns(plan, h, src, out, sems, t0, t1):
+    deal16(
+        plan, h, columns(src, out.shape[3]), lambda c: out.at[c, h.core], lambda c, core: out.at[c, core], sems, t0, t1
+    )
+
+
+def entry_kernel(x, wq, wk, wv, gains, xg, q_out, k_out, v_out, g_out, *refs):
+    refs = list(refs)
+    h = Here()
+    greet_all(h)
+    plan = Plan()
+    for src, out in ((wq, q_out), (wk, k_out), (wv, v_out)):
+        deal_columns(plan, h, src, out, take(refs, 5), 0, 20)
+    deal16(
+        plan, h, lambda c: gains, lambda c: g_out.at[c, h.core], lambda c, core: g_out.at[c, core], take(refs, 5), 0, 21
+    )
+    gather16(plan, h, x, xg, take(refs, 13), 0, 14, 20)
+    plan.run()
+
+
+def entry(x, wq, wk, wv, gains):
+    rows, width = x.shape
+    block = (16, 2, wq.shape[0], width // 16)
+    outs = (
+        jax.ShapeDtypeStruct((16, rows, width), BF),
+        *[jax.ShapeDtypeStruct(block, BF)] * 3,
+        jax.ShapeDtypeStruct((16, 2) + gains.shape, BF),
+    )
+    return comm_call(entry_kernel, outs, [ANY] * 5, [ANY] * 5, DEAL_SEMS * 4 + GATHER_SEMS, 0, "entry")(
+        x, wq, wk, wv, gains
+    )
+
+
+def weights_kernel(wg, wu, wd, wo, cot, g_out, u_out, d_out, o_out, c_out, *refs):
+    refs = list(refs)
+    h = Here()
+    greet_all(h)
+    plan = Plan()
+    for src, out in ((wg, g_out), (wu, u_out), (wd, d_out)):
+        deal_columns(plan, h, src, out, take(refs, 5), 0, 100)
+    gather16(plan, h, wo, o_out.at[:, h.core], take(refs, 13), 0, 14, 18)
+    gather16(plan, h, cot, c_out, take(refs, 13), 10, 20, 28)
+    send, recv = take(refs, 2)
+    mine, other = o_out.at[:, h.core], o_out.at[:, 1 - h.core]
+    across = remote(mine, mine, send, recv, fsdp=1 - h.core)
+    plan.at(105, across.start)
+
+    def end():
+        remote(other, other, send, recv, fsdp=1 - h.core).wait_recv()
+        across.wait_send()
+
+    plan.at(200, end)
+    plan.run()
+
+
+def weights(wg, wu, wd, wo, cot):
+    rows, width = cot.shape
+    block = (16, 2, wg.shape[0], wg.shape[1] // 16)
+    outs = (
+        *[jax.ShapeDtypeStruct(block, BF)] * 3,
+        jax.ShapeDtypeStruct((16, 2) + wo.shape, BF),
+        jax.ShapeDtypeStruct((16, rows, width), BF),
+    )
+    return comm_call(
+        weights_kernel, outs, [ANY] * 5, [ANY] * 5, DEAL_SEMS * 3 + GATHER_SEMS * 2 + [DMA, DMA], 1, "weights"
+    )(wg, wu, wd, wo, cot)
+
+
+def to_tokens_kernel(src, out, *sems):
+    h = Here()
+    greet_all(h)
+    plan = Plan()
+    deal16(plan, h, lambda c: src.at[c], columns_of(out, 128), None, sems, 0, 8, both=False)
+    plan.run()
+
+
+def columns_of(out, width):
+    return lambda c: out.at[:, pl.ds(pl.multiple_of(c * width, 128), width)]
+
+
+def to_tokens(src):
+    ctx, rows, width = src.shape
+    outs = jax.ShapeDtypeStruct((rows, ctx * width), BF)
+    return comm_call(to_tokens_kernel, outs, ANY, [ANY], DEAL_SEMS, 2, "to_tokens")(src)
+
+
+def to_heads_kernel(src, out, *sems):
+    h = Here()
+    greet_all(h)
+    plan = Plan()
+    deal16(plan, h, columns(src, out.shape[2]), lambda c: out.at[c], None, sems, 0, 8, both=False)
+    plan.run()
+
+
+def to_heads(src):
+    rows, width = src.shape
+    outs = jax.ShapeDtypeStruct((16, rows, width // 16), BF)
+    return comm_call(to_heads_kernel, outs, ANY, [ANY], DEAL_SEMS, 3, "to_heads")(src)
+
+
+def gather_kernel(src, out, *sems):
+    h = Here()
+    greet_all(h)
+    plan = Plan()
+    gather16(plan, h, src, out, sems, 0, 12, 17)
+    plan.run()
+
+
+def gather(src):
+    outs = jax.ShapeDtypeStruct((16,) + src.shape, BF)
+    return comm_call(gather_kernel, outs, ANY, [ANY], GATHER_SEMS, 4, "gather")(src)
+
+
+def scatter_kernel(part, out, *scratch):
+    h = Here()
+    greet_all(h)
+    plan = Plan()
+    scatter16(plan, h, part, out, scratch, 0, 17)
+    plan.run()
+
+
+def scatter(part, cid):
+    rows, width = part.shape[0] // 16, part.shape[1]
+    outs = jax.ShapeDtypeStruct((rows, width), F32)
+    return comm_call(
+        scatter_kernel, outs, INNER, [INNER], scatter_scratch(rows, width), cid, f"scatter{cid}", 48
+    )(part.reshape(4, 2, 2, rows, width))
+
+
+def core_sum(plan, h, part, got, total, sems, t0, t1):
+    send, recv = sems
+    across = remote(part.at[:, 1 - h.core], got, send, recv, fsdp=1 - h.core)
+    plan.at(t0, across.start)
+
+    def add():
+        remote(part.at[:, h.core], got, send, recv, fsdp=1 - h.core).wait_recv()
+        for c in range(16):
+            total[c] = (part[c, h.core].astype(F32) + got[c].astype(F32)).astype(BF)
+        across.wait_send()
+
+    plan.at(t1, add)
+
+
+def home_kernel(*refs):
+    refs = list(refs)
+    parts, gains = take(refs, 6), take(refs, 1)[0]
+    outs, gains_out = take(refs, 6), take(refs, 1)[0]
+    h = Here()
+    greet_all(h)
+    plan = Plan()
+    for i, (part, out) in enumerate(zip(parts, outs)):
+        got, total = take(refs, 2)
+        core_sum(plan, h, part, got, total, take(refs, 2), 0.1 * i, 2 * i + 1)
+        deal16(
+            plan, h, lambda c, t=total: t.at[c], columns_of(out, part.shape[3]), None, take(refs, 5), 2 * i + 1.5, 90 + i,
+            both=False,
+        )
+    deal16(plan, h, lambda c: gains.at[c], lambda c: gains_out.at[c], None, take(refs, 5), 0, 20, both=False)
+    plan.run()
+
+
+def home(parts, gains):
+    scratch = []
+    for p in parts:
+        buffer = pltpu.VMEM((p.shape[0],) + p.shape[2:], BF)
+        scratch += [buffer, buffer, DMA, DMA] + DEAL_SEMS
+    outs = [jax.ShapeDtypeStruct((p.shape[2], 16 * p.shape[3]), BF) for p in parts]
+    outs.append(jax.ShapeDtypeStruct(gains.shape, F32))
+    return comm_call(
+        home_kernel, tuple(outs), [ANY] * 7, [INNER] * 7, scratch + DEAL_SEMS, 6, "home", 52
+    )(*parts, gains)
+
+
+def out_home_kernel(part, out, got, total, s, r, *scratch):
+    h = Here()
+    greet_all(h)
+    plan = Plan()
+    core_sum(plan, h, part, got, total, (s, r), 0, 1)
+    plan.run()
+    plan = Plan()
+    view = total.reshape(4, 2, 2, *total.shape[1:])
+    scatter16(plan, h, view, out, scratch, 2, 9)
+    plan.run()
+
+
+def out_home(part):
+    ctx, _, rows, width = part.shape
+    buffer = pltpu.VMEM((ctx, rows, width), BF)
+    outs = jax.ShapeDtypeStruct((rows, width), F32)
+    return comm_call(
+        out_home_kernel, outs, INNER, [INNER], [buffer, buffer, DMA, DMA] + scatter_scratch(rows, width), 7, "out_home", 48
+    )(part)
+
+
+def rope_tables(positions):
+    inv_freq = THETA_BASE ** (-(jnp.arange(HD // 2, dtype=F32) * 2.0 / HD))
+    angles = positions.astype(F32)[:, None] * inv_freq[None, :]
+    return jnp.tile(jnp.cos(angles), (1, 4)), jnp.tile(jnp.sin(angles), (1, 4))
+
+
+def swap(values):
+    a, b, c, d = jnp.split(values, 4, -1)
+    return jnp.concatenate([b, a, d, c], -1)
+
+
+def fast_body(x, table, attn_gain, wq, wk, wv, wo, mlp_gain, wg, wu, wd, cot):
+    x, cot, table = x[0], cot[0], table[0].reshape(32)
+    rows, width = x.shape
+    length = rows * 16
+    core = lax.axis_index("fsdp")
+    gains = jnp.pad(jnp.concatenate([attn_gain, mlp_gain])[None], ((0, 15), (0, 0)))
+    xg, bq, bk, bv, gains = entry(x, wq, wk, wv, gains)
+    gains = gains[:, :, 0].reshape(32, 2, 64).astype(F32)
+    again, mgain = gains[:, 0].reshape(width), gains[:, 1].reshape(width)
+    slots = jnp.arange(32, dtype=jnp.int32)
+    order = jnp.sum(jnp.where(table[None, :] == slots[:, None], slots[None, :], 0), 1)
+    positions = (table[:, None] * 64 + jnp.arange(64, dtype=jnp.int32)[None]).reshape(length)
+    cos, sin = rope_tables(positions)
+    turn = jnp.where(jnp.arange(128) % 64 < 32, -1.0, 1.0).astype(F32)
+    sin = sin * turn
+
+    source = xg.reshape(length, width).astype(F32)
+    inv_all = lax.rsqrt(jnp.mean(source * source, -1, keepdims=True) + EPSILON)
+    normed = (source * inv_all * again).astype(BF)
+    bq, bk, bv = (b.reshape(width, 128) for b in (bq, bk, bv))
+
+    def dot(a, b):
+        return jnp.dot(a, b, preferred_element_type=F32)
+
+    def dot_nt(a, b):
+        return lax.dot_general(a, b, (((1,), (1,)), ((), ())), preferred_element_type=F32)
+
+    def dot_tn(a, b):
+        return lax.dot_general(a, b, (((0,), (0,)), ((), ())), preferred_element_type=F32)
+
+    qkv = dot(normed, jnp.concatenate([bq, bk, bv], 1))
+    q, k, v = qkv[:, :128], qkv[:, 128:256], qkv[:, 256:].astype(BF)
+    q = (q * cos + swap(q) * sin).astype(BF)
+    k = (k * cos + swap(k) * sin).astype(BF)
+    o, lse, qs, ks, vs = attention(order, table, q, k, v)
+    bg, bu, bd, full_out, cot_all = weights(wg, wu, wd, wo, cot)
+    full_out = full_out.reshape(width, width)
+    bg, bu, bd = (b.reshape(width, b.shape[3]) for b in (bg, bu, bd))
+    cot_all = cot_all.reshape(length, width)
+    attn_low = to_tokens(o.reshape(16, rows, 128))
+    own = x.astype(F32)
+    inv_in = lax.rsqrt(jnp.mean(own * own, -1, keepdims=True) + EPSILON)
+    hidden = own + dot(attn_low, full_out)
+    inv_mid = lax.rsqrt(jnp.mean(hidden * hidden, -1, keepdims=True) + EPSILON)
+    mlp_in = gather((hidden * inv_mid * mgain).astype(BF)).reshape(length, width)
+    gate, up = dot(mlp_in, bg), dot(mlp_in, bu)
+    sig = jax.nn.sigmoid(gate)
+    act = (gate * sig * up).astype(BF)
+    out_part = dot_nt(act, bd).astype(BF)
+    grad_act = dot(cot_all, bd)
+    grad_gate = (grad_act * up * sig * (1.0 + gate * (1.0 - sig))).astype(BF)
+    grad_up = (grad_act * gate * sig).astype(BF)
+    gmi_part = (dot_nt(grad_gate, bg) + dot_nt(grad_up, bu)).astype(BF)
+    gmi = scatter(gmi_part, 5)
+    layer_output = (hidden + scatter(out_part, 8)).astype(BF)
+
+    def norm_back(grad, source, inv, gain):
+        scaled = grad * gain
+        inner = jnp.sum(scaled * source, -1, keepdims=True)
+        return inv * scaled - inv * inv * inv / width * source * inner
+
+    mgain_part = jnp.sum(gmi * hidden * inv_mid, 0)
+    grad_hidden = cot.astype(F32) + norm_back(gmi, hidden, inv_mid, mgain)
+    grad_branch = grad_hidden.astype(BF)
+    grad_att = to_heads(dot_nt(grad_branch, full_out).astype(BF)).reshape(length, 128)
+    dq, dk, dv = attention_back(order, table, qs, ks, vs, grad_att, lse)
+    dq = (dq * cos - swap(dq) * sin).astype(BF)
+    dk = (dk * cos - swap(dk) * sin).astype(BF)
+    grad_qkv = jnp.concatenate([dq, dk, dv.astype(BF)], 1)
+    gn_part = dot_nt(grad_qkv, jnp.concatenate([bq, bk, bv], 1)).astype(BF)
+    gn = scatter(gn_part, 9)
+    input_grad = grad_hidden + norm_back(gn, own, inv_in, again)
+    again_part = jnp.sum(gn * own * inv_in, 0)
+    gains = jnp.stack([again_part, mgain_part]).reshape(2, 16, 128).transpose(1, 0, 2)
+    gains = jnp.pad(gains, ((0, 0), (0, 6), (0, 0)))
+
+    def pieces(grad):
+        return grad.astype(BF).reshape(16, 2, 64, grad.shape[1])
+
+    wo_grad = out_home(pieces(dot_tn(attn_low, grad_branch)))
+    parts = [
+        pieces(dot_tn(normed, dq)),
+        pieces(dot_tn(normed, dk)),
+        pieces(dot_tn(normed, dv.astype(BF))),
+        pieces(dot_tn(mlp_in, grad_gate)),
+        pieces(dot_tn(mlp_in, grad_up)),
+        pieces(dot_tn(cot_all, act)),
+    ]
+    *grads, gains = home(parts, gains)
+    gq, gk, gv, gg, gu, gd = (g.astype(F32) for g in grads)
+    gains = lax.psum(jnp.sum(gains, 0), "fsdp")
+    gains = lax.dynamic_slice_in_dim(gains, core * 64, 64, 1)
+    return (layer_output[None], input_grad[None], gains[0], gq, gk, gv, wo_grad, gains[1], gg, gu, gd)
+
+
 MASKED = -1e30
 
 
-def rope_tables(positions):
+def general_tables(positions):
     inv_freq = THETA_BASE ** (-(jnp.arange(HD // 2, dtype=jnp.float32) * 2.0 / HD))
     angles = positions.astype(jnp.float32)[:, None] * inv_freq[None, :]
     cosine = jnp.cos(angles)
@@ -37,7 +784,7 @@
     return lax.rsqrt(jnp.mean(rows_in * rows_in, -1, keepdims=True) + EPSILON)
 
 
-def norm_back(grad_normed, rows_in, inverse, gain_vec):
+def general_norm_back(grad_normed, rows_in, inverse, gain_vec):
     scaled = grad_normed * gain_vec
     inner_sum = jnp.sum(scaled * rows_in, -1, keepdims=True)
     return inverse * scaled - inverse * inverse * inverse / rows_in.shape[-1] * rows_in * inner_sum
@@ -80,7 +827,7 @@
     return final_state
 
 
-def body(
+def general_body(
     layer_input,
     block_table,
     attn_gain,
@@ -104,7 +851,7 @@
     own_blocks = lax.dynamic_slice_in_dim(block_ids, lax.axis_index("ctx") * 2, 2)
     inner = jnp.arange(half_rows, dtype=jnp.int32)
     query_pos = (own_blocks[:, None] * half_rows + inner[None, :]).reshape(tokens)
-    cosine, sine_tab = rope_tables(query_pos)
+    cosine, sine_tab = general_tables(query_pos)
     full_query, full_key, full_value, full_out, full_attn_gain = (
         lax.all_gather(query_weight, ("ctx", "fsdp"), axis=0, tiled=True),
         lax.all_gather(key_weight, ("ctx", "fsdp"), axis=0, tiled=True),
@@ -127,9 +874,10 @@
     kv_dev = lax.all_gather(jnp.concatenate([keys_low, value_low], 1), "ctx", axis=0, tiled=True)
     slot_ids = jnp.arange(2 * ranks, dtype=jnp.int32)
     holder = jnp.sum(jnp.where(block_ids[None, :] == slot_ids[:, None], slot_ids[None, :], 0), 1)
-    kv_seq = jnp.take(kv_dev.reshape(2 * ranks, half_rows, 2 * width), holder, axis=0).reshape(
-        length, 2 * width
-    )
+    chosen = (holder[:, None] == slot_ids[None, :]).astype(jnp.bfloat16)
+    kv_seq = jnp.einsum(
+        "ab,bn->an", chosen, kv_dev.reshape(2 * ranks, half_rows * 2 * width)
+    ).reshape(length, 2 * width)
     step_rows = min(512, length)
     kv_steps = kv_seq.reshape(length // step_rows, step_rows, 2 * width)
     log_totals = []
@@ -205,7 +953,7 @@
         "tf,df->td", grad_gate, back_gate, preferred_element_type=jnp.float32
     ) + jnp.einsum("tf,df->td", grad_up, back_up, preferred_element_type=jnp.float32)
     mlp_gain_term = jnp.sum(grad_mlp_in * hidden * inverse_mid, 0)
-    grad_hidden = grad_out_low.astype(jnp.float32) + norm_back(
+    grad_hidden = grad_out_low.astype(jnp.float32) + general_norm_back(
         grad_mlp_in, hidden, inverse_mid, back_mlp_gain.astype(jnp.float32)
     )
     grad_branch = grad_hidden.astype(jnp.bfloat16)
@@ -266,8 +1014,7 @@
     stats_both = lax.all_gather(
         jnp.stack([log_all.T, delta_all.T], 1).astype(jnp.bfloat16), "ctx", axis=0, tiled=True
     ).astype(jnp.float32)
-    all_rows = jnp.arange(length, dtype=jnp.int32)
-    all_pos = jnp.take(block_ids, all_rows // half_rows) * half_rows + all_rows % half_rows
+    all_pos = (block_ids[:, None] * half_rows + inner[None, :]).reshape(length)
     own_keys = keys_low.reshape(tokens, HEADS, HD)
     own_values = value_low.reshape(tokens, HEADS, HD)
 
@@ -335,7 +1082,7 @@
         "te,de->td", grad_value_low, back_value, preferred_element_type=jnp.float32
     )
     attn_gain_term = jnp.sum(grad_normed * source * inverse_in, 0)
-    input_grad = grad_hidden + norm_back(
+    input_grad = grad_hidden + general_norm_back(
         grad_normed, source, inverse_in, back_attn_gain.astype(jnp.float32)
     )
 
@@ -383,35 +1130,13 @@
 
 
 def solution(mesh):
+    both = ("ctx", "fsdp")
+    rows = P(both, None)
+    tokens = P("fsdp", "ctx", None)
     return jax.shard_map(
-        body,
+        fast_body if mesh.shape["ctx"] == 16 and mesh.shape["fsdp"] == 2 else general_body,
         mesh=mesh,
-        in_specs=(
-            P("fsdp", "ctx", None),
-            P("fsdp", None, None),
-            P(("ctx", "fsdp")),
-            P(("ctx", "fsdp"), None),
-            P(("ctx", "fsdp"), None),
-            P(("ctx", "fsdp"), None),
-            P(("ctx", "fsdp"), None),
-            P(("ctx", "fsdp")),
-            P(("ctx", "fsdp"), None),
-            P(("ctx", "fsdp"), None),
-            P(("ctx", "fsdp"), None),
-            P("fsdp", "ctx", None),
-        ),
-        out_specs=(
-            P("fsdp", "ctx", None),
-            P("fsdp", "ctx", None),
-            P(("ctx", "fsdp")),
-            P(("ctx", "fsdp"), None),
-            P(("ctx", "fsdp"), None),
-            P(("ctx", "fsdp"), None),
-            P(("ctx", "fsdp"), None),
-            P(("ctx", "fsdp")),
-            P(("ctx", "fsdp"), None),
-            P(("ctx", "fsdp"), None),
-            P(("ctx", "fsdp"), None),
-        ),
+        in_specs=(tokens, P("fsdp", None, None), P(both), rows, rows, rows, rows, P(both), rows, rows, rows, tokens),
+        out_specs=(tokens, tokens, P(both), rows, rows, rows, rows, P(both), rows, rows, rows),
         check_vma=False,
     )

time: 4500 us -> 968 us (0.22)
  waiting for transfers between devices: 3650 us -> 0 us
  Pallas kernels: 0 us -> 787 us
  matrix products: 410 us -> 125 us
  local copies, waits for them, and re-layouts: 243 us -> 12.2 us
  blocking collectives: 75.2 us -> 3.75 us
    reduce_scatter x1 -> x0, waiting for transfers between devices: 2810 us -> none  [body(): lax.psum_scatter(jnp.concatenate([outer_sum(normed, grad_query_low), oute...]
    all_gather x9 -> x0, waiting for transfers between devices: 829 us -> none  [the longest x1 180 us: body(): lax.all_gather(jnp.concatenate([keys_low, value_low], 1), 'ctx', axis=0,...]
    pallas_call x0 -> x12, Pallas kernels: none -> 787 us  [the longest x3 235 us: scatter(): comm_call(scatter_kernel, outs, INNER, [INNER], scatter_scratch(rows, wid...]
    dot_general x53 -> x17, matrix products: 410 us -> 125 us  [the longest x5 44.9 us: dot_nt(): lax.dot_general(a, b, (((1,), (1,)), ((), ())), preferred_element_type=F32)]
    slice x29 -> x2, local copies, waits for them, and re-layouts: 56.9 us -> 0.14 us  [the longest x1 0.09 us: fast_body(): again, mgain = (gains[:, 0].reshape(width), gains[:, 1].reshape(width))]
    unnamed x136 -> x66, local copies, waits for them, and re-layouts: 53.5 us -> 3.14 us
  transfers between devices with their start and end apart: 11 -> 0, of which waited for: 9 -> 0; matrix products, arithmetic and copies ran while one was open for 11% -> 0% of each run, Pallas kernels for 0% -> 0%
where the time goes in v1:
time: 968 us; the launch traced here: 961 us
  Pallas kernels  787 us (81%)
  matrix products  125 us (13%)
  other arithmetic  31.1 us (3%)
  local copies, waits for them, and re-layouts  12.2 us (1%)
    pallas_call x3, Pallas kernels, scatter(): comm_call(scatter_kernel, outs, INNER, [INNER], scatter_scratch(rows, wid...  235 us
    pallas_call x1, Pallas kernels, weights(): comm_call(weights_kernel, outs, [ANY] * 5, [ANY] * 5, DEAL_SEMS * 3 + GAT...  167 us
    pallas_call x1, Pallas kernels, home(): comm_call(home_kernel, tuple(outs), [ANY] * 7, [INNER] * 7, scratch + DEA...  100 us
    pallas_call x1, Pallas kernels, entry(): comm_call(entry_kernel, outs, [ANY] * 5, [ANY] * 5, DEAL_SEMS * 4 + GATHE...  89.2 us
    pallas_call x1, Pallas kernels, gather(): comm_call(gather_kernel, outs, ANY, [ANY], GATHER_SEMS, 4, 'gather')(src)  69.4 us
    pallas_call x1, Pallas kernels, out_home(): comm_call(out_home_kernel, outs, INNER, [INNER], [buffer, buffer, DMA, DM...  55 us
    dot_general x5, matrix products, dot_nt(): lax.dot_general(a, b, (((1,), (1,)), ((), ())), preferred_element_type=F32)  44.9 us
    dot_general x7, matrix products, dot_tn(): lax.dot_general(a, b, (((0,), (0,)), ((), ())), preferred_element_type=F32)  43 us

profile of v1, /device:TPU:9, one launch (start us, length us, event | category | flops | bytes accessed | tf_op | source)
XLA Modules:
  0.0 961.0 jit_solution(14235436505434719386)
XLA Ops:
  8.3 89.2 %entry.1 = (bf16[16,128,2048]{2,1,0:T(8,128)(2,1)S(1)}, bf16[16,2,64,128]{3,2,1,0:T(8,128)(2,1)S(1)}, bf16[16,2,64,128]{3,2,1,0:T(8,128)(2,1)S(1)}, bf16[16,2,64...) custom-call(bf16[128,2048]{1,0:T(8,128)(2,1)S(1)} %bitcast.82, bf16[64,2048]{1,0:T(8,128)(2,1)S(1)} %copy-done.6, ...), custom_call_target="tpu_custom_call" | custom-call | tf_op jit(solution)/shard_map/entry/pallas_call | solution.py:487
  101.1 8.6 fusion.1
  109.7 7.1 fusion.23
  120.5 10.4 %attention.1 = (bf16[2048,128]{1,0:T(8,128)(2,1)S(1)}, f32[2,2048]{1,0:T(2,128)S(1)}, bf16[2048,128]{1,0:T(8,128)(2,1)S(1)}, bf16[2048,128]{1,0:T(8,128)(2,1)S(1)}, bf16[2048,128]{1,0:T(8,128)(2,1)S(1)}) custom-call(s32[32]{0:T(128)S(1)} %select_reduce_fusion.order, s32[32]{0:T(128)S(1)} %eq.17.table, bf16[2048,128]{1,0:T(8,128)(2,1)S(1)} %get-tuple-element.71.q, ...), custom_call_target="tpu_custom_call" | custom-call | tf_op jit(solution)/shard_map/attention/pallas_call | solution.py:395
  130.8 20.9 %to_tokens.1 = bf16[128,2048]{1,0:T(8,128)(2,1)S(1)} custom-call(bf16[16,128,128]{2,1,0:T(8,128)(2,1)S(1)} %bitcast.89), custom_call_target="tpu_custom_call" | custom-call | tf_op jit(solution)/shard_map/to_tokens/pallas_call | solution.py:542
  151.8 166.9 %weights.1 = (bf16[16,2,64,512]{3,2,1,0:T(8,128)(2,1)S(1)}, bf16[16,2,64,512]{3,2,1,0:T(8,128)(2,1)S(1)}, bf16[16,2,64,512]{3,2,1,0:T(8,128)(2,1)S(1)}, bf16[16,...) custom-call(bf16[64,8192]{1,0:T(8,128)(2,1)S(1)} %copy-done.3, bf16[64,8192]{1,0:T(8,128)(2,1)S(1)} %copy-done.4, ...), custom_call_target="tpu_custom_call" | custom-call | tf_op jit(solution)/shard_map/weights/pallas_call | solution.py:522
  318.8 5.6 multiply_reduce_fusion.3
  324.5 69.4 %gather.1 = bf16[16,128,2048]{2,1,0:T(8,128)(2,1)S(1)} custom-call(bf16[128,2048]{1,0:T(8,128)(2,1)S(1)} %multiply_convert_fusion.3.src), custom_call_target="tpu_custom_call" | custom-call | tf_op jit(solution)/shard_map/gather/pallas_call | solution.py:569
  394.0 6.0 fusion.35
  400.0 6.0 fusion.34
  406.0 12.6 %multiply_convert_fusion = (bf16[2048,512]{1,0:T(8,128)(2,1)}, bf16[2048,512]{1,0:T(8,128)(2,1)S(1)}, bf16[2048,512]{1,0:T(8,128)(2,1)}) fusion(f32[2048,512]{1,0:T(8,128)} %fusion.34, f32[2048,512]{1,0:T(8,128)} %fusion.35, bf16[2048,2048]{1,0:T(8,128)(2,1)} %bitcast.120, bf16[2048,512]{1,0:T(8,128)(2,1)S(1)} %bitcast.96), kind=kOutput, calls=%fused_computation.8 | convolution fusion | flops 4311744512 | bytes 25165824 | tf_op jit(solution)/shard_map/dot_general | solution.py:686
  418.5 10.7 %convolution_convert_fusion.3 = bf16[2048,512]{1,0:T(8,128)(2,1)} fusion(bf16[2048,2048]{1,0:T(8,128)(2,1)} %bitcast.121, bf16[2048,512]{1,0:T(8,128)(2,1)} %get-tuple-element.69), kind=kOutput, calls=%fused_computation.12 | convolution fusion | flops 4296015872 | bytes 12582912 | tf_op jit(solution)/shard_map/dot_general | solution.py:692
  429.3 5.8 convolution_convert_fusion.4
  435.1 5.7 convolution_convert_fusion.5
  440.8 8.4 convolution_convert_fusion.1
  449.2 78.2 %scatter8.1 = f32[128,2048]{1,0:T(8,128)S(1)} custom-call(bf16[4,2,2,128,2048]{4,3,2,1,0:T(8,128)(2,1)} %bitcast.111), custom_call_target="tpu_custom_call" | custom-call | tf_op jit(solution)/shard_map/scatter8/pallas_call | solution.py:583
  527.4 8.6 fusion.36
  536.0 14.8 %add_convert_fusion = bf16[2048,2048]{1,0:T(8,128)(2,1)} fusion(f32[2048,2048]{1,0:T(8,128)} %fusion.36, bf16[2048,512]{1,0:T(8,128)(2,1)} %get-tuple-element.67, bf16[2048,512]{1,0:T(8,128)(2,1)} %bitcast.93), kind=kOutput, calls=%fused_computation.3 | convolution fusion | flops 4303355904 | bytes 29360128 | tf_op jit(solution)/shard_map/dot_general | solution.py:689
  550.8 75.5 %scatter5.1 = f32[128,2048]{1,0:T(8,128)S(1)} custom-call(bf16[4,2,2,128,2048]{4,3,2,1,0:T(8,128)(2,1)} %bitcast.110), custom_call_target="tpu_custom_call" | custom-call | tf_op jit(solution)/shard_map/scatter5/pallas_call | solution.py:583
  627.9 6.3 convolution_convert_fusion.9.src
  634.1 22.9 %to_heads.1 = bf16[16,128,128]{2,1,0:T(8,128)(2,1)S(1)} custom-call(bf16[128,2048]{1,0:T(8,128)(2,1)S(1)} %convolution_convert_fusion.9.src), custom_call_target="tpu_custom_call" | custom-call | tf_op jit(solution)/shard_map/to_heads/pallas_call | solution.py:556
  657.0 17.6 %attention_back.1 = (f32[2048,128]{1,0:T(8,128)S(1)}, f32[2048,128]{1,0:T(8,128)S(1)}, f32[2048,128]{1,0:T(8,128)S(1)}) custom-call(s32[32]{0:T(128)S(1)} %select_reduce_fusion.order, s32[32]{0:T(128)S(1)} %eq.17.table, bf16[2048,128]{1,0:T(8,128)(2,1)S(1)} %get-tuple-element.47.qs, bf16[2048,128]{1,0:T(8,128)(2,1)S(1)} %get-tuple-element.48.ks, ...), custom_call_target="tpu_custom_call" | custom-call | tf_op jit(solution)/shard_map/attention_back/pallas_call | solution.py:412
  674.7 6.6 convolution_convert_fusion.6
  681.2 5.6 convolution_convert_fusion.2
  686.8 55.0 %out_home.1 = f32[64,2048]{1,0:T(8,128)S(1)} custom-call(bf16[16,2,64,2048]{3,2,1,0:T(8,128)(2,1)} %bitcast.106), custom_call_target="tpu_custom_call" | custom-call | tf_op jit(solution)/shard_map/out_home/pallas_call | solution.py:648
  741.8 3.3 fusion.32
  745.2 3.6 fusion.20
  751.5 5.9 convolution_convert_fusion.7
  757.4 6.8 convolution_convert_fusion
  764.2 81.0 %scatter9.1 = f32[128,2048]{1,0:T(8,128)S(1)} custom-call(bf16[4,2,2,128,2048]{4,3,2,1,0:T(8,128)(2,1)} %bitcast.109), custom_call_target="tpu_custom_call" | custom-call | tf_op jit(solution)/shard_map/scatter9/pallas_call | solution.py:583
  847.0 100.3 %home.1 = (bf16[64,2048]{1,0:T(8,128)(2,1)S(1)}, bf16[64,2048]{1,0:T(8,128)(2,1)S(1)}, bf16[64,2048]{1,0:T(8,128)(2,1)S(1)}, bf16[64,8192]{1,0:T(8,128)(2,1)}, b...) custom-call(bf16[16,2,64,128]{3,2,1,0:T(8,128)(2,1)S(1)} %bitcast.90, ...), custom_call_target="tpu_custom_call" | custom-call | tf_op jit(solution)/shard_map/home/pallas_call | solution.py:627
  947.3 3.7 psum.7
  (112 shorter events, 30.4 us)
Async XLA Ops:
  0.6 7.6 copy-start.1
  0.7 7.6 copy-start.8
  0.7 7.6 copy-start.7
  0.7 7.6 copy-start.6
  97.5 3.2 copy-start
  97.5 12.2 %copy-start.11 = (bf16[16,2,64,128]{3,2,1,0:T(8,128)(2,1)}, bf16[16,2,64,128]{3,2,1,0:T(8,128)(2,1)S(1)}, u32[]{:S(2)}) copy-start(bf16[16,2,64,128]{3,2,1,0:T(8,128)(2,1)S(1)} %get-tuple-element.39) | copy-start | bytes 1572868
  97.5 12.1 %copy-start.13 = (bf16[16,2,64,128]{3,2,1,0:T(8,128)(2,1)}, bf16[16,2,64,128]{3,2,1,0:T(8,128)(2,1)S(1)}, u32[]{:S(2)}) copy-start(bf16[16,2,64,128]{3,2,1,0:T(8,128)(2,1)S(1)} %get-tuple-element.40) | copy-start | bytes 1572868
  101.1 8.6 copy-start.23
  116.8 1.8 copy-start.17
  116.9 1.8 copy-start.19
  118.6 33.2 %copy-start.2 = (bf16[1,128,2048]{2,1,0:T(8,128)(2,1)S(1)}, bf16[1,128,2048]{2,1,0:T(8,128)(2,1)}, u32[]{:S(2)}) copy-start(bf16[1,128,2048]{2,1,0:T(8,128)(2,1)} %param.23) | copy-start | bytes 1572868
  118.7 33.2 %copy-start.3 = (bf16[64,8192]{1,0:T(8,128)(2,1)S(1)}, bf16[64,8192]{1,0:T(8,128)(2,1)}, u32[]{:S(2)}) copy-start(bf16[64,8192]{1,0:T(8,128)(2,1)} %wg.1) | copy-start | bytes 3145732
  118.7 33.1 %copy-start.4 = (bf16[64,8192]{1,0:T(8,128)(2,1)S(1)}, bf16[64,8192]{1,0:T(8,128)(2,1)}, u32[]{:S(2)}) copy-start(bf16[64,8192]{1,0:T(8,128)(2,1)} %wu.1) | copy-start | bytes 3145732
  118.7 33.1 %copy-start.5 = (bf16[64,8192]{1,0:T(8,128)(2,1)S(1)}, bf16[64,8192]{1,0:T(8,128)(2,1)}, u32[]{:S(2)}) copy-start(bf16[64,8192]{1,0:T(8,128)(2,1)} %wd.1) | copy-start | bytes 3145732
  118.7 33.1 %copy-start.9 = (bf16[64,2048]{1,0:T(8,128)(2,1)S(1)}, bf16[64,2048]{1,0:T(8,128)(2,1)}, u32[]{:S(2)}) copy-start(bf16[64,2048]{1,0:T(8,128)(2,1)} %wo.1) | copy-start | bytes 786436
  318.8 75.2 %copy-start.10 = (bf16[16,2,64,512]{3,2,1,0:T(8,128)(2,1)}, bf16[16,2,64,512]{3,2,1,0:T(8,128)(2,1)S(1)}, u32[]{:S(2)}) copy-start(bf16[16,2,64,512]{3,2,1,0:T(8,128)(2,1)S(1)} %get-tuple-element.44) | copy-start | bytes 6291460
  324.4 69.6 %copy-start.15 = (f32[128,2048]{1,0:T(8,128)}, f32[128,2048]{1,0:T(8,128)S(1)}, u32[]{:S(2)}) copy-start(f32[128,2048]{1,0:T(8,128)S(1)} %get-tuple-element.101) | copy-start | bytes 3145732
  418.5 16.5 %copy-start.27 = (bf16[2048,512]{1,0:T(8,128)(2,1)}, bf16[2048,512]{1,0:T(8,128)(2,1)S(1)}, u32[]{:S(2)}) copy-start(bf16[2048,512]{1,0:T(8,128)(2,1)S(1)} %get-tuple-element.68) | copy-start | bytes 6291460
  418.5 10.7 %copy-start.29 = (bf16[2048,512]{1,0:T(8,128)(2,1)S(1)}, bf16[2048,512]{1,0:T(8,128)(2,1)}, u32[]{:S(2)}) copy-start(bf16[2048,512]{1,0:T(8,128)(2,1)} %get-tuple-element.67) | copy-start | bytes 6291460
  449.2 78.2 %copy-start.28 = (bf16[2048,512]{1,0:T(8,128)(2,1)S(1)}, bf16[2048,512]{1,0:T(8,128)(2,1)}, u32[]{:S(2)}) copy-start(bf16[2048,512]{1,0:T(8,128)(2,1)} %copy-done.27) | copy-start | bytes 6291460
  550.8 75.6 %copy-start.16 = (f32[128,2048]{1,0:T(8,128)S(1)}, f32[128,2048]{1,0:T(8,128)}, u32[]{:S(2)}) copy-start(f32[128,2048]{1,0:T(8,128)} %copy-done.15) | copy-start | bytes 3145732
  686.8 61.9 %slice-start = ((s8[8388608]{0:T(1024)(128)(4,1)}), s8[4194304]{0:T(1024)(128)(4,1)S(1)}, s32[]{:S(2)}) async-start(s8[8388608]{0:T(1024)(128)(4,1)} %bitcast.107), calls=%async_computation | async-start | bytes 8388608
  741.8 3.4 copy-start.18
  741.8 3.4 copy-start.20
  741.8 6.9 slice-start.1
  751.5 5.9 copy-start.12
  751.5 5.9 copy-start.14
  764.2 81.0 %copy-start.24 = (f32[2048]{0:T(1024)S(1)}, f32[2048]{0:T(1024)}, u32[]{:S(2)}) copy-start(f32[2048]{0:T(1024)} %copy-done.23) | copy-start | bytes 24580
  764.2 81.0 %copy-start.25 = (f32[128]{0:T(128)S(1)}, f32[128]{0:T(128)}, u32[]{:S(2)}) copy-start(f32[128]{0:T(128)} %get-tuple-element.97) | copy-start | bytes 1540
  764.2 81.3 %copy-start.26 = (f32[128]{0:T(128)S(1)}, f32[128]{0:T(128)}, u32[]{:S(2)}) copy-start(f32[128]{0:T(128)} %get-tuple-element.96) | copy-start | bytes 1540
  947.3 9.5 copy-start.22
  951.7 6.6 copy-start.21

commit v2 on v1

--- a/solution.py
+++ b/solution.py
@@ -51,7 +51,7 @@
 GATHER_SEMS = [DMA((4,))] * 12 + [DMA]
 
 
-def gather16(plan, h, src, out, sems, t0, tz, tx):
+def gather16(plan, h, src, out, sems, t0, tz, tx, by_plane=False):
     us, ur, ds, dr, xs, xr, ys, yr, xfs, xfr, yfs, yfr, own = sems
     half = src.shape[0] // 2
 
@@ -134,17 +134,19 @@
             plan.at(t0 + (k + 0.8) * tx, lambda v=valid, q=zz: pl.when(v())(lambda: forward(q())))
 
     def drain():
-        for zz in range(4):
-            finish(zz)
+        if not by_plane:
+            for zz in range(4):
+                finish(zz)
         for k in range(3):
             pl.when((h.z >= k) & (h.z < 3))(lambda: hop(k, True).wait_send())
             pl.when((h.z + k <= 3) & (h.z > 0))(lambda: hop(k, False).wait_send())
         for zz in range(4):
             for c in plane(zz) + across(zz):
                 c.wait_send()
-        local.wait()
-
+
+    plan.at(t0 + 0.85 * tx, local.wait)
     plan.at(t0 + 4.5 * tx, drain)
+    return finish
 
 
 SCATTER_SEMS = [DMA((4,))] * 8 + [DMA((4,))] * 2
@@ -165,7 +167,7 @@
 
 
 N_SCATTER = 18
-AHEAD = 2
+AHEAD = 1
 
 
 def scatter16(plan, h, part, out, scratch, t0, tx):
@@ -177,7 +179,7 @@
     xo, yo = 1 - h.x, 1 - h.y
 
     def place(k):
-        return lax.rem(h.z + k, 4)
+        return jnp.bitwise_xor(h.z, k)
 
     def first(i, k):
         return (
@@ -228,11 +230,11 @@
         out[...] += rz[0].astype(F32) + rz[1].astype(F32) + rz[2].astype(F32)
         for k in (1, 2, 3):
             third(k).wait_send()
-        for i, k in enumerate((2, 1, 3, 0)):
+        for i, k in enumerate((1, 2, 3, 0)):
             for c in first(i, k) + second(i):
                 c.wait_send()
 
-    for i, k in enumerate((2, 1, 3, 0)):
+    for i, k in enumerate((1, 2, 3, 0)):
         plan.at(t0 + max(0, i - AHEAD + 0.71) * tx if i >= AHEAD else t0 + 0.01 * i, functools.partial(start, i, k))
         plan.at(t0 + i * tx + 0.7 * tx, functools.partial(middle, i, k))
         plan.at(t0 + i * tx + 1.35 * tx, functools.partial(total, i, k))
@@ -242,7 +244,7 @@
 DEAL_SEMS = [DMA((16,))] * 4 + [DMA]
 
 
-def deal16(plan, h, piece, put, passed, sems, t0, t1, both=True):
+def deal16(plan, h, piece, put, passed, sems, t0, t1, both=True, pace=0.0, relay_from=None):
     ss, sr, fs, fr, own = sems
 
     def send(step):
@@ -264,21 +266,21 @@
     local = pltpu.make_async_copy(piece(h.me), put(h.me), own)
 
     def first():
-        for step in ORDER:
-            send(step).start()
         local.start()
         if both:
             hand(0).start()
 
     plan.at(t0, first)
     for i, step in enumerate(ORDER):
+        plan.at(t0 + pace * i, lambda step=step: send(step).start())
 
         def relay(step=step):
             got(step).wait_recv()
             if both:
                 hand(step).start()
 
-        plan.at(t0 + (t1 - t0) * (i + 1) / 15, relay)
+        since = t0 if relay_from is None else relay_from
+        plan.at(since + (t1 - since) * (i + 1) / 15 if both else t1, relay)
 
     def drain():
         if both:
@@ -287,12 +289,12 @@
                 hand(step).wait_send()
         for step in ORDER:
             send(step).wait_send()
-        local.wait()
-
+
+    plan.at(t1, local.wait)
     plan.at(t1 + 2, drain)
 
 
-ORDER = (1, 2, 3, 4, 5, 6, 7, 8, 9, 10, 11, 12, 13, 14, 15)
+ORDER = (12, 8, 13, 9, 14, 10, 15, 11, 4, 5, 6, 7, 3, 1, 2)
 
 ROWS = 256
 
@@ -328,99 +330,51 @@
     return low if n == ROWS else jnp.concatenate([scores[: n - ROWS], low], 0)
 
 
-def sort_rows(order_ref, src, dst, blk=64):
-    for b in range(src.shape[0] // blk):
-        at = pl.multiple_of(order_ref[b] * blk, blk)
-        dst[b * blk : (b + 1) * blk, :] = src[pl.ds(at, blk), :]
-
-
-def attend(qs, ks, vs, os, lse):
+def sort_rows(order_ref, src, dst):
+    for b in range(src.shape[0]):
+        dst[b * 64 : (b + 1) * 64, :] = src[order_ref[b]]
+
+
+def attend_step(i, qs, ks, vs, os, lse):
     tri = _tri()
-    for i in range(qs.shape[0] // ROWS):
-        n = (i + 1) * ROWS
-        mine = slice(i * ROWS, n)
-        total = None
-        for head, query in enumerate(_heads(qs[mine, :] * BF(0.125))):
-            scores = _scores(ks[:n, :], query, tri)
-            top = jnp.max(scores, 0, keepdims=True)
-            raw = jnp.exp(scores - top)
-            size = jnp.sum(raw, 0, keepdims=True)
-            lse[head : head + 1, mine] = top + jnp.log(size)
-            probs = (raw * (1.0 / size)).astype(BF)
-            part = _tn(probs, _heads(vs[:n, :])[head])
-            total = part if total is None else total + part
-        os[mine, :] = total.astype(BF)
-
-
-def attend_back(qs, ks, vs, gs, lse, dq, dk, dv):
+    n = (i + 1) * ROWS
+    mine = slice(i * ROWS, n)
+    total = None
+    for head, query in enumerate(_heads(qs[mine, :] * BF(0.125))):
+        scores = _scores(ks[:n, :], query, tri)
+        top = jnp.max(scores, 0, keepdims=True)
+        raw = jnp.exp(scores - top)
+        size = jnp.sum(raw, 0, keepdims=True)
+        lse[head : head + 1, mine] = top + jnp.log(size)
+        probs = (raw * (1.0 / size)).astype(BF)
+        part = _tn(probs, _heads(vs[:n, :])[head])
+        total = part if total is None else total + part
+    os[mine, :] = total.astype(BF)
+
+
+def back_step(i, qs, ks, vs, gs, lse, dq, dk, dv):
     tri = _tri()
-    dk[...] = jnp.zeros_like(dk)
-    dv[...] = jnp.zeros_like(dv)
-    for i in range(qs.shape[0] // ROWS):
-        n = (i + 1) * ROWS
-        mine = slice(i * ROWS, n)
-        total = None
-        queries = _heads(qs[mine, :] * BF(0.125))
-        grads = _heads(gs[mine, :])
-        for head in range(2):
-            scores = _scores(ks[:n, :], queries[head], tri)
-            probs = jnp.exp(scores - lse[head : head + 1, mine])
-            gp = _nt(vs[:n, :], grads[head])
-            delta = jnp.sum(probs * gp, 0, keepdims=True)
-            ds = (probs * (gp - delta)).astype(BF)
-            dv[:n, :] += _nn(probs.astype(BF), grads[head])
-            dk[:n, :] += _nn(ds, queries[head])
-            part = _tn(ds, _heads(ks[:n, :])[head])
-            total = part if total is None else total + part
-        dq[mine, :] = total * 0.125
-
-
-def fwd_kernel(order, table, q, k, v, o, lse, qs, ks, vs, os):
-    for a, b in ((q, qs), (k, ks), (v, vs)):
-        sort_rows(order, a, b)
-    attend(qs, ks, vs, os, lse)
-    sort_rows(table, os, o)
-
-
-def bwd_kernel(order, table, qs, ks, vs, g, lse, dq, dk, dv, gs, dqs, dks, dvs):
-    sort_rows(order, g, gs)
-    attend_back(qs, ks, vs, gs, lse, dqs, dks, dvs)
-    for a, b in ((dqs, dq), (dks, dk), (dvs, dv)):
-        sort_rows(table, a, b)
-
-
-def attention(order, table, q, k, v):
-    n = q.shape[0]
-    rows = jax.ShapeDtypeStruct((n, 128), BF)
-    return pl.pallas_call(
-        fwd_kernel,
-        out_shape=(rows, jax.ShapeDtypeStruct((2, n), F32), rows, rows, rows),
-        grid_spec=pltpu.PrefetchScalarGridSpec(
-            num_scalar_prefetch=2, grid=(),
-            in_specs=[pl.BlockSpec(memory_space=pltpu.VMEM)] * 3,
-            out_specs=[pl.BlockSpec(memory_space=pltpu.VMEM)] * 5,
-            scratch_shapes=[pltpu.VMEM((n, 128), BF)],
-        ),
-        compiler_params=pltpu.CompilerParams(vmem_limit_bytes=48 << 20),
-        name="attention",
-    )(order, table, q, k, v)
-
-
-def attention_back(order, table, qs, ks, vs, g, lse):
-    n = qs.shape[0]
-    rows = jax.ShapeDtypeStruct((n, 128), F32)
-    return pl.pallas_call(
-        bwd_kernel,
-        out_shape=(rows, rows, rows),
-        grid_spec=pltpu.PrefetchScalarGridSpec(
-            num_scalar_prefetch=2, grid=(),
-            in_specs=[pl.BlockSpec(memory_space=pltpu.VMEM)] * 5,
-            out_specs=[pl.BlockSpec(memory_space=pltpu.VMEM)] * 3,
-            scratch_shapes=[pltpu.VMEM((n, 128), BF)] + [pltpu.VMEM((n, 128), F32)] * 3,
-        ),
-        compiler_params=pltpu.CompilerParams(vmem_limit_bytes=48 << 20),
-        name="attention_back",
-    )(order, table, qs, ks, vs, g, lse)
+    n = (i + 1) * ROWS
+    mine = slice(i * ROWS, n)
+    total = None
+    queries = _heads(qs[mine, :] * BF(0.125))
+    grads = _heads(gs[mine, :])
+    for head in range(2):
+        scores = _scores(ks[:n, :], queries[head], tri)
+        probs = jnp.exp(scores - lse[head : head + 1, mine])
+        gp = _nt(vs[:n, :], grads[head])
+        delta = jnp.sum(probs * gp, 0, keepdims=True)
+        ds = (probs * (gp - delta)).astype(BF)
+        dv[:n, :] += _nn(probs.astype(BF), grads[head])
+        dk[:n, :] += _nn(ds, queries[head])
+        part = _tn(ds, _heads(ks[:n, :])[head])
+        total = part if total is None else total + part
+    dq[mine, :] = total * 0.125
+
+
+def swap_halves(values):
+    lane = lax.broadcasted_iota(jnp.int32, values.shape, 1)
+    return jnp.where(lax.rem(lane, 64) < 32, pltpu.roll(values, 96, 1), pltpu.roll(values, 32, 1))
 
 
 from jax.sharding import PartitionSpec as P
@@ -456,198 +410,435 @@
     return lambda c: src.at[:, pl.ds(pl.multiple_of(c * width, 128), width)]
 
 
-def deal_columns(plan, h, src, out, sems, t0, t1):
+def columns_of(out, width):
+    return lambda c: out.at[:, pl.ds(pl.multiple_of(c * width, 128), width)]
+
+
+def deal_columns(plan, h, src, out, sems, t0, t1, relay_from, lanes=None):
+    lanes = pl.ds(0, out.shape[3]) if lanes is None else lanes
     deal16(
-        plan, h, columns(src, out.shape[3]), lambda c: out.at[c, h.core], lambda c, core: out.at[c, core], sems, t0, t1
-    )
-
-
-def entry_kernel(x, wq, wk, wv, gains, xg, q_out, k_out, v_out, g_out, *refs):
+        plan, h, columns(src, lanes.size), lambda c: out.at[c, h.core, :, lanes], lambda c, core: out.at[c, core, :, lanes],
+        sems, t0, t1, relay_from=relay_from,
+    )
+
+
+def front_kernel(
+    order, table, x, wq, wk, wv, wg, wu, wd, wo, cot, tile, cos, sin,
+    normed, w_out, gains, qs, ks, vs, lse, low, g_out, u_out, d_out, o_out, c_out, *refs
+):
     refs = list(refs)
+    xg, wqkv, tiles, stage, q, k_rows, v, o, o_rows = take(refs, 9)
+    stage_sem, send, recv = take(refs, 3)
+    rows, width = x.shape
     h = Here()
     greet_all(h)
     plan = Plan()
-    for src, out in ((wq, q_out), (wk, k_out), (wv, v_out)):
-        deal_columns(plan, h, src, out, take(refs, 5), 0, 20)
+    for i, src in enumerate((wq, wk, wv)):
+        deal_columns(plan, h, src, wqkv, take(refs, 5), 0, 16, 10, pl.ds(i * 128, 128))
     deal16(
-        plan, h, lambda c: gains, lambda c: g_out.at[c, h.core], lambda c, core: g_out.at[c, core], take(refs, 5), 0, 21
-    )
-    gather16(plan, h, x, xg, take(refs, 13), 0, 14, 20)
+        plan, h, lambda c: tile, lambda c: tiles.at[c, h.core], lambda c, core: tiles.at[c, core], take(refs, 5), 0, 17,
+        relay_from=11,
+    )
+    done = gather16(plan, h, x, xg, take(refs, 13), 0, 14, 20, by_plane=True)
+    for i, (src, out) in enumerate(((wg, g_out), (wu, u_out), (wd, d_out))):
+        deal_columns(plan, h, src, out, take(refs, 5), 20 + i, 190 + i, 170)
+    gather16(plan, h, wo, o_out.at[:, h.core], take(refs, 13), 75, 10, 14)
+    gather16(plan, h, cot, c_out, take(refs, 13), 105, 18, 26)
+    to_sems = take(refs, 5)
+    mine, other = o_out.at[:, h.core], o_out.at[:, 1 - h.core]
+    across = remote(mine, mine, send, recv, fsdp=1 - h.core)
+    plan.at(160, across.start)
+
+    def plane(k):
+        return jnp.bitwise_xor(h.z, k)
+
+    def put_normed(k):
+        at = pl.ds(pl.multiple_of(plane(k) * 4 * rows, 4 * rows), 4 * rows)
+        return pltpu.make_async_copy(stage, normed.at[at], stage_sem)
+
+    def spread_gains():
+        gains[...] = jnp.zeros_like(gains)
+        for c in range(16):
+            both = tiles[c, 0].astype(F32) + tiles[c, 1].astype(F32)
+            gains[:, c * 128 : (c + 1) * 128] = both[0:8]
+
+    def work(k):
+        zz = plane(k)
+        done(zz)
+        if k:
+            put_normed(k - 1).wait()
+        else:
+            spread_gains()
+        for p in range(2):
+            at = pl.ds(pl.multiple_of((zz * 4 + p * 2) * rows, 2 * rows), 2 * rows)
+            blocks = pl.ds(zz * 8 + p * 4, 4)
+            value = xg[pl.ds(zz * 4 + p * 2, 2)].reshape(2 * rows, width).astype(F32)
+            inverse = lax.rsqrt(jnp.mean(value * value, -1, keepdims=True) + EPSILON)
+            value = (value * inverse * gains[0:1, :]).astype(BF)
+            stage[p * 2 * rows : (p + 1) * 2 * rows, :] = value
+            pre = _nn(value, wqkv[...].reshape(width, 384))
+            for i, out in enumerate((q, k_rows)):
+                part = pre[:, i * 128 : (i + 1) * 128]
+                turned = part * cos[at, :] + swap_halves(part) * sin[at, :]
+                out[blocks] = turned.astype(BF).reshape(4, 64, 128)
+            v[blocks] = pre[:, 256:].astype(BF).reshape(4, 64, 128)
+        put_normed(k).start()
+
+    for k in range(4):
+        plan.at((24, 42, 62, 82)[k], functools.partial(work, k))
+
+    def sort():
+        put_normed(3).wait()
+        for a, b in ((q, qs), (k_rows, ks), (v, vs)):
+            sort_rows(order, a, b)
+        w_out[...] = wqkv[...].reshape(width, 384)
+
+    plan.at(83, sort)
+    for i in range(16 * rows // ROWS):
+        plan.at(84 + 1.3 * i, functools.partial(attend_step, i, qs, ks, vs, o.reshape(16 * rows, 128), lse))
+
+    def unsort():
+        for b in range(32):
+            o_rows[b // 2, (b % 2) * 64 : (b % 2 + 1) * 64, :] = o[table[b]]
+
+    plan.at(96, unsort)
+    deal16(plan, h, lambda c: o_rows.at[c], columns_of(low, 128), None, to_sems, 96.1, 200, both=False)
+
+    def end():
+        remote(other, other, send, recv, fsdp=1 - h.core).wait_recv()
+        across.wait_send()
+
+    plan.at(210, end)
     plan.run()
 
 
-def entry(x, wq, wk, wv, gains):
+def front(order, table, x, wq, wk, wv, wg, wu, wd, wo, cot, tile, cos, sin):
     rows, width = x.shape
-    block = (16, 2, wq.shape[0], width // 16)
+    length = 16 * rows
+    block = jax.ShapeDtypeStruct((16, 2, wg.shape[0], wg.shape[1] // 16), BF)
+    heads = jax.ShapeDtypeStruct((length, 128), BF)
     outs = (
-        jax.ShapeDtypeStruct((16, rows, width), BF),
-        *[jax.ShapeDtypeStruct(block, BF)] * 3,
-        jax.ShapeDtypeStruct((16, 2) + gains.shape, BF),
-    )
-    return comm_call(entry_kernel, outs, [ANY] * 5, [ANY] * 5, DEAL_SEMS * 4 + GATHER_SEMS, 0, "entry")(
-        x, wq, wk, wv, gains
-    )
-
-
-def weights_kernel(wg, wu, wd, wo, cot, g_out, u_out, d_out, o_out, c_out, *refs):
+        jax.ShapeDtypeStruct((length, width), BF), jax.ShapeDtypeStruct((width, 384), BF),
+        jax.ShapeDtypeStruct((8, width), F32), heads, heads, heads, jax.ShapeDtypeStruct((2, length), F32),
+        jax.ShapeDtypeStruct((rows, width), BF), block, block, block,
+        jax.ShapeDtypeStruct((16, 2) + wo.shape, BF), jax.ShapeDtypeStruct((16, rows, width), BF),
+    )
+    smem = pl.BlockSpec(memory_space=pltpu.SMEM)
+    scratch = [
+        pltpu.VMEM((16, rows, width), BF), pltpu.VMEM((16, 2, wq.shape[0], 384), BF), pltpu.VMEM((16, 2) + tile.shape, BF),
+        pltpu.VMEM((4 * rows, width), BF), *[pltpu.VMEM((32, 64, 128), BF)] * 4, pltpu.VMEM((16, rows, 128), BF),
+        DMA, DMA, DMA,
+    ]
+    scratch += DEAL_SEMS * 4 + GATHER_SEMS + DEAL_SEMS * 3 + GATHER_SEMS * 2 + DEAL_SEMS
+    return comm_call(
+        front_kernel, outs, [ANY] + [INNER] * 6 + [ANY] * 6, [smem] * 2 + [INNER] + [ANY] * 8 + [INNER] * 3, scratch, 0,
+        "front", 58,
+    )(order, table, x, wq, wk, wv, wg, wu, wd, wo, cot, tile, cos, sin)
+
+
+def mlp_kernel(src, cot, bg, bu, bd, gmi, out_part, own_gu, d_home, *refs):
     refs = list(refs)
+    xm, ct, wg, wu, wd, grads, act, part, stage, cols = take(refs, 10)
+    other_gu, got_gu, own_d, other_d, got_d = take(refs, 5)
+    w_sem, ct_sem, cols_sem, stage_sem, ex_sems = take(refs, 5)
+    rows, width = src.shape
+    hidden = wg.shape[1]
+    block = own_d.shape[1]
+    h = Here()
+    loads = [pltpu.make_async_copy(a, b, w_sem.at[i]) for i, (a, b) in enumerate(((bg, wg), (bu, wu), (bd, wd)))]
+
+    def plane(k):
+        return jnp.bitwise_xor(h.z, k)
+
+    def load_cot(k):
+        return pltpu.make_async_copy(cot.at[pl.ds(plane(k) * 4, 4)], ct.at[k % 2], ct_sem.at[k % 2])
+
+    def put_out(k):
+        return pltpu.make_async_copy(stage, out_part.at[pl.ds(plane(k) * 4, 4)], stage_sem)
+
+    for c in loads + [load_cot(0), load_cot(1)]:
+        c.start()
+    greet_all(h)
+    plan = Plan()
+    done = gather16(plan, h, src, xm, take(refs, 13), 0, 12, 17, by_plane=True)
+
+    def work(k):
+        zz = plane(k)
+        done(zz)
+        if k == 0:
+            for c in loads:
+                c.wait()
+        load_cot(k).wait()
+        if k:
+            put_out(k - 1).wait()
+
+        def pair(p, carry):
+            two = pl.ds(p * 2, 2)
+            at = pl.ds(pl.multiple_of((zz * 4 + p * 2) * rows, 2 * rows), 2 * rows)
+            x = xm[pl.ds(zz * 4 + p * 2, 2)].reshape(2 * rows, width)
+            gate, up = _nn(x, wg[...]), _nn(x, wu[...])
+            sig = jax.nn.sigmoid(gate)
+            silu = gate * sig
+            low = (silu * up).astype(BF)
+            act[at, :] = low
+            stage[two] = _nt(low, wd[...]).astype(BF).reshape(2, rows, width)
+            grad = _nn(ct[k % 2, two].reshape(2 * rows, width), wd[...])
+            grad_gate = (grad * up * sig * (1.0 + gate * (1.0 - sig))).astype(BF)
+            grad_up = (grad * silu).astype(BF)
+            grads[at, pl.ds(0, hidden)] = grad_gate
+            grads[at, pl.ds(hidden, hidden)] = grad_up
+            back = _nt(grad_gate, wg[...]) + _nt(grad_up, wu[...])
+            part[zz, pl.ds(p, 1)] = back.astype(BF).reshape(1, 2, rows, width)
+            return carry
+
+        lax.fori_loop(0, 2, pair, 0)
+        put_out(k).start()
+        if k + 2 < 4:
+            load_cot(k + 2).start()
+
+    for k in range(4):
+        plan.at((22, 38, 55, 72)[k], functools.partial(work, k))
+    plan.at(76, lambda: put_out(3).wait())
+    scatter16(plan, h, part, gmi, take(refs, N_SCATTER), 44, 18)
+
+    def split(c, both, own, other):
+        both = both.astype(BF).reshape(2, block, both.shape[1])
+        own[c] = jnp.where(h.core == 0, both[0], both[1])
+        other[c] = jnp.where(h.core == 0, both[1], both[0])
+
+    def exchange(i, other, got):
+        return remote(other, got, ex_sems.at[i], ex_sems.at[2 + i], fsdp=1 - h.core)
+
+    def load_cols(c):
+        slot = lax.rem(c, 2)
+        at = pl.ds(pl.multiple_of(c * 2 * block, 128), 2 * block)
+        return pltpu.make_async_copy(cot.at[:, :, at], cols.at[slot], cols_sem.at[slot])
+
+    def grads_gu(first):
+        def one(c, carry):
+            at = pl.ds(pl.multiple_of(c * 2 * block, 128), 2 * block)
+            lhs = xm[:, :, at].reshape(16 * rows, 2 * block)
+            split(c, _tn(lhs, grads[...]), own_gu, other_gu)
+            return carry
+
+        lax.fori_loop(first, first + 4, one, 0)
+
+    def grads_d(first):
+        def one(c, carry):
+            pl.when(c < 15)(lambda: load_cols(c + 1).start())
+            load_cols(c).wait()
+            lhs = cols[lax.rem(c, 2)].reshape(16 * rows, 2 * block)
+            split(c, _tn(lhs, act[...]), own_d, other_d)
+            return carry
+
+        lax.fori_loop(first, first + 4, one, 0)
+
+    def join(i, own, other, got):
+        exchange(i, other, got).wait_recv()
+        for c in range(16):
+            own[c] = (own[c].astype(F32) + got[c].astype(F32)).astype(BF)
+        exchange(i, other, got).wait_send()
+
+    plan.at(74, lambda: load_cols(0).start())
+    for i in range(4):
+        plan.at(76.5 + 2 * i, functools.partial(grads_d, 4 * i))
+        plan.at(88 + 3 * i, functools.partial(grads_gu, 4 * i))
+    plan.at(85, lambda: exchange(1, other_d, got_d).start())
+    plan.at(89, lambda: join(1, own_d, other_d, got_d))
+    plan.at(100, lambda: exchange(0, other_gu, got_gu).start())
+    plan.at(110, lambda: join(0, own_gu, other_gu, got_gu))
+    deal16(plan, h, lambda c: own_d.at[c], columns_of(d_home, hidden), None, take(refs, 5), 89.1, 182, both=False)
+    plan.run()
+
+
+def mlp(src, cot, bg, bu, bd):
+    rows, width = src.shape
+    block, hidden = bg.shape[2:]
+    full = pltpu.VMEM((width, hidden), BF)
+    gu, d = pltpu.VMEM((16, block, 2 * hidden), BF), pltpu.VMEM((16, block, hidden), BF)
+    scratch = [
+        pltpu.VMEM((16, rows, width), BF), pltpu.VMEM((2, 4, rows, width), BF), full, full, full,
+        pltpu.VMEM((16 * rows, 2 * hidden), BF), pltpu.VMEM((16 * rows, hidden), BF),
+        pltpu.VMEM((4, 2, 2, rows, width), BF), pltpu.VMEM((4, rows, width), BF),
+        pltpu.VMEM((2, 16, rows, 2 * block), BF), gu, gu, d, d, d,
+        DMA((3,)), DMA((2,)), DMA((2,)), DMA, DMA((4,)),
+    ]
+    scratch += GATHER_SEMS + scatter_scratch(rows, width) + DEAL_SEMS
+    home = jax.ShapeDtypeStruct((block, 16 * hidden), BF)
+    outs = (jax.ShapeDtypeStruct((rows, width), F32), jax.ShapeDtypeStruct((16, rows, width), BF), jax.ShapeDtypeStruct((16, block, 2 * hidden), BF), home)
+    return comm_call(mlp_kernel, outs, [INNER, ANY, INNER, ANY], [ANY] * 5, scratch, 5, "mlp", 61)(
+        src, cot, *(b.reshape(width, hidden) for b in (bg, bu, bd))
+    )
+
+
+def outer_home(plan, h, left, right, own, other, got, send, recv, t0, t1):
+    rows = own.shape[1]
+    over = remote(other, got, send, recv, fsdp=1 - h.core)
+
+    def compute():
+        mine, theirs = pl.multiple_of(h.core * rows, rows), pl.multiple_of((1 - h.core) * rows, rows)
+        for c in range(16):
+            lhs = left[:, c * 2 * rows : (c + 1) * 2 * rows]
+            both = _tn(lhs, right[...]).astype(BF).reshape(2, rows, right.shape[1])
+            own[c] = jnp.where(h.core == 0, both[0], both[1])
+            other[c] = jnp.where(h.core == 0, both[1], both[0])
+        over.start()
+
+    def add():
+        over.wait_recv()
+        for c in range(16):
+            own[c] = (own[c].astype(F32) + got[c].astype(F32)).astype(BF)
+        over.wait_send()
+
+    plan.at(t0, compute)
+    plan.at(t1, add)
+
+
+def back_kernel(order, table, ga, qs, ks, vs, lse, cos, sin, out_part, low, branch, gu, dqkv, out_sum, wo_sum, g_home, *refs):
+    refs = list(refs)
+    gh, gs, dq, dk, dv, own, other, got = take(refs, 8)
+    send, recv = take(refs, 2)
+    gh_rows = gh.reshape(16, ga.shape[0], 128)
+    flat = [g.reshape(qs.shape) for g in (dq, dk, dv)]
     h = Here()
     greet_all(h)
     plan = Plan()
-    for src, out in ((wg, g_out), (wu, u_out), (wd, d_out)):
-        deal_columns(plan, h, src, out, take(refs, 5), 0, 100)
-    gather16(plan, h, wo, o_out.at[:, h.core], take(refs, 13), 0, 14, 18)
-    gather16(plan, h, cot, c_out, take(refs, 13), 10, 20, 28)
-    send, recv = take(refs, 2)
-    mine, other = o_out.at[:, h.core], o_out.at[:, 1 - h.core]
-    across = remote(mine, mine, send, recv, fsdp=1 - h.core)
-    plan.at(105, across.start)
+    deal16(plan, h, columns(ga, 128), lambda c: gh_rows.at[c], None, take(refs, 5), 0, 14, both=False)
+    gu_sems = take(refs, 5)
+    scatter16(plan, h, out_part, out_sum, take(refs, N_SCATTER), 1, 20)
+    outer_home(plan, h, low, branch, own, other, got, send, recv, 2, 8)
+    first = pl.ds(0, gu.shape[2] // 2)
+    deal16(
+        plan, h, lambda c: gu.at[c, :, first], columns_of(g_home, gu.shape[2] // 2), None, gu_sems, 3, 198, both=False
+    )
+    scatter16(plan, h, own.reshape(4, 2, 2, *own.shape[1:]), wo_sum, take(refs, N_SCATTER), 8.1, 18)
+
+    def begin():
+        sort_rows(order, gh, gs)
+        dk[...] = jnp.zeros_like(dk)
+        dv[...] = jnp.zeros_like(dv)
+
+    plan.at(15, begin)
+    for i in range(qs.shape[0] // ROWS):
+        plan.at(16 + 2.2 * i, functools.partial(back_step, i, qs, ks, vs, gs, lse, *flat))
 
     def end():
-        remote(other, other, send, recv, fsdp=1 - h.core).wait_recv()
+        for b in range(32):
+            rows = slice(b * 64, (b + 1) * 64)
+            for i, grad in enumerate((dq, dk)):
+                value = grad[table[b]]
+                turned = swap_halves(value)
+                dqkv[rows, i * 128 : (i + 1) * 128] = (value * cos[rows, :] - turned * sin[rows, :]).astype(BF)
+            dqkv[rows, 256:] = dv[table[b]].astype(BF)
+
+    plan.at(34.5, end)
+    plan.run()
+
+
+def back(order, table, ga, qs, ks, vs, lse, cos, sin, out_part, low, branch, gu):
+    rows, width = ga.shape
+    length = qs.shape[0]
+    smem = pl.BlockSpec(memory_space=pltpu.SMEM)
+    half = pltpu.VMEM((16, width // 32, width), BF)
+    outs = (
+        jax.ShapeDtypeStruct((length, 384), BF),
+        jax.ShapeDtypeStruct((rows, width), F32),
+        jax.ShapeDtypeStruct((width // 32, width), F32),
+        jax.ShapeDtypeStruct((gu.shape[1], 8 * gu.shape[2]), BF),
+    )
+    scratch = [pltpu.VMEM((32, 64, 128), BF), pltpu.VMEM((length, 128), BF)]
+    scratch += [pltpu.VMEM((32, 64, 128), F32)] * 3 + [half] * 3 + [DMA] * 2 + DEAL_SEMS * 2
+    scratch += scatter_scratch(rows, width) + scatter_scratch(width // 32, width)
+    return comm_call(back_kernel, outs, [INNER] * 3 + [ANY], [smem] * 2 + [INNER] * 10 + [ANY], scratch, 6, "back", 60)(
+        order, table, ga, qs, ks, vs, lse, cos, sin, out_part.reshape(4, 2, 2, rows, width), low, branch, gu
+    )
+
+
+def core_sum(plan, h, part, got, total, sems, t0, t1):
+    send, recv, mine = sems
+    across = remote(part.at[:, 1 - h.core], got, send, recv, fsdp=1 - h.core)
+    local = pltpu.make_async_copy(part.at[:, h.core], total, mine)
+
+    def start():
+        across.start()
+        local.start()
+
+    def add():
+        across.wait_recv()
+        local.wait()
+        for c in range(16):
+            total[c] = (total[c].astype(F32) + got[c].astype(F32)).astype(BF)
         across.wait_send()
 
-    plan.at(200, end)
-    plan.run()
-
-
-def weights(wg, wu, wd, wo, cot):
-    rows, width = cot.shape
-    block = (16, 2, wg.shape[0], wg.shape[1] // 16)
-    outs = (
-        *[jax.ShapeDtypeStruct(block, BF)] * 3,
-        jax.ShapeDtypeStruct((16, 2) + wo.shape, BF),
-        jax.ShapeDtypeStruct((16, rows, width), BF),
-    )
-    return comm_call(
-        weights_kernel, outs, [ANY] * 5, [ANY] * 5, DEAL_SEMS * 3 + GATHER_SEMS * 2 + [DMA, DMA], 1, "weights"
-    )(wg, wu, wd, wo, cot)
-
-
-def to_tokens_kernel(src, out, *sems):
-    h = Here()
-    greet_all(h)
-    plan = Plan()
-    deal16(plan, h, lambda c: src.at[c], columns_of(out, 128), None, sems, 0, 8, both=False)
-    plan.run()
-
-
-def columns_of(out, width):
-    return lambda c: out.at[:, pl.ds(pl.multiple_of(c * width, 128), width)]
-
-
-def to_tokens(src):
-    ctx, rows, width = src.shape
-    outs = jax.ShapeDtypeStruct((rows, ctx * width), BF)
-    return comm_call(to_tokens_kernel, outs, ANY, [ANY], DEAL_SEMS, 2, "to_tokens")(src)
-
-
-def to_heads_kernel(src, out, *sems):
-    h = Here()
-    greet_all(h)
-    plan = Plan()
-    deal16(plan, h, columns(src, out.shape[2]), lambda c: out.at[c], None, sems, 0, 8, both=False)
-    plan.run()
-
-
-def to_heads(src):
-    rows, width = src.shape
-    outs = jax.ShapeDtypeStruct((16, rows, width // 16), BF)
-    return comm_call(to_heads_kernel, outs, ANY, [ANY], DEAL_SEMS, 3, "to_heads")(src)
-
-
-def gather_kernel(src, out, *sems):
-    h = Here()
-    greet_all(h)
-    plan = Plan()
-    gather16(plan, h, src, out, sems, 0, 12, 17)
-    plan.run()
-
-
-def gather(src):
-    outs = jax.ShapeDtypeStruct((16,) + src.shape, BF)
-    return comm_call(gather_kernel, outs, ANY, [ANY], GATHER_SEMS, 4, "gather")(src)
-
-
-def scatter_kernel(part, out, *scratch):
-    h = Here()
-    greet_all(h)
-    plan = Plan()
-    scatter16(plan, h, part, out, scratch, 0, 17)
-    plan.run()
-
-
-def scatter(part, cid):
-    rows, width = part.shape[0] // 16, part.shape[1]
-    outs = jax.ShapeDtypeStruct((rows, width), F32)
-    return comm_call(
-        scatter_kernel, outs, INNER, [INNER], scatter_scratch(rows, width), cid, f"scatter{cid}", 48
-    )(part.reshape(4, 2, 2, rows, width))
-
-
-def core_sum(plan, h, part, got, total, sems, t0, t1):
-    send, recv = sems
-    across = remote(part.at[:, 1 - h.core], got, send, recv, fsdp=1 - h.core)
-    plan.at(t0, across.start)
-
-    def add():
-        remote(part.at[:, h.core], got, send, recv, fsdp=1 - h.core).wait_recv()
-        for c in range(16):
-            total[c] = (part[c, h.core].astype(F32) + got[c].astype(F32)).astype(BF)
-        across.wait_send()
-
+    plan.at(t0, start)
     plan.at(t1, add)
 
 
-def home_kernel(*refs):
+def home_kernel(n, *refs):
     refs = list(refs)
-    parts, gains = take(refs, 6), take(refs, 1)[0]
-    outs, gains_out = take(refs, 6), take(refs, 1)[0]
+    gn, parts, (scaled, other_gain, gu) = take(refs, 1)[0], take(refs, n), take(refs, 3)
+    gn_out, outs, gains_out, u_home = take(refs, 1)[0], take(refs, n), *take(refs, 2)
     h = Here()
     greet_all(h)
     plan = Plan()
     for i, (part, out) in enumerate(zip(parts, outs)):
         got, total = take(refs, 2)
-        core_sum(plan, h, part, got, total, take(refs, 2), 0.1 * i, 2 * i + 1)
+        core_sum(plan, h, part, got, total, take(refs, 3), 0.1 * i, 2 * i + 1)
         deal16(
-            plan, h, lambda c, t=total: t.at[c], columns_of(out, part.shape[3]), None, take(refs, 5), 2 * i + 1.5, 90 + i,
+            plan, h, lambda c, t=total: t.at[c], columns_of(out, part.shape[3]), None, take(refs, 5), 2 * i + 1.5, 198 + i,
             both=False,
         )
-    deal16(plan, h, lambda c: gains.at[c], lambda c: gains_out.at[c], None, take(refs, 5), 0, 20, both=False)
+    last = pl.ds(gu.shape[2] // 2, gu.shape[2] // 2)
+    deal16(
+        plan, h, lambda c: gu.at[c, :, last], columns_of(u_home, gu.shape[2] // 2), None, take(refs, 5), 0.5, 197, both=False
+    )
+    gains, got, landed, send, recv = take(refs, 5)
+    gain_sems = take(refs, 5)
+    scatter16(plan, h, gn, gn_out, refs, 0.5, 20)
+    over = remote(gains, got, send, recv, fsdp=1 - h.core)
+
+    def sums():
+        gains[...] = jnp.zeros_like(gains)
+        total = jnp.sum(gn_out[...] * scaled[...], 0, keepdims=True)
+        for c in range(16):
+            at = slice(c * 128, (c + 1) * 128)
+            gains[c, 0:1] = total[:, at]
+            gains[c, 1:2] = other_gain[:, at]
+        over.start()
+        over.wait_recv()
+        over.wait_send()
+        gains[...] += got[...]
+
+    plan.at(200, sums)
+    deal16(plan, h, lambda c: gains.at[c], lambda c: landed.at[c], None, gain_sems, 201, 204, both=False)
+
+    def add():
+        total = landed[0]
+        for c in range(1, 16):
+            total = total + landed[c]
+        gains_out[...] = total
+
+    plan.at(300, add)
     plan.run()
 
 
-def home(parts, gains):
+def home(gn, parts, scaled, other_gain, gu):
     scratch = []
+    rows, width = gn.shape[0] // 16, gn.shape[1]
     for p in parts:
         buffer = pltpu.VMEM((p.shape[0],) + p.shape[2:], BF)
-        scratch += [buffer, buffer, DMA, DMA] + DEAL_SEMS
-    outs = [jax.ShapeDtypeStruct((p.shape[2], 16 * p.shape[3]), BF) for p in parts]
-    outs.append(jax.ShapeDtypeStruct(gains.shape, F32))
+        scratch += [buffer, buffer, DMA, DMA, DMA] + DEAL_SEMS
+    outs = [jax.ShapeDtypeStruct((rows, width), F32)]
+    outs += [jax.ShapeDtypeStruct((p.shape[2], 16 * p.shape[3]), BF) for p in parts]
+    outs.append(jax.ShapeDtypeStruct((8, 128), F32))
+    outs.append(jax.ShapeDtypeStruct((gu.shape[1], 8 * gu.shape[2]), BF))
+    n = len(parts)
+    tile = pltpu.VMEM((16, 8, 128), F32)
+    scratch += DEAL_SEMS + [tile, tile, tile, DMA, DMA] + DEAL_SEMS + scatter_scratch(rows, width)
     return comm_call(
-        home_kernel, tuple(outs), [ANY] * 7, [INNER] * 7, scratch + DEAL_SEMS, 6, "home", 52
-    )(*parts, gains)
-
-
-def out_home_kernel(part, out, got, total, s, r, *scratch):
-    h = Here()
-    greet_all(h)
-    plan = Plan()
-    core_sum(plan, h, part, got, total, (s, r), 0, 1)
-    plan.run()
-    plan = Plan()
-    view = total.reshape(4, 2, 2, *total.shape[1:])
-    scatter16(plan, h, view, out, scratch, 2, 9)
-    plan.run()
-
-
-def out_home(part):
-    ctx, _, rows, width = part.shape
-    buffer = pltpu.VMEM((ctx, rows, width), BF)
-    outs = jax.ShapeDtypeStruct((rows, width), F32)
-    return comm_call(
-        out_home_kernel, outs, INNER, [INNER], [buffer, buffer, DMA, DMA] + scatter_scratch(rows, width), 7, "out_home", 48
-    )(part)
+        functools.partial(home_kernel, n), tuple(outs), [INNER] + [ANY] * n + [INNER, ANY], [INNER] + [ANY] * n + [INNER] * 2 + [ANY],
+        scratch, 7, "home", 58,
+    )(gn.reshape(4, 2, 2, rows, width), *parts, scaled, other_gain, gu)
 
 
 def rope_tables(positions):
@@ -666,10 +857,6 @@
     rows, width = x.shape
     length = rows * 16
     core = lax.axis_index("fsdp")
-    gains = jnp.pad(jnp.concatenate([attn_gain, mlp_gain])[None], ((0, 15), (0, 0)))
-    xg, bq, bk, bv, gains = entry(x, wq, wk, wv, gains)
-    gains = gains[:, :, 0].reshape(32, 2, 64).astype(F32)
-    again, mgain = gains[:, 0].reshape(width), gains[:, 1].reshape(width)
     slots = jnp.arange(32, dtype=jnp.int32)
     order = jnp.sum(jnp.where(table[None, :] == slots[:, None], slots[None, :], 0), 1)
     positions = (table[:, None] * 64 + jnp.arange(64, dtype=jnp.int32)[None]).reshape(length)
@@ -677,11 +864,6 @@
     turn = jnp.where(jnp.arange(128) % 64 < 32, -1.0, 1.0).astype(F32)
     sin = sin * turn
 
-    source = xg.reshape(length, width).astype(F32)
-    inv_all = lax.rsqrt(jnp.mean(source * source, -1, keepdims=True) + EPSILON)
-    normed = (source * inv_all * again).astype(BF)
-    bq, bk, bv = (b.reshape(width, 128) for b in (bq, bk, bv))
-
     def dot(a, b):
         return jnp.dot(a, b, preferred_element_type=F32)
 
@@ -691,31 +873,19 @@
     def dot_tn(a, b):
         return lax.dot_general(a, b, (((0,), (0,)), ((), ())), preferred_element_type=F32)
 
-    qkv = dot(normed, jnp.concatenate([bq, bk, bv], 1))
-    q, k, v = qkv[:, :128], qkv[:, 128:256], qkv[:, 256:].astype(BF)
-    q = (q * cos + swap(q) * sin).astype(BF)
-    k = (k * cos + swap(k) * sin).astype(BF)
-    o, lse, qs, ks, vs = attention(order, table, q, k, v)
-    bg, bu, bd, full_out, cot_all = weights(wg, wu, wd, wo, cot)
+    lane = jnp.arange(128) // 64
+    tile = jnp.where(lane[None] == core, jnp.tile(jnp.stack([attn_gain, mlp_gain]), (1, 2)), 0)
+    tile = jnp.pad(tile, ((0, 14), (0, 0)))
+    normed, wqkv, gains, qs, ks, vs, lse, attn_low, bg, bu, bd, full_out, cot_all = front(
+        order, table, x, wq, wk, wv, wg, wu, wd, wo, cot, tile, cos, sin
+    )
+    again, mgain = gains[0], gains[1]
     full_out = full_out.reshape(width, width)
-    bg, bu, bd = (b.reshape(width, b.shape[3]) for b in (bg, bu, bd))
-    cot_all = cot_all.reshape(length, width)
-    attn_low = to_tokens(o.reshape(16, rows, 128))
     own = x.astype(F32)
     inv_in = lax.rsqrt(jnp.mean(own * own, -1, keepdims=True) + EPSILON)
     hidden = own + dot(attn_low, full_out)
     inv_mid = lax.rsqrt(jnp.mean(hidden * hidden, -1, keepdims=True) + EPSILON)
-    mlp_in = gather((hidden * inv_mid * mgain).astype(BF)).reshape(length, width)
-    gate, up = dot(mlp_in, bg), dot(mlp_in, bu)
-    sig = jax.nn.sigmoid(gate)
-    act = (gate * sig * up).astype(BF)
-    out_part = dot_nt(act, bd).astype(BF)
-    grad_act = dot(cot_all, bd)
-    grad_gate = (grad_act * up * sig * (1.0 + gate * (1.0 - sig))).astype(BF)
-    grad_up = (grad_act * gate * sig).astype(BF)
-    gmi_part = (dot_nt(grad_gate, bg) + dot_nt(grad_up, bu)).astype(BF)
-    gmi = scatter(gmi_part, 5)
-    layer_output = (hidden + scatter(out_part, 8)).astype(BF)
+    gmi, out_part, part_gu, gd = mlp((hidden * inv_mid * mgain).astype(BF), cot_all, bg, bu, bd)
 
     def norm_back(grad, source, inv, gain):
         scaled = grad * gain
@@ -725,33 +895,21 @@
     mgain_part = jnp.sum(gmi * hidden * inv_mid, 0)
     grad_hidden = cot.astype(F32) + norm_back(gmi, hidden, inv_mid, mgain)
     grad_branch = grad_hidden.astype(BF)
-    grad_att = to_heads(dot_nt(grad_branch, full_out).astype(BF)).reshape(length, 128)
-    dq, dk, dv = attention_back(order, table, qs, ks, vs, grad_att, lse)
-    dq = (dq * cos - swap(dq) * sin).astype(BF)
-    dk = (dk * cos - swap(dk) * sin).astype(BF)
-    grad_qkv = jnp.concatenate([dq, dk, dv.astype(BF)], 1)
-    gn_part = dot_nt(grad_qkv, jnp.concatenate([bq, bk, bv], 1)).astype(BF)
-    gn = scatter(gn_part, 9)
-    input_grad = grad_hidden + norm_back(gn, own, inv_in, again)
-    again_part = jnp.sum(gn * own * inv_in, 0)
-    gains = jnp.stack([again_part, mgain_part]).reshape(2, 16, 128).transpose(1, 0, 2)
-    gains = jnp.pad(gains, ((0, 0), (0, 6), (0, 0)))
+    grad_att = dot_nt(grad_branch, full_out).astype(BF)
+    grad_qkv, out_sum, wo_grad, gg = back(
+        order, table, grad_att, qs, ks, vs, lse, cos, sin, out_part, attn_low, grad_branch, part_gu
+    )
+    layer_output = (hidden + out_sum).astype(BF)
+    gn_part = dot_nt(grad_qkv, wqkv).astype(BF)
 
     def pieces(grad):
         return grad.astype(BF).reshape(16, 2, 64, grad.shape[1])
 
-    wo_grad = out_home(pieces(dot_tn(attn_low, grad_branch)))
-    parts = [
-        pieces(dot_tn(normed, dq)),
-        pieces(dot_tn(normed, dk)),
-        pieces(dot_tn(normed, dv.astype(BF))),
-        pieces(dot_tn(mlp_in, grad_gate)),
-        pieces(dot_tn(mlp_in, grad_up)),
-        pieces(dot_tn(cot_all, act)),
-    ]
-    *grads, gains = home(parts, gains)
-    gq, gk, gv, gg, gu, gd = (g.astype(F32) for g in grads)
-    gains = lax.psum(jnp.sum(gains, 0), "fsdp")
+    parts = [pieces(dot_tn(normed, grad_qkv))]
+    gn, gqkv, gains, gu = home(gn_part, parts, own * inv_in, mgain_part[None], part_gu)
+    input_grad = grad_hidden + norm_back(gn, own, inv_in, again)
+    gg, gu, gd, gqkv = (g.astype(F32) for g in (gg, gu, gd, gqkv))
+    gq, gk, gv = (gqkv.reshape(64, 16, 3, 128)[:, :, i].reshape(64, width) for i in range(3))
     gains = lax.dynamic_slice_in_dim(gains, core * 64, 64, 1)
     return (layer_output[None], input_grad[None], gains[0], gq, gk, gv, wo_grad, gains[1], gg, gu, gd)
 

time: 968 us -> 799 us (0.83)
  matrix products: 125 us -> 29 us
  Pallas kernels: 787 us -> 721 us
  other arithmetic: 31.1 us -> 15.3 us
    pallas_call x12 -> x4, Pallas kernels: 787 us -> 721 us  [the longest x1 248 us: front(): comm_call(front_kernel, outs, [ANY] + [INNER] * 6 + [ANY] * 6, [smem] * 2...]
    dot_general x7 -> x1, matrix products: 43 us -> 9.65 us  [dot_tn(): lax.dot_general(a, b, (((0,), (0,)), ((), ())), preferred_element_type=F32)]
    dot_general x5 -> x1, matrix products: 37.2 us -> 4.96 us  [dot(): return jnp.dot(a, b, preferred_element_type=F32)]
    dot_general x5 -> x2, matrix products: 44.9 us -> 14.4 us  [dot_nt(): lax.dot_general(a, b, (((1,), (1,)), ((), ())), preferred_element_type=F32)]
    convert_element_type x11 -> x4, other arithmetic: 22.1 us -> 5.98 us  [the longest x3 5.6 us: fast_body(): gg, gu, gd, gqkv = (g.astype(F32) for g in (gg, gu, gd, gqkv))]
where the time goes in v2:
time: 799 us; the launch traced here: 786 us
  Pallas kernels  721 us (90%)
  matrix products  29 us (4%)
  local copies, waits for them, and re-layouts  19.5 us (2%)
  other arithmetic  15.3 us (2%)
    pallas_call x1, Pallas kernels, front(): comm_call(front_kernel, outs, [ANY] + [INNER] * 6 + [ANY] * 6, [smem] * 2...  248 us
    pallas_call x1, Pallas kernels, mlp(): comm_call(mlp_kernel, outs, [INNER, ANY, INNER, ANY], [ANY] * 5, scratch,...  215 us
    pallas_call x1, Pallas kernels, back(): comm_call(back_kernel, outs, [INNER] * 3 + [ANY], [smem] * 2 + [INNER] *...  143 us
    pallas_call x1, Pallas kernels, home(): comm_call(functools.partial(home_kernel, n), tuple(outs), [INNER] + [ANY]...  114 us

profile of v2, /device:TPU:9, one launch (start us, length us, event | category | flops | bytes accessed | tf_op | source)
XLA Modules:
  0.0 786.0 jit_solution(15407541028804629160)
XLA Ops:
  0.6 0.8 copy.28
  1.7 1.0 multiply_sine_fusion
  2.8 0.3 copy.29
  3.1 1.0 broadcast_multiply_fusion.sin
  4.3 1.3 copy.30.cos
  5.6 0.6 select_reduce_fusion.order
  6.3 0.6 pad.4.tile
  6.9 248.2 %front.1 = (bf16[2048,2048]{1,0:T(8,128)(2,1)}, bf16[2048,384]{1,0:T(8,128)(2,1)}, f32[8,2048]{1,0:T(8,128)}, bf16[2048,128]{1,0:T(8,128)(2,1)}, bf16[2048,128]{...) custom-call(s32[32]{0:T(128)} %select_reduce_fusion.order, ...), custom_call_target="tpu_custom_call" | custom-call | tf_op jit(solution)/shard_map/front/pallas_call | solution.py:533
  255.1 5.0 multiply_reduce_fusion.2
  260.1 0.9 fusion.11
  261.0 0.9 multiply_convert_fusion.src
  262.0 215.4 %mlp.1 = (f32[128,2048]{1,0:T(8,128)}, bf16[16,128,2048]{2,1,0:T(8,128)(2,1)}, bf16[16,64,1024]{2,1,0:T(8,128)(2,1)}, bf16[64,8192]{1,0:T(8,128)(2,1)}) custom-call(bf16[128,2048]{1,0:T(8,128)(2,1)} %multiply_convert_fusion.src, bf16[16,128,2048]{2,1,0:T(8,128)(2,1)} %get-tuple-element.39.cot, bf16[2048,512]{1,0:T(8,128)(2,1)} %bitcast.60, ...), custom_call_target="tpu_custom_call" | custom-call | tf_op jit(solution)/shard_map/mlp/pallas_call | solution.py:669
  477.5 2.2 multiply_reduce_fusion
  479.7 0.4 fusion.10
  480.1 7.3 convolution_convert_fusion.2.ga
  487.4 143.0 %back.1 = (bf16[2048,384]{1,0:T(8,128)(2,1)}, f32[128,2048]{1,0:T(8,128)}, f32[64,2048]{1,0:T(8,128)}, bf16[64,8192]{1,0:T(8,128)(2,1)}) custom-call(s32[32]{0:T(128)} %select_reduce_fusion.order, s32[32]{0:T(128)} %copy-done.9, bf16[128,2048]{1,0:T(8,128)(2,1)} %convolution_convert_fusion.2.ga, bf16[2048,128]{1,0:T(8,128)(2,1)} %get-tuple-element.44.qs, ...), custom_call_target="tpu_custom_call" | custom-call | tf_op jit(solution)/shard_map/back/pallas_call | solution.py:752
  630.4 9.7 %convolution_convert_fusion.1 = bf16[2048,384]{1,0:T(8,128)(2,1)} fusion(bf16[2048,2048]{1,0:T(8,128)(2,1)} %get-tuple-element.53, bf16[2048,384]{1,0:T(8,128)(2,1)} %get-tuple-element.51), kind=kOutput, calls=%fused_computation.1 | convolution fusion | flops 3222011904 | bytes 11534336 | tf_op jit(solution)/shard_map/dot_general | solution.py:874
  640.1 7.1 convolution_convert_fusion
  647.2 0.2 fusion
  647.4 1.1 convert_multiply_fusion.2.refs_2_
  648.5 114.4 %home.1 = (f32[128,2048]{1,0:T(8,128)}, bf16[64,6144]{1,0:T(8,128)(2,1)}, f32[8,128]{1,0:T(8,128)}, bf16[64,8192]{1,0:T(8,128)(2,1)}) custom-call(bf16[4,2,2,128,2048]{4,3,2,1,0:T(8,128)(2,1)} %bitcast.53, bf16[16,2,64,384]{3,2,1,0:T(8,128)(2,1)} %bitcast.63, f32[128,2048]{1,0:T(8,128)} %convert_multiply_fusion.2.refs_2_, f32[1,2048]{1,0:T(1,128)} %bitcast.70, ...), custom_call_target="tpu_custom_call" | custom-call | tf_op jit(solution)/shard_map/home/pallas_call | solution.py:838
  762.9 3.8 reshape.213
  766.7 7.6 slice_reduce_fusion
  774.3 1.3 copy_bitcast_fusion
  775.6 1.0 copy.38
  776.6 1.5 convert_element_type.59
  778.0 0.2 fusion.5
  778.3 1.8 fusion.4
  780.1 0.5 slice_bitcast_fusion
  780.7 2.7 convert_element_type.58
  783.4 1.5 convert_element_type.60
  784.8 0.8 copy.40
  (46 shorter events, 0.7 us)
Async XLA Ops:
  1.5 4.1 copy-start.9
  4.2 2.1 copy-start.13
  4.2 2.1 copy-start.14
  6.9 248.2 %copy-start = (bf16[1,128,2048]{2,1,0:T(8,128)(2,1)S(1)}, bf16[1,128,2048]{2,1,0:T(8,128)(2,1)}, u32[]{:S(2)}) copy-start(bf16[1,128,2048]{2,1,0:T(8,128)(2,1)} %param.12) | copy-start | bytes 1572868
  477.4 2.2 copy-start.2
  477.5 2.2 copy-start.4
  480.1 7.3 copy-start.1
  630.4 9.7 %copy-start.11 = (bf16[2048,384]{1,0:T(8,128)(2,1)S(1)}, bf16[2048,384]{1,0:T(8,128)(2,1)}, u32[]{:S(2)}) copy-start(bf16[2048,384]{1,0:T(8,128)(2,1)} %get-tuple-element.52) | copy-start | bytes 4718596
  630.4 9.7 %copy-start.12 = (bf16[2048,384]{1,0:T(8,128)(2,1)S(1)}, bf16[2048,384]{1,0:T(8,128)(2,1)}, u32[]{:S(2)}) copy-start(bf16[2048,384]{1,0:T(8,128)(2,1)} %get-tuple-element.51) | copy-start | bytes 4718596
  774.3 2.3 copy-start.6
  775.6 2.4 copy-start.3
  776.6 1.7 copy-start.7
  778.3 1.8 copy-start.10
  780.1 3.3 copy-start.5
  783.3 1.5 copy-start.8

commit v3 on v2

--- a/solution.py
+++ b/solution.py
@@ -295,6 +295,149 @@
 
 
 ORDER = (12, 8, 13, 9, 14, 10, 15, 11, 4, 5, 6, 7, 3, 1, 2)
+
+
+GATHER8_SEMS = [DMA((4,))] * 6 + [DMA]
+
+
+def gather8(plan, h, src, out, sems, t0, tz, tx):
+    us, ur, ds, dr, xs, xr, own = sems
+
+    def level(zz, source=None):
+        s = zz * 2 + h.x
+        return remote(out.at[s] if source is None else source, out.at[s], xs.at[zz], xr.at[zz], ctx=h.xn)
+
+    def hop(k, up, source=None):
+        it = (h.z - k if up else h.z + k) * 2 + h.x
+        send, recv = (us, ur) if up else (ds, dr)
+        to = h.me + 4 if up else h.me - 4
+        return remote(out.at[it] if source is None else source, out.at[it], send.at[k], recv.at[k + 1], ctx=to)
+
+    def landed(k, up):
+        it = (h.z - k if up else h.z + k) * 2 + h.x
+        send, recv = (us, ur) if up else (ds, dr)
+        return remote(out.at[it], out.at[it], send.at[k - 1], recv.at[k], ctx=h.me)
+
+    local = pltpu.make_async_copy(src, out.at[h.z * 2 + h.x], own)
+
+    def first():
+        pl.when(h.z < 3)(lambda: hop(0, True, src).start())
+        pl.when(h.z > 0)(lambda: hop(0, False, src).start())
+        level(h.z, src).start()
+        local.start()
+
+    plan.at(t0, first)
+
+    def step(k, up):
+        def go():
+            landed(k, up).wait_recv()
+            if k < 3:
+                pl.when((h.z < 3) if up else (h.z > 0))(lambda: hop(k, up).start())
+            level(h.z - k if up else h.z + k).start()
+
+        pl.when((h.z >= k) if up else (h.z + k <= 3))(go)
+
+    for k in (1, 2, 3):
+        for up in (True, False):
+            plan.at(t0 + k * tz, functools.partial(step, k, up))
+
+    def finish(zz):
+        s = zz * 2 + 1 - h.x
+        remote(out.at[s], out.at[s], xs.at[zz], xr.at[zz], ctx=h.xn).wait_recv()
+
+    def drain():
+        for k in range(3):
+            pl.when((h.z >= k) & (h.z < 3))(lambda: hop(k, True).wait_send())
+            pl.when((h.z + k <= 3) & (h.z > 0))(lambda: hop(k, False).wait_send())
+        for zz in range(4):
+            level(zz).wait_send()
+
+    plan.at(t0 + 0.85 * tx, local.wait)
+    plan.at(t0 + 4.5 * tx, drain)
+    return finish
+
+
+def scatter8_scratch(rows, width):
+    few = pltpu.VMEM((3, rows, width), BF)
+    return [pltpu.VMEM((4, rows, width), BF), few, few] + [DMA((4,))] * 4
+
+
+N_SCATTER8 = 7
+
+
+def scatter8(plan, h, part, out, scratch, starts, totals, end):
+    ra, sz, rz, as_, ar, zs, zr = scratch
+
+    def place(k):
+        return jnp.bitwise_xor(h.z, k)
+
+    def first(i, k):
+        return remote(part.at[place(k), 1 - h.x], ra.at[i], as_.at[i], ar.at[i], ctx=h.xn)
+
+    def second(k):
+        return remote(sz.at[k - 1], rz.at[k - 1], zs.at[k], zr.at[k], ctx=place(k) * 4 + h.xy)
+
+    def total(i, k):
+        first(i, k).wait_recv()
+        value = part[place(k), h.x].astype(F32) + ra[i].astype(F32)
+        if k:
+            sz[k - 1] = value.astype(BF)
+            second(k).start()
+        else:
+            out[...] = value
+
+    def last():
+        for k in (1, 2, 3):
+            second(k).wait_recv()
+        out[...] += rz[0].astype(F32) + rz[1].astype(F32) + rz[2].astype(F32)
+        for k in (1, 2, 3):
+            second(k).wait_send()
+        for i, k in enumerate((1, 2, 3, 0)):
+            first(i, k).wait_send()
+
+    for i, k in enumerate((1, 2, 3, 0)):
+        plan.at(starts[i], lambda i=i, k=k: first(i, k).start())
+        plan.at(totals[i], functools.partial(total, i, k))
+    plan.at(end, last)
+
+
+DEAL8_SEMS = [DMA((8,))] * 2 + [DMA]
+
+
+def deal8(plan, h, piece, put, sems, t0, t1):
+    ss, sr, own = sems
+    row = h.z * 2 + h.x
+
+    def place(r):
+        return (r // 2) * 4 + h.y * 2 + lax.rem(r, 2)
+
+    def send(step):
+        to = jnp.bitwise_xor(row, step)
+        return remote(piece(to), put(row), ss.at[step], sr.at[step], ctx=place(to))
+
+    def got(step):
+        at = jnp.bitwise_xor(row, step)
+        return remote(put(at), put(at), ss.at[step], sr.at[step], ctx=place(at))
+
+    local = pltpu.make_async_copy(piece(row), put(row), own)
+
+    def start():
+        for step in (7, 5, 6, 4, 3, 2, 1):
+            send(step).start()
+        local.start()
+
+    def end():
+        for step in (7, 5, 6, 4, 3, 2, 1):
+            got(step).wait_recv()
+        local.wait()
+
+    def drain():
+        for step in (7, 5, 6, 4, 3, 2, 1):
+            send(step).wait_send()
+
+    plan.at(t0, start)
+    plan.at(t1, end)
+    plan.at(t1 + 40, drain)
 
 ROWS = 256
 
@@ -422,6 +565,35 @@
     )
 
 
+SPREAD = ((22, 83, 140, 200), (60, 97, 160, 201), (84, 125, 190, 202))
+
+
+def spread_columns(plan, h, src, out, sems, t0, t1, t2, t3):
+    ys, yr, cs, cr = sems[3].at[0], sems[3].at[1], sems[3].at[2], sems[3].at[3]
+    w = out.shape[5]
+    deal8(
+        plan, h, lambda r: src.at[:, pl.ds(pl.multiple_of(r * w, 128), w)],
+        lambda r: out.at[r // 2, h.y, lax.rem(r, 2), h.core], sems[:3], t0, t1,
+    )
+    mine, theirs = out.at[:, h.y, :, h.core], out.at[:, 1 - h.y, :, h.core]
+    over_y = remote(mine, mine, ys, yr, ctx=h.yn)
+    all_mine, all_other = out.at[:, :, :, h.core], out.at[:, :, :, 1 - h.core]
+    over_core = remote(all_mine, all_mine, cs, cr, fsdp=1 - h.core)
+    plan.at(t1 + 0.5, over_y.start)
+
+    def pass_on():
+        remote(theirs, theirs, ys, yr, ctx=h.yn).wait_recv()
+        over_core.start()
+
+    def end():
+        remote(all_other, all_other, cs, cr, fsdp=1 - h.core).wait_recv()
+        over_y.wait_send()
+        over_core.wait_send()
+
+    plan.at(t2, pass_on)
+    plan.at(t3, end)
+
+
 def front_kernel(
     order, table, x, wq, wk, wv, wg, wu, wd, wo, cot, tile, cos, sin,
     normed, w_out, gains, qs, ks, vs, lse, low, g_out, u_out, d_out, o_out, c_out, *refs
@@ -441,13 +613,14 @@
     )
     done = gather16(plan, h, x, xg, take(refs, 13), 0, 14, 20, by_plane=True)
     for i, (src, out) in enumerate(((wg, g_out), (wu, u_out), (wd, d_out))):
-        deal_columns(plan, h, src, out, take(refs, 5), 20 + i, 190 + i, 170)
-    gather16(plan, h, wo, o_out.at[:, h.core], take(refs, 13), 75, 10, 14)
-    gather16(plan, h, cot, c_out, take(refs, 13), 105, 18, 26)
+        spread_columns(plan, h, src, out, take(refs, 4), *SPREAD[i])
+    gather16(plan, h, wo, o_out.at[:, h.core], take(refs, 13), 98, 10, 14)
+    seen = gather8(plan, h, cot, c_out, take(refs, 7), 82.5, 18, 20)
+    plan.at(185, lambda: [seen(zz) for zz in range(4)])
     to_sems = take(refs, 5)
     mine, other = o_out.at[:, h.core], o_out.at[:, 1 - h.core]
     across = remote(mine, mine, send, recv, fsdp=1 - h.core)
-    plan.at(160, across.start)
+    plan.at(165, across.start)
 
     def plane(k):
         return jnp.bitwise_xor(h.z, k)
@@ -515,13 +688,13 @@
 def front(order, table, x, wq, wk, wv, wg, wu, wd, wo, cot, tile, cos, sin):
     rows, width = x.shape
     length = 16 * rows
-    block = jax.ShapeDtypeStruct((16, 2, wg.shape[0], wg.shape[1] // 16), BF)
+    block = jax.ShapeDtypeStruct((4, 2, 2, 2, wg.shape[0], wg.shape[1] // 8), BF)
     heads = jax.ShapeDtypeStruct((length, 128), BF)
     outs = (
         jax.ShapeDtypeStruct((length, width), BF), jax.ShapeDtypeStruct((width, 384), BF),
         jax.ShapeDtypeStruct((8, width), F32), heads, heads, heads, jax.ShapeDtypeStruct((2, length), F32),
         jax.ShapeDtypeStruct((rows, width), BF), block, block, block,
-        jax.ShapeDtypeStruct((16, 2) + wo.shape, BF), jax.ShapeDtypeStruct((16, rows, width), BF),
+        jax.ShapeDtypeStruct((16, 2) + wo.shape, BF), jax.ShapeDtypeStruct((8, rows, width), BF),
     )
     smem = pl.BlockSpec(memory_space=pltpu.SMEM)
     scratch = [
@@ -529,17 +702,17 @@
         pltpu.VMEM((4 * rows, width), BF), *[pltpu.VMEM((32, 64, 128), BF)] * 4, pltpu.VMEM((16, rows, 128), BF),
         DMA, DMA, DMA,
     ]
-    scratch += DEAL_SEMS * 4 + GATHER_SEMS + DEAL_SEMS * 3 + GATHER_SEMS * 2 + DEAL_SEMS
+    scratch += DEAL_SEMS * 4 + GATHER_SEMS + (DEAL8_SEMS + [DMA((4,))]) * 3 + GATHER_SEMS + GATHER8_SEMS + DEAL_SEMS
     return comm_call(
         front_kernel, outs, [ANY] + [INNER] * 6 + [ANY] * 6, [smem] * 2 + [INNER] + [ANY] * 8 + [INNER] * 3, scratch, 0,
         "front", 58,
     )(order, table, x, wq, wk, wv, wg, wu, wd, wo, cot, tile, cos, sin)
 
 
-def mlp_kernel(src, cot, bg, bu, bd, gmi, out_part, own_gu, d_home, *refs):
+def mlp_kernel(src, cot, bg, bu, bd, gmi, out_part, sum_g, own_u, d_home, *refs):
     refs = list(refs)
     xm, ct, wg, wu, wd, grads, act, part, stage, cols = take(refs, 10)
-    other_gu, got_gu, own_d, other_d, got_d = take(refs, 5)
+    own_g, other_gu, got_gu, own_d, other_d, got_d, sum_d = take(refs, 7)
     w_sem, ct_sem, cols_sem, stage_sem, ex_sems = take(refs, 5)
     rows, width = src.shape
     hidden = wg.shape[1]
@@ -551,16 +724,16 @@
         return jnp.bitwise_xor(h.z, k)
 
     def load_cot(k):
-        return pltpu.make_async_copy(cot.at[pl.ds(plane(k) * 4, 4)], ct.at[k % 2], ct_sem.at[k % 2])
+        return pltpu.make_async_copy(cot.at[pl.ds(plane(k) * 2, 2)], ct.at[k % 2], ct_sem.at[k % 2])
 
     def put_out(k):
-        return pltpu.make_async_copy(stage, out_part.at[pl.ds(plane(k) * 4, 4)], stage_sem)
+        return pltpu.make_async_copy(stage, out_part.at[pl.ds(plane(k) * 2, 2)], stage_sem)
 
     for c in loads + [load_cot(0), load_cot(1)]:
         c.start()
     greet_all(h)
     plan = Plan()
-    done = gather16(plan, h, src, xm, take(refs, 13), 0, 12, 17, by_plane=True)
+    done = gather8(plan, h, src, xm, take(refs, 7), 0, 12, 12)
 
     def work(k):
         zz = plane(k)
@@ -571,40 +744,34 @@
         load_cot(k).wait()
         if k:
             put_out(k - 1).wait()
-
-        def pair(p, carry):
-            two = pl.ds(p * 2, 2)
-            at = pl.ds(pl.multiple_of((zz * 4 + p * 2) * rows, 2 * rows), 2 * rows)
-            x = xm[pl.ds(zz * 4 + p * 2, 2)].reshape(2 * rows, width)
-            gate, up = _nn(x, wg[...]), _nn(x, wu[...])
-            sig = jax.nn.sigmoid(gate)
-            silu = gate * sig
-            low = (silu * up).astype(BF)
-            act[at, :] = low
-            stage[two] = _nt(low, wd[...]).astype(BF).reshape(2, rows, width)
-            grad = _nn(ct[k % 2, two].reshape(2 * rows, width), wd[...])
-            grad_gate = (grad * up * sig * (1.0 + gate * (1.0 - sig))).astype(BF)
-            grad_up = (grad * silu).astype(BF)
-            grads[at, pl.ds(0, hidden)] = grad_gate
-            grads[at, pl.ds(hidden, hidden)] = grad_up
-            back = _nt(grad_gate, wg[...]) + _nt(grad_up, wu[...])
-            part[zz, pl.ds(p, 1)] = back.astype(BF).reshape(1, 2, rows, width)
-            return carry
-
-        lax.fori_loop(0, 2, pair, 0)
+        at = pl.ds(pl.multiple_of(zz * 2 * rows, 2 * rows), 2 * rows)
+        x = xm[pl.ds(zz * 2, 2)].reshape(2 * rows, width)
+        gate, up = _nn(x, wg[...]), _nn(x, wu[...])
+        sig = jax.nn.sigmoid(gate)
+        silu = gate * sig
+        low = (silu * up).astype(BF)
+        act[at, :] = low
+        stage[...] = _nt(low, wd[...]).astype(BF).reshape(2, rows, width)
+        grad = _nn(ct[k % 2].reshape(2 * rows, width), wd[...])
+        grad_gate = (grad * up * sig * (1.0 + gate * (1.0 - sig))).astype(BF)
+        grad_up = (grad * silu).astype(BF)
+        grads[at, pl.ds(0, hidden)] = grad_gate
+        grads[at, pl.ds(hidden, hidden)] = grad_up
+        back = _nt(grad_gate, wg[...]) + _nt(grad_up, wu[...])
+        part[zz] = back.astype(BF).reshape(2, rows, width)
         put_out(k).start()
         if k + 2 < 4:
             load_cot(k + 2).start()
 
     for k in range(4):
-        plan.at((22, 38, 55, 72)[k], functools.partial(work, k))
-    plan.at(76, lambda: put_out(3).wait())
-    scatter16(plan, h, part, gmi, take(refs, N_SCATTER), 44, 18)
-
-    def split(c, both, own, other):
+        plan.at((15, 26, 38, 50)[k], functools.partial(work, k))
+    plan.at(55, lambda: put_out(3).wait())
+    scatter8(plan, h, part, gmi, take(refs, N_SCATTER8), (27, 39, 50.2, 50.3), (50.4, 58.5, 66.5, 75), 110)
+
+    def split(c, both, own, other, lanes):
         both = both.astype(BF).reshape(2, block, both.shape[1])
         own[c] = jnp.where(h.core == 0, both[0], both[1])
-        other[c] = jnp.where(h.core == 0, both[1], both[0])
+        other[c, :, lanes] = jnp.where(h.core == 0, both[1], both[0])
 
     def exchange(i, other, got):
         return remote(other, got, ex_sems.at[i], ex_sems.at[2 + i], fsdp=1 - h.core)
@@ -617,8 +784,9 @@
     def grads_gu(first):
         def one(c, carry):
             at = pl.ds(pl.multiple_of(c * 2 * block, 128), 2 * block)
-            lhs = xm[:, :, at].reshape(16 * rows, 2 * block)
-            split(c, _tn(lhs, grads[...]), own_gu, other_gu)
+            lhs = xm[:, :, at].reshape(8 * rows, 2 * block)
+            split(c, _tn(lhs, grads[:, :hidden]), own_g, other_gu, pl.ds(0, hidden))
+            split(c, _tn(lhs, grads[:, hidden:]), own_u, other_gu, pl.ds(hidden, hidden))
             return carry
 
         lax.fori_loop(first, first + 4, one, 0)
@@ -627,46 +795,74 @@
         def one(c, carry):
             pl.when(c < 15)(lambda: load_cols(c + 1).start())
             load_cols(c).wait()
-            lhs = cols[lax.rem(c, 2)].reshape(16 * rows, 2 * block)
-            split(c, _tn(lhs, act[...]), own_d, other_d)
+            lhs = cols[lax.rem(c, 2)].reshape(8 * rows, 2 * block)
+            split(c, _tn(lhs, act[...]), own_d, other_d, pl.ds(0, hidden))
             return carry
 
         lax.fori_loop(first, first + 4, one, 0)
 
-    def join(i, own, other, got):
+    def over_y(i, own, result):
+        own, result = own.reshape(4, 2, 2, *own.shape[1:]), result.reshape(4, 2, *own.shape[1:])
+        return remote(own.at[:, 1 - h.y], result, ex_sems.at[4 + i], ex_sems.at[6 + i], ctx=h.yn)
+
+    def join(i, own, other, got, result):
         exchange(i, other, got).wait_recv()
         for c in range(16):
-            own[c] = (own[c].astype(F32) + got[c].astype(F32)).astype(BF)
+            own[c] = (own[c].astype(F32) + got[c, :, 0:hidden].astype(F32)).astype(BF)
+        over_y(i, own, result).start()
+
+    def join_u():
+        for c in range(16):
+            own_u[c] = (own_u[c].astype(F32) + got_gu[c, :, hidden:].astype(F32)).astype(BF)
+
+    def add_y(i, own, other, got, result):
+        over_y(i, own, result).wait_recv()
+        for r in range(8):
+            z, x = r // 2, r % 2
+            mine = jnp.where(h.y == 0, own[z * 4 + x], own[z * 4 + 2 + x])
+            result[r] = (mine.astype(F32) + result[r].astype(F32)).astype(BF)
+
+    def sent(i, own, other, got, result):
         exchange(i, other, got).wait_send()
-
-    plan.at(74, lambda: load_cols(0).start())
+        over_y(i, own, result).wait_send()
+
+    d, g = (own_d, other_d, got_d, sum_d), (own_g, other_gu, got_gu, sum_g)
+    plan.at(50.5, lambda: load_cols(0).start())
     for i in range(4):
-        plan.at(76.5 + 2 * i, functools.partial(grads_d, 4 * i))
-        plan.at(88 + 3 * i, functools.partial(grads_gu, 4 * i))
-    plan.at(85, lambda: exchange(1, other_d, got_d).start())
-    plan.at(89, lambda: join(1, own_d, other_d, got_d))
-    plan.at(100, lambda: exchange(0, other_gu, got_gu).start())
-    plan.at(110, lambda: join(0, own_gu, other_gu, got_gu))
-    deal16(plan, h, lambda c: own_d.at[c], columns_of(d_home, hidden), None, take(refs, 5), 89.1, 182, both=False)
+        plan.at(56 + 2 * i, functools.partial(grads_d, 4 * i))
+        plan.at(68 + 3 * i, functools.partial(grads_gu, 4 * i))
+    plan.at(64, lambda: exchange(1, other_d, got_d).start())
+    plan.at(68.5, lambda: join(1, *d))
+    plan.at(82, lambda: exchange(0, other_gu, got_gu).start())
+    plan.at(86, lambda: join(0, *g))
+    plan.at(86.5, join_u)
+    plan.at(90, lambda: add_y(1, *d))
+    deal8(plan, h, lambda r: sum_d.at[r], columns_of(d_home, hidden), take(refs, 3), 90.1, 200)
+    plan.at(112, lambda: add_y(0, *g))
+    plan.at(201, lambda: [sent(1, *d), sent(0, *g)])
     plan.run()
 
 
 def mlp(src, cot, bg, bu, bd):
     rows, width = src.shape
-    block, hidden = bg.shape[2:]
+    block, hidden = bg.shape[4:]
     full = pltpu.VMEM((width, hidden), BF)
     gu, d = pltpu.VMEM((16, block, 2 * hidden), BF), pltpu.VMEM((16, block, hidden), BF)
     scratch = [
-        pltpu.VMEM((16, rows, width), BF), pltpu.VMEM((2, 4, rows, width), BF), full, full, full,
-        pltpu.VMEM((16 * rows, 2 * hidden), BF), pltpu.VMEM((16 * rows, hidden), BF),
-        pltpu.VMEM((4, 2, 2, rows, width), BF), pltpu.VMEM((4, rows, width), BF),
-        pltpu.VMEM((2, 16, rows, 2 * block), BF), gu, gu, d, d, d,
-        DMA((3,)), DMA((2,)), DMA((2,)), DMA, DMA((4,)),
+        pltpu.VMEM((8, rows, width), BF), pltpu.VMEM((2, 2, rows, width), BF), full, full, full,
+        pltpu.VMEM((8 * rows, 2 * hidden), BF), pltpu.VMEM((8 * rows, hidden), BF),
+        pltpu.VMEM((4, 2, rows, width), BF), pltpu.VMEM((2, rows, width), BF),
+        pltpu.VMEM((2, 8, rows, 2 * block), BF), d, gu, gu, d, d, d,
+        pltpu.VMEM((8, block, hidden), BF),
+        DMA((3,)), DMA((2,)), DMA((2,)), DMA, DMA((8,)),
     ]
-    scratch += GATHER_SEMS + scatter_scratch(rows, width) + DEAL_SEMS
-    home = jax.ShapeDtypeStruct((block, 16 * hidden), BF)
-    outs = (jax.ShapeDtypeStruct((rows, width), F32), jax.ShapeDtypeStruct((16, rows, width), BF), jax.ShapeDtypeStruct((16, block, 2 * hidden), BF), home)
-    return comm_call(mlp_kernel, outs, [INNER, ANY, INNER, ANY], [ANY] * 5, scratch, 5, "mlp", 61)(
+    scratch += GATHER8_SEMS + scatter8_scratch(rows, width) + DEAL8_SEMS
+    outs = (
+        jax.ShapeDtypeStruct((rows, width), F32), jax.ShapeDtypeStruct((8, rows, width), BF),
+        jax.ShapeDtypeStruct((8, block, hidden), BF), jax.ShapeDtypeStruct((16, block, hidden), BF),
+        jax.ShapeDtypeStruct((block, 8 * hidden), BF),
+    )
+    return comm_call(mlp_kernel, outs, [INNER, ANY, INNER, INNER, ANY], [ANY] * 5, scratch, 5, "mlp", 62)(
         src, cot, *(b.reshape(width, hidden) for b in (bg, bu, bd))
     )
 
@@ -694,7 +890,7 @@
     plan.at(t1, add)
 
 
-def back_kernel(order, table, ga, qs, ks, vs, lse, cos, sin, out_part, low, branch, gu, dqkv, out_sum, wo_sum, g_home, *refs):
+def back_kernel(order, table, ga, qs, ks, vs, lse, cos, sin, out_part, low, branch, sum_g, own_u, dqkv, out_sum, wo_sum, sum_u, g_home, *refs):
     refs = list(refs)
     gh, gs, dq, dk, dv, own, other, got = take(refs, 8)
     send, recv = take(refs, 2)
@@ -704,13 +900,28 @@
     greet_all(h)
     plan = Plan()
     deal16(plan, h, columns(ga, 128), lambda c: gh_rows.at[c], None, take(refs, 5), 0, 14, both=False)
-    gu_sems = take(refs, 5)
-    scatter16(plan, h, out_part, out_sum, take(refs, N_SCATTER), 1, 20)
+    gu_sems = take(refs, 3)
+    scatter8(plan, h, out_part, out_sum, take(refs, N_SCATTER8), (1, 18, 35, 52), (18.8, 35.8, 52.8, 69.8), 94)
     outer_home(plan, h, low, branch, own, other, got, send, recv, 2, 8)
-    first = pl.ds(0, gu.shape[2] // 2)
-    deal16(
-        plan, h, lambda c: gu.at[c, :, first], columns_of(g_home, gu.shape[2] // 2), None, gu_sems, 3, 198, both=False
-    )
+    deal8(plan, h, lambda r: sum_g.at[r], columns_of(g_home, sum_g.shape[2]), gu_sems, 3, 198)
+    half_u, u_sems = take(refs, 2)
+    split_u = own_u.reshape(4, 2, 2, *own_u.shape[1:])
+    over_u = remote(split_u.at[:, 1 - h.y], sum_u, u_sems.at[0], u_sems.at[1], ctx=h.yn)
+    keep_u = pltpu.make_async_copy(split_u.at[:, h.y], half_u, u_sems.at[2])
+
+    def start_u():
+        over_u.start()
+        keep_u.start()
+
+    def end_u():
+        over_u.wait_recv()
+        keep_u.wait()
+        for z in range(4):
+            sum_u[z] = (sum_u[z].astype(F32) + half_u[z].astype(F32)).astype(BF)
+        over_u.wait_send()
+
+    plan.at(2.5, start_u)
+    plan.at(90, end_u)
     scatter16(plan, h, own.reshape(4, 2, 2, *own.shape[1:]), wo_sum, take(refs, N_SCATTER), 8.1, 18)
 
     def begin():
@@ -735,7 +946,7 @@
     plan.run()
 
 
-def back(order, table, ga, qs, ks, vs, lse, cos, sin, out_part, low, branch, gu):
+def back(order, table, ga, qs, ks, vs, lse, cos, sin, out_part, low, branch, sum_g, own_u):
     rows, width = ga.shape
     length = qs.shape[0]
     smem = pl.BlockSpec(memory_space=pltpu.SMEM)
@@ -744,101 +955,152 @@
         jax.ShapeDtypeStruct((length, 384), BF),
         jax.ShapeDtypeStruct((rows, width), F32),
         jax.ShapeDtypeStruct((width // 32, width), F32),
-        jax.ShapeDtypeStruct((gu.shape[1], 8 * gu.shape[2]), BF),
+        jax.ShapeDtypeStruct((4, 2) + sum_g.shape[1:], BF),
+        jax.ShapeDtypeStruct((sum_g.shape[1], 8 * sum_g.shape[2]), BF),
     )
     scratch = [pltpu.VMEM((32, 64, 128), BF), pltpu.VMEM((length, 128), BF)]
-    scratch += [pltpu.VMEM((32, 64, 128), F32)] * 3 + [half] * 3 + [DMA] * 2 + DEAL_SEMS * 2
-    scratch += scatter_scratch(rows, width) + scatter_scratch(width // 32, width)
-    return comm_call(back_kernel, outs, [INNER] * 3 + [ANY], [smem] * 2 + [INNER] * 10 + [ANY], scratch, 6, "back", 60)(
-        order, table, ga, qs, ks, vs, lse, cos, sin, out_part.reshape(4, 2, 2, rows, width), low, branch, gu
-    )
-
-
-def core_sum(plan, h, part, got, total, sems, t0, t1):
-    send, recv, mine = sems
-    across = remote(part.at[:, 1 - h.core], got, send, recv, fsdp=1 - h.core)
-    local = pltpu.make_async_copy(part.at[:, h.core], total, mine)
-
-    def start():
-        across.start()
-        local.start()
-
-    def add():
-        across.wait_recv()
-        local.wait()
-        for c in range(16):
-            total[c] = (total[c].astype(F32) + got[c].astype(F32)).astype(BF)
-        across.wait_send()
-
-    plan.at(t0, start)
-    plan.at(t1, add)
-
-
-def home_kernel(n, *refs):
+    scratch += [pltpu.VMEM((32, 64, 128), F32)] * 3 + [half] * 3 + [DMA] * 2 + DEAL_SEMS + DEAL8_SEMS
+    scratch += scatter8_scratch(rows, width) + [pltpu.VMEM((4, 2) + sum_g.shape[1:], BF), DMA((3,))]
+    scratch += scatter_scratch(width // 32, width)
+    return comm_call(back_kernel, outs, [INNER] * 4 + [ANY], [smem] * 2 + [INNER] * 10 + [ANY] * 2, scratch, 6, "back", 60)(
+        order, table, ga, qs, ks, vs, lse, cos, sin, out_part.reshape(4, 2, rows, width), low, branch, sum_g, own_u
+    )
+
+
+def home_kernel(
+    dqkv, wqkv, normed, gd, gg, gu, x, grad_hidden, gain, other_gain,
+    input_grad, q_out, k_out, v_out, gains_out, d_out, g_out, u_out, *refs
+):
     refs = list(refs)
-    gn, parts, (scaled, other_gain, gu) = take(refs, 1)[0], take(refs, n), take(refs, 3)
-    gn_out, outs, gains_out, u_home = take(refs, 1)[0], take(refs, n), *take(refs, 2)
+    part, nm, own, other, got, landed, d32, g32, u16, u32, gn, gains, gains_got, gains_landed = take(refs, 14)
+    nm_sem, ex_sems, out_sems, gain_sems = take(refs, 4)
+    rows, width = x.shape
+    block = own.shape[1]
     h = Here()
+    load = pltpu.make_async_copy(normed, nm, nm_sem)
+    load.start()
     greet_all(h)
     plan = Plan()
-    for i, (part, out) in enumerate(zip(parts, outs)):
-        got, total = take(refs, 2)
-        core_sum(plan, h, part, got, total, take(refs, 3), 0.1 * i, 2 * i + 1)
-        deal16(
-            plan, h, lambda c, t=total: t.at[c], columns_of(out, part.shape[3]), None, take(refs, 5), 2 * i + 1.5, 198 + i,
-            both=False,
-        )
-    last = pl.ds(gu.shape[2] // 2, gu.shape[2] // 2)
-    deal16(
-        plan, h, lambda c: gu.at[c, :, last], columns_of(u_home, gu.shape[2] // 2), None, take(refs, 5), 0.5, 197, both=False
-    )
-    gains, got, landed, send, recv = take(refs, 5)
-    gain_sems = take(refs, 5)
-    scatter16(plan, h, gn, gn_out, refs, 0.5, 20)
-    over = remote(gains, got, send, recv, fsdp=1 - h.core)
+    deal8(plan, h, lambda r: gu.at[r], columns_of(u16, gu.shape[2]), take(refs, 3), 0.4, 150)
+
+    def plane(k):
+        zz = jnp.bitwise_xor(h.z, k)
+        for p in range(2):
+            at = pl.ds(pl.multiple_of((zz * 4 + p * 2) * rows, 2 * rows), 2 * rows)
+            part[zz, pl.ds(p, 1)] = _nt(dqkv[at, :], wqkv[...]).astype(BF).reshape(1, 2, rows, width)
+
+    for i, k in enumerate((1, 2, 3, 0)):
+        plan.at((0.1, 1, 2, 3)[i], functools.partial(plane, k))
+    scatter16(plan, h, part, gn, take(refs, N_SCATTER), 0.2, 20)
+    plan.at(4, load.wait)
+
+    def grads(first):
+        def one(c, carry):
+            at = pl.ds(pl.multiple_of(c * 2 * block, 128), 2 * block)
+            both = _tn(nm[:, at], dqkv[...]).astype(BF).reshape(2, block, 384)
+            own[c] = jnp.where(h.core == 0, both[0], both[1])
+            other[c] = jnp.where(h.core == 0, both[1], both[0])
+            return carry
+
+        lax.fori_loop(first, first + 4, one, 0)
+
+    for i in range(4):
+        plan.at(4.1 + i, functools.partial(grads, 4 * i))
+    over = remote(other, got, ex_sems.at[0], ex_sems.at[1], fsdp=1 - h.core)
+    plan.at(8, over.start)
+
+    def join():
+        over.wait_recv()
+        for c in range(16):
+            own[c] = (own[c].astype(F32) + got[c].astype(F32)).astype(BF)
+        over.wait_send()
+
+    plan.at(10, join)
+    deal16(plan, h, lambda c: own.at[c], lambda c: landed.at[c], None, take(refs, 5), 10.1, 151, both=False)
+    writes = [
+        pltpu.make_async_copy(a, b, out_sems.at[i]) for i, (a, b) in enumerate(((d32, d_out), (g32, g_out), (u32, u_out)))
+    ]
+
+    def widen(i, source, target):
+        target[...] = source[...].astype(F32)
+        writes[i].start()
+
+    plan.at(15, functools.partial(widen, 0, gd, d32))
+    plan.at(25, functools.partial(widen, 1, gg, g32))
+    plan.at(152, functools.partial(widen, 2, u16, u32))
+
+    def finish_qkv():
+        for c in range(16):
+            for i, out in enumerate((q_out, k_out, v_out)):
+                out[:, c * 128 : (c + 1) * 128] = landed[c, :, i * 128 : (i + 1) * 128].astype(F32)
+
+    plan.at(203, finish_qkv)
+    gain_over = remote(gains, gains_got, ex_sems.at[2], ex_sems.at[3], fsdp=1 - h.core)
+
+    def source():
+        value = x[...].astype(F32)
+        return value, lax.rsqrt(jnp.mean(value * value, -1, keepdims=True) + EPSILON)
 
     def sums():
+        value, inverse = source()
         gains[...] = jnp.zeros_like(gains)
-        total = jnp.sum(gn_out[...] * scaled[...], 0, keepdims=True)
+        total = jnp.sum(gn[...] * value * inverse, 0, keepdims=True)
         for c in range(16):
             at = slice(c * 128, (c + 1) * 128)
             gains[c, 0:1] = total[:, at]
             gains[c, 1:2] = other_gain[:, at]
-        over.start()
-        over.wait_recv()
-        over.wait_send()
-        gains[...] += got[...]
+        gain_over.start()
+
+    def pass_on():
+        gain_over.wait_recv()
+        gain_over.wait_send()
+        gains[...] += gains_got[...]
+
+    def result():
+        value, inverse = source()
+        scaled = gn[...] * gain[0:1, :]
+        inner = jnp.sum(scaled * value, -1, keepdims=True)
+        input_grad[...] = (
+            grad_hidden[...] + inverse * scaled - inverse * inverse * inverse / width * value * inner
+        )
 
     plan.at(200, sums)
-    deal16(plan, h, lambda c: gains.at[c], lambda c: landed.at[c], None, gain_sems, 201, 204, both=False)
+    plan.at(201, pass_on)
+    deal16(plan, h, lambda c: gains.at[c], lambda c: gains_landed.at[c], None, take(refs, 5), 201.5, 204, both=False)
+    plan.at(202, result)
 
     def add():
-        total = landed[0]
+        total = gains_landed[0]
         for c in range(1, 16):
-            total = total + landed[c]
+            total = total + gains_landed[c]
         gains_out[...] = total
+        for w in writes:
+            w.wait()
 
     plan.at(300, add)
     plan.run()
 
 
-def home(gn, parts, scaled, other_gain, gu):
-    scratch = []
-    rows, width = gn.shape[0] // 16, gn.shape[1]
-    for p in parts:
-        buffer = pltpu.VMEM((p.shape[0],) + p.shape[2:], BF)
-        scratch += [buffer, buffer, DMA, DMA, DMA] + DEAL_SEMS
-    outs = [jax.ShapeDtypeStruct((rows, width), F32)]
-    outs += [jax.ShapeDtypeStruct((p.shape[2], 16 * p.shape[3]), BF) for p in parts]
-    outs.append(jax.ShapeDtypeStruct((8, 128), F32))
-    outs.append(jax.ShapeDtypeStruct((gu.shape[1], 8 * gu.shape[2]), BF))
-    n = len(parts)
+def home(dqkv, wqkv, normed, gd, gg, gu, x, grad_hidden, gain, other_gain):
+    rows, width = x.shape
+    block, wide = gd.shape
+    third = pltpu.VMEM((16, block, 384), BF)
     tile = pltpu.VMEM((16, 8, 128), F32)
-    scratch += DEAL_SEMS + [tile, tile, tile, DMA, DMA] + DEAL_SEMS + scatter_scratch(rows, width)
+    wide32 = pltpu.VMEM((block, wide), F32)
+    small = jax.ShapeDtypeStruct((block, width), F32)
+    large = jax.ShapeDtypeStruct((block, wide), F32)
+    outs = (
+        jax.ShapeDtypeStruct((rows, width), F32), small, small, small, jax.ShapeDtypeStruct((8, 128), F32), large, large, large
+    )
+    scratch = [
+        pltpu.VMEM((4, 2, 2, rows, width), BF), pltpu.VMEM(normed.shape, BF), third, third, third, third, wide32, wide32,
+        pltpu.VMEM((block, wide), BF), wide32, pltpu.VMEM((rows, width), F32), tile, tile, tile,
+        DMA, DMA((4,)), DMA((3,)), DMA,
+    ]
+    scratch += DEAL8_SEMS + scatter_scratch(rows, width) + DEAL_SEMS * 2
     return comm_call(
-        functools.partial(home_kernel, n), tuple(outs), [INNER] + [ANY] * n + [INNER, ANY], [INNER] + [ANY] * n + [INNER] * 2 + [ANY],
-        scratch, 7, "home", 58,
-    )(gn.reshape(4, 2, 2, rows, width), *parts, scaled, other_gain, gu)
+        home_kernel, outs, [INNER] * 5 + [ANY] * 3, [INNER, INNER, ANY, INNER, INNER, ANY] + [INNER] * 4, scratch, 7, "home", 60
+    )(dqkv, wqkv, normed, gd, gg, gu, x, grad_hidden, gain, other_gain)
 
 
 def rope_tables(positions):
@@ -885,7 +1147,7 @@
     inv_in = lax.rsqrt(jnp.mean(own * own, -1, keepdims=True) + EPSILON)
     hidden = own + dot(attn_low, full_out)
     inv_mid = lax.rsqrt(jnp.mean(hidden * hidden, -1, keepdims=True) + EPSILON)
-    gmi, out_part, part_gu, gd = mlp((hidden * inv_mid * mgain).astype(BF), cot_all, bg, bu, bd)
+    gmi, out_part, sum_g, own_u, gd = mlp((hidden * inv_mid * mgain).astype(BF), cot_all, bg, bu, bd)
 
     def norm_back(grad, source, inv, gain):
         scaled = grad * gain
@@ -896,21 +1158,14 @@
     grad_hidden = cot.astype(F32) + norm_back(gmi, hidden, inv_mid, mgain)
     grad_branch = grad_hidden.astype(BF)
     grad_att = dot_nt(grad_branch, full_out).astype(BF)
-    grad_qkv, out_sum, wo_grad, gg = back(
-        order, table, grad_att, qs, ks, vs, lse, cos, sin, out_part, attn_low, grad_branch, part_gu
+    grad_qkv, out_sum, wo_grad, sum_u, gg = back(
+        order, table, grad_att, qs, ks, vs, lse, cos, sin, out_part, attn_low, grad_branch, sum_g, own_u
     )
     layer_output = (hidden + out_sum).astype(BF)
-    gn_part = dot_nt(grad_qkv, wqkv).astype(BF)
-
-    def pieces(grad):
-        return grad.astype(BF).reshape(16, 2, 64, grad.shape[1])
-
-    parts = [pieces(dot_tn(normed, grad_qkv))]
-    gn, gqkv, gains, gu = home(gn_part, parts, own * inv_in, mgain_part[None], part_gu)
-    input_grad = grad_hidden + norm_back(gn, own, inv_in, again)
-    gg, gu, gd, gqkv = (g.astype(F32) for g in (gg, gu, gd, gqkv))
-    gq, gk, gv = (gqkv.reshape(64, 16, 3, 128)[:, :, i].reshape(64, width) for i in range(3))
-    gains = lax.dynamic_slice_in_dim(gains, core * 64, 64, 1)
+    input_grad, gq, gk, gv, both, gd, gg, gu = home(
+        grad_qkv, wqkv, normed, gd, gg, sum_u.reshape(sum_g.shape), x, grad_hidden, gains, mgain_part[None]
+    )
+    gains = lax.dynamic_slice_in_dim(both, core * 64, 64, 1)
     return (layer_output[None], input_grad[None], gains[0], gq, gk, gv, wo_grad, gains[1], gg, gu, gd)
 
 

time: 799 us -> 682 us (0.85)
  Pallas kernels: 721 us -> 630 us
  matrix products: 29 us -> 12.2 us
    pallas_call x3, Pallas kernels: 473 us -> 392 us  [the longest x1 144 us: mlp(): comm_call(mlp_kernel, outs, [INNER, ANY, INNER, INNER, ANY], [ANY] * 5, s...]
    pallas_call x1, Pallas kernels: 248 us -> 238 us  [front(): comm_call(front_kernel, outs, [ANY] + [INNER] * 6 + [ANY] * 6, [smem] * 2...]
    dot_general x1 -> x0, matrix products: 9.65 us -> none  [dot_tn(): lax.dot_general(a, b, (((0,), (0,)), ((), ())), preferred_element_type=F32)]
where the time goes in v3:
time: 682 us; the launch traced here: 669 us
  Pallas kernels  630 us (92%)
  local copies, waits for them, and re-layouts  15.5 us (2%)
  matrix products  12.2 us (2%)
  other arithmetic  10 us (1%)
    pallas_call x1, Pallas kernels, front(): comm_call(front_kernel, outs, [ANY] + [INNER] * 6 + [ANY] * 6, [smem] * 2...  238 us
    pallas_call x1, Pallas kernels, mlp(): comm_call(mlp_kernel, outs, [INNER, ANY, INNER, INNER, ANY], [ANY] * 5, s...  144 us
    pallas_call x1, Pallas kernels, back(): comm_call(back_kernel, outs, [INNER] * 4 + [ANY], [smem] * 2 + [INNER] *...  128 us
    pallas_call x1, Pallas kernels, home(): comm_call(home_kernel, outs, [INNER] * 5 + [ANY] * 3, [INNER, INNER, ANY,...  120 us

profile of v3, /device:TPU:9, one launch (start us, length us, event | category | flops | bytes accessed | tf_op | source)
XLA Modules:
  0.0 668.6 jit_solution(2702593932970358536)
XLA Ops:
  0.7 0.7 pad_maximum_fusion
  1.4 0.1 tile.13
  1.5 0.6 pad.4.tile
  2.1 0.8 copy.28
  2.9 0.6 select_reduce_fusion.order
  3.7 1.0 multiply_sine_fusion
  4.7 0.1 tile.31
  4.8 0.3 copy.29
  5.1 1.0 broadcast_multiply_fusion.sin
  6.2 0.1 tile.14
  6.3 1.3 copy.30.cos
  7.6 237.8 %front.1 = (bf16[2048,2048]{1,0:T(8,128)(2,1)}, bf16[2048,384]{1,0:T(8,128)(2,1)}, f32[8,2048]{1,0:T(8,128)}, bf16[2048,128]{1,0:T(8,128)(2,1)}, bf16[2048,128]{...) custom-call(s32[32]{0:T(128)} %select_reduce_fusion.order, ...), custom_call_target="tpu_custom_call" | custom-call | tf_op jit(solution)/shard_map/front/pallas_call | solution.py:706
  245.4 0.8 slice.9
  246.2 5.0 multiply_reduce_fusion.2
  251.2 1.0 multiply_convert_fusion.src
  252.1 143.9 %mlp.1 = (f32[128,2048]{1,0:T(8,128)}, bf16[8,128,2048]{2,1,0:T(8,128)(2,1)}, bf16[8,64,1024]{2,1,0:T(8,128)(2,1)}, bf16[16,64,1024]{2,1,0:T(8,128)(2,1)}, bf16[64,8192]{1,0:T(8,128)(2,1)}) custom-call(bf16[128,2048]{1,0:T(8,128)(2,1)} %multiply_convert_fusion.src, bf16[8,128,2048]{2,1,0:T(8,128)(2,1)} %get-tuple-element.45.cot, ...), custom_call_target="tpu_custom_call" | custom-call | tf_op jit(solution)/shard_map/mlp/pallas_call | solution.py:865
  396.1 2.1 multiply_reduce_fusion
  398.2 2.6 fusion.3
  400.7 7.2 %convolution_convert_fusion.ga = bf16[128,2048]{1,0:T(8,128)(2,1)} fusion(bf16[128,2048]{1,0:T(8,128)(2,1)S(1)} %get-tuple-element.75.branch, bf16[2048,2048]{1,0:T(8,128)(2,1)} %bitcast.29), kind=kOutput, calls=%fused_computation.1 | convolution fusion | flops 1074003968 | bytes 9437184 | tf_op jit(solution)/shard_map/dot_general | solution.py:1133
  408.0 128.5 %back.1 = (bf16[2048,384]{1,0:T(8,128)(2,1)}, f32[128,2048]{1,0:T(8,128)}, f32[64,2048]{1,0:T(8,128)}, bf16[4,2,64,1024]{3,2,1,0:T(8,128)(2,1)}, bf16[64,8192]{1,0:T(8,128)(2,1)}) custom-call(s32[32]{0:T(128)} %select_reduce_fusion.order, s32[32]{0:T(128)} %copy-done.11, bf16[128,2048]{1,0:T(8,128)(2,1)} %convolution_convert_fusion.ga, ...), custom_call_target="tpu_custom_call" | custom-call | tf_op jit(solution)/shard_map/back/pallas_call | solution.py:965
  536.5 119.8 %home.1 = (f32[128,2048]{1,0:T(8,128)}, f32[64,2048]{1,0:T(8,128)}, f32[64,2048]{1,0:T(8,128)}, f32[64,2048]{1,0:T(8,128)}, f32[8,128]{1,0:T(8,128)}, /*index=5*...) custom-call(bf16[2048,384]{1,0:T(8,128)(2,1)} %get-tuple-element.58.dqkv, ...), custom_call_target="tpu_custom_call" | custom-call | tf_op jit(solution)/shard_map/home/pallas_call | solution.py:1101
  656.3 0.9 fusion
  657.2 1.2 constant_dynamic-slice_fusion
  658.5 0.5 slice_bitcast_fusion
  659.0 2.3 copy.40
  661.3 0.8 copy.41
  662.1 0.8 copy.42
  662.9 0.8 copy.43
  663.7 0.8 copy.44
  664.5 1.3 copy.45
  665.8 1.3 copy.46
  667.1 1.3 copy.47
  (34 shorter events, 0.3 us)
Async XLA Ops:
  2.9 4.7 copy-start.11
  7.6 238.6 %copy-start = (bf16[1,128,2048]{2,1,0:T(8,128)(2,1)S(1)}, bf16[1,128,2048]{2,1,0:T(8,128)(2,1)}, u32[]{:S(2)}) copy-start(bf16[1,128,2048]{2,1,0:T(8,128)(2,1)} %param.12) | copy-start | bytes 1572868
  252.1 146.0 %copy-start.2 = (bf16[1,128,2048]{2,1,0:T(8,128)(2,1)S(1)}, bf16[1,128,2048]{2,1,0:T(8,128)(2,1)}, u32[]{:S(2)}) copy-start(bf16[1,128,2048]{2,1,0:T(8,128)(2,1)} %param.23) | copy-start | bytes 1572868
  400.7 7.3 %copy-start.1 = (bf16[128,2048]{1,0:T(8,128)(2,1)}, bf16[128,2048]{1,0:T(8,128)(2,1)S(1)}, u32[]{:S(2)}) copy-start(bf16[128,2048]{1,0:T(8,128)(2,1)S(1)} %get-tuple-element.75.branch) | copy-start | bytes 1572868
  536.5 119.8 %copy-start.6 = (f32[128,2048]{1,0:T(8,128)S(1)}, f32[128,2048]{1,0:T(8,128)}, u32[]{:S(2)}) copy-start(f32[128,2048]{1,0:T(8,128)} %get-tuple-element.57) | copy-start | bytes 3145732
  656.3 5.0 copy-start.10
  656.3 5.8 copy-start.9
  656.3 6.6 copy-start.8
  656.3 7.4 %copy-start.7 = (f32[64,2048]{1,0:T(8,128)S(1)}, f32[64,2048]{1,0:T(8,128)}, u32[]{:S(2)}) copy-start(f32[64,2048]{1,0:T(8,128)} %get-tuple-element.102) | copy-start | bytes 1572868
  656.3 8.2 %copy-start.5 = (f32[64,8192]{1,0:T(8,128)S(1)}, f32[64,8192]{1,0:T(8,128)}, u32[]{:S(2)}) copy-start(f32[64,8192]{1,0:T(8,128)} %get-tuple-element.104) | copy-start | bytes 6291460
  661.3 4.5 copy-start.4
  664.5 2.6 copy-start.3

commit v4 on v3

--- a/solution.py
+++ b/solution.py
@@ -596,11 +596,11 @@
 
 def front_kernel(
     order, table, x, wq, wk, wv, wg, wu, wd, wo, cot, tile, cos, sin,
-    normed, w_out, gains, qs, ks, vs, lse, low, g_out, u_out, d_out, o_out, c_out, *refs
+    normed, w_out, gains, qs, ks, vs, lse, low, hidden, mlp_in, g_out, u_out, d_out, o_out, c_out, *refs
 ):
     refs = list(refs)
-    xg, wqkv, tiles, stage, q, k_rows, v, o, o_rows = take(refs, 9)
-    stage_sem, send, recv = take(refs, 3)
+    xg, wqkv, tiles, stage, q, k_rows, v, o, o_rows, w_part = take(refs, 10)
+    stage_sem, send, recv, w_sems = take(refs, 4)
     rows, width = x.shape
     h = Here()
     greet_all(h)
@@ -675,13 +675,31 @@
             o_rows[b // 2, (b % 2) * 64 : (b % 2 + 1) * 64, :] = o[table[b]]
 
     plan.at(96, unsort)
-    deal16(plan, h, lambda c: o_rows.at[c], columns_of(low, 128), None, to_sems, 96.1, 200, both=False)
+    deal16(plan, h, lambda c: o_rows.at[c], columns_of(low, 128), None, to_sems, 96.1, 172, both=False)
 
     def end():
         remote(other, other, send, recv, fsdp=1 - h.core).wait_recv()
         across.wait_send()
 
-    plan.at(210, end)
+    def load(b):
+        return pltpu.make_async_copy(o_out.at[pl.ds(4 * b, 4)], w_part.at[b % 2], w_sems.at[b % 2])
+
+    def project():
+        load(0).start()
+        load(1).start()
+        total = x[...].astype(F32)
+        for b in range(4):
+            load(b).wait()
+            depth = width // 4
+            total = total + _nn(low[:, b * depth : (b + 1) * depth], w_part[b % 2].reshape(depth, width))
+            if b + 2 < 4:
+                load(b + 2).start()
+        hidden[...] = total
+        inverse = lax.rsqrt(jnp.mean(total * total, -1, keepdims=True) + EPSILON)
+        mlp_in[...] = (total * inverse * gains[1:2, :]).astype(BF)
+
+    plan.at(173, end)
+    plan.at(176, project)
     plan.run()
 
 
@@ -693,6 +711,7 @@
     outs = (
         jax.ShapeDtypeStruct((length, width), BF), jax.ShapeDtypeStruct((width, 384), BF),
         jax.ShapeDtypeStruct((8, width), F32), heads, heads, heads, jax.ShapeDtypeStruct((2, length), F32),
+        jax.ShapeDtypeStruct((rows, width), BF), jax.ShapeDtypeStruct((rows, width), F32),
         jax.ShapeDtypeStruct((rows, width), BF), block, block, block,
         jax.ShapeDtypeStruct((16, 2) + wo.shape, BF), jax.ShapeDtypeStruct((8, rows, width), BF),
     )
@@ -700,11 +719,11 @@
     scratch = [
         pltpu.VMEM((16, rows, width), BF), pltpu.VMEM((16, 2, wq.shape[0], 384), BF), pltpu.VMEM((16, 2) + tile.shape, BF),
         pltpu.VMEM((4 * rows, width), BF), *[pltpu.VMEM((32, 64, 128), BF)] * 4, pltpu.VMEM((16, rows, 128), BF),
-        DMA, DMA, DMA,
+        pltpu.VMEM((2, 4, 2) + wo.shape, BF), DMA, DMA, DMA, DMA((2,)),
     ]
     scratch += DEAL_SEMS * 4 + GATHER_SEMS + (DEAL8_SEMS + [DMA((4,))]) * 3 + GATHER_SEMS + GATHER8_SEMS + DEAL_SEMS
     return comm_call(
-        front_kernel, outs, [ANY] + [INNER] * 6 + [ANY] * 6, [smem] * 2 + [INNER] + [ANY] * 8 + [INNER] * 3, scratch, 0,
+        front_kernel, outs, [ANY] + [INNER] * 9 + [ANY] * 5, [smem] * 2 + [INNER] + [ANY] * 8 + [INNER] * 3, scratch, 0,
         "front", 58,
     )(order, table, x, wq, wk, wv, wg, wu, wd, wo, cot, tile, cos, sin)
 
@@ -890,20 +909,37 @@
     plan.at(t1, add)
 
 
-def back_kernel(order, table, ga, qs, ks, vs, lse, cos, sin, out_part, low, branch, sum_g, own_u, dqkv, out_sum, wo_sum, sum_u, g_home, *refs):
+def back_kernel(order, table, wo, qs, ks, vs, lse, cos, sin, out_part, low, branch, sum_g, own_u, dqkv, out_sum, wo_sum, sum_u, g_home, *refs):
     refs = list(refs)
-    gh, gs, dq, dk, dv, own, other, got = take(refs, 8)
+    ga, w_part, gh, gs, dq, dk, dv, own, other, got = take(refs, 10)
+    w_sems = take(refs, 1)[0]
     send, recv = take(refs, 2)
     gh_rows = gh.reshape(16, ga.shape[0], 128)
     flat = [g.reshape(qs.shape) for g in (dq, dk, dv)]
     h = Here()
+    depth = w_part.shape[1]
+
+    def load(b):
+        return pltpu.make_async_copy(wo.at[pl.ds(b * depth, depth)], w_part.at[b % 2], w_sems.at[b % 2])
+
+    load(0).start()
+    load(1).start()
     greet_all(h)
     plan = Plan()
-    deal16(plan, h, columns(ga, 128), lambda c: gh_rows.at[c], None, take(refs, 5), 0, 14, both=False)
+
+    def project():
+        for b in range(wo.shape[0] // depth):
+            load(b).wait()
+            ga[:, b * depth : (b + 1) * depth] = _nt(branch[...], w_part[b % 2]).astype(BF)
+            if b + 2 < wo.shape[0] // depth:
+                load(b + 2).start()
+
+    plan.at(0.5, project)
+    deal16(plan, h, columns(ga, 128), lambda c: gh_rows.at[c], None, take(refs, 5), 0.6, 14, both=False)
     gu_sems = take(refs, 3)
-    scatter8(plan, h, out_part, out_sum, take(refs, N_SCATTER8), (1, 18, 35, 52), (18.8, 35.8, 52.8, 69.8), 94)
+    scatter8(plan, h, out_part, out_sum, take(refs, N_SCATTER8), (0.1, 18, 35, 52), (18.8, 35.8, 52.8, 69.8), 94)
     outer_home(plan, h, low, branch, own, other, got, send, recv, 2, 8)
-    deal8(plan, h, lambda r: sum_g.at[r], columns_of(g_home, sum_g.shape[2]), gu_sems, 3, 198)
+    deal8(plan, h, lambda r: sum_g.at[r], columns_of(g_home, sum_g.shape[2]), gu_sems, 0.3, 198)
     half_u, u_sems = take(refs, 2)
     split_u = own_u.reshape(4, 2, 2, *own_u.shape[1:])
     over_u = remote(split_u.at[:, 1 - h.y], sum_u, u_sems.at[0], u_sems.at[1], ctx=h.yn)
@@ -920,7 +956,7 @@
             sum_u[z] = (sum_u[z].astype(F32) + half_u[z].astype(F32)).astype(BF)
         over_u.wait_send()
 
-    plan.at(2.5, start_u)
+    plan.at(0.2, start_u)
     plan.at(90, end_u)
     scatter16(plan, h, own.reshape(4, 2, 2, *own.shape[1:]), wo_sum, take(refs, N_SCATTER), 8.1, 18)
 
@@ -946,8 +982,8 @@
     plan.run()
 
 
-def back(order, table, ga, qs, ks, vs, lse, cos, sin, out_part, low, branch, sum_g, own_u):
-    rows, width = ga.shape
+def back(order, table, wo, qs, ks, vs, lse, cos, sin, out_part, low, branch, sum_g, own_u):
+    rows, width = low.shape
     length = qs.shape[0]
     smem = pl.BlockSpec(memory_space=pltpu.SMEM)
     half = pltpu.VMEM((16, width // 32, width), BF)
@@ -958,22 +994,23 @@
         jax.ShapeDtypeStruct((4, 2) + sum_g.shape[1:], BF),
         jax.ShapeDtypeStruct((sum_g.shape[1], 8 * sum_g.shape[2]), BF),
     )
-    scratch = [pltpu.VMEM((32, 64, 128), BF), pltpu.VMEM((length, 128), BF)]
-    scratch += [pltpu.VMEM((32, 64, 128), F32)] * 3 + [half] * 3 + [DMA] * 2 + DEAL_SEMS + DEAL8_SEMS
+    scratch = [pltpu.VMEM((rows, width), BF), pltpu.VMEM((2, width // 4, width), BF)]
+    scratch += [pltpu.VMEM((32, 64, 128), BF), pltpu.VMEM((length, 128), BF)]
+    scratch += [pltpu.VMEM((32, 64, 128), F32)] * 3 + [half] * 3 + [DMA((2,))] + [DMA] * 2 + DEAL_SEMS + DEAL8_SEMS
     scratch += scatter8_scratch(rows, width) + [pltpu.VMEM((4, 2) + sum_g.shape[1:], BF), DMA((3,))]
     scratch += scatter_scratch(width // 32, width)
-    return comm_call(back_kernel, outs, [INNER] * 4 + [ANY], [smem] * 2 + [INNER] * 10 + [ANY] * 2, scratch, 6, "back", 60)(
-        order, table, ga, qs, ks, vs, lse, cos, sin, out_part.reshape(4, 2, rows, width), low, branch, sum_g, own_u
+    return comm_call(back_kernel, outs, [INNER] * 4 + [ANY], [smem] * 2 + [ANY] + [INNER] * 9 + [ANY] * 2, scratch, 6, "back", 60)(
+        order, table, wo, qs, ks, vs, lse, cos, sin, out_part.reshape(4, 2, rows, width), low, branch, sum_g, own_u
     )
 
 
 def home_kernel(
-    dqkv, wqkv, normed, gd, gg, gu, x, grad_hidden, gain, other_gain,
-    input_grad, q_out, k_out, v_out, gains_out, d_out, g_out, u_out, *refs
+    dqkv, wqkv, normed, gd, gg, gu, x, grad_hidden, gain, wq, wk, wv, wg, wu,
+    input_grad, q_out, k_out, v_out, gain_a, gain_m, d_out, g_out, u_out, *refs
 ):
     refs = list(refs)
-    part, nm, own, other, got, landed, d32, g32, u16, u32, gn, gains, gains_got, gains_landed = take(refs, 14)
-    nm_sem, ex_sems, out_sems, gain_sems = take(refs, 4)
+    part, nm, own, other, got, landed, d32, g32, u16, u32, gn = take(refs, 11)
+    nm_sem, ex_sems, out_sems = take(refs, 3)
     rows, width = x.shape
     block = own.shape[1]
     h = Here()
@@ -981,7 +1018,7 @@
     load.start()
     greet_all(h)
     plan = Plan()
-    deal8(plan, h, lambda r: gu.at[r], columns_of(u16, gu.shape[2]), take(refs, 3), 0.4, 150)
+    deal8(plan, h, lambda r: gu.at[r], columns_of(u16, gu.shape[2]), take(refs, 3), 0.4, 90)
 
     def plane(k):
         zz = jnp.bitwise_xor(h.z, k)
@@ -1016,7 +1053,7 @@
         over.wait_send()
 
     plan.at(10, join)
-    deal16(plan, h, lambda c: own.at[c], lambda c: landed.at[c], None, take(refs, 5), 10.1, 151, both=False)
+    deal16(plan, h, lambda c: own.at[c], lambda c: landed.at[c], None, take(refs, 5), 10.1, 91, both=False)
     writes = [
         pltpu.make_async_copy(a, b, out_sems.at[i]) for i, (a, b) in enumerate(((d32, d_out), (g32, g_out), (u32, u_out)))
     ]
@@ -1027,80 +1064,56 @@
 
     plan.at(15, functools.partial(widen, 0, gd, d32))
     plan.at(25, functools.partial(widen, 1, gg, g32))
-    plan.at(152, functools.partial(widen, 2, u16, u32))
+    plan.at(92, functools.partial(widen, 2, u16, u32))
 
     def finish_qkv():
         for c in range(16):
             for i, out in enumerate((q_out, k_out, v_out)):
                 out[:, c * 128 : (c + 1) * 128] = landed[c, :, i * 128 : (i + 1) * 128].astype(F32)
 
-    plan.at(203, finish_qkv)
-    gain_over = remote(gains, gains_got, ex_sems.at[2], ex_sems.at[3], fsdp=1 - h.core)
-
-    def source():
+    def sums():
+        terms = ((wq, q_out), (wk, k_out), (wv, v_out))
+        gain_a[...] = sum(jnp.sum(w[...].astype(F32) * g[...], -1, keepdims=True) for w, g in terms)
+        terms = ((wg, g32), (wu, u32))
+        gain_m[...] = sum(jnp.sum(w[...].astype(F32) * g[...], -1, keepdims=True) for w, g in terms)
+
+    plan.at(93, finish_qkv)
+    plan.at(94, sums)
+
+    def result():
         value = x[...].astype(F32)
-        return value, lax.rsqrt(jnp.mean(value * value, -1, keepdims=True) + EPSILON)
-
-    def sums():
-        value, inverse = source()
-        gains[...] = jnp.zeros_like(gains)
-        total = jnp.sum(gn[...] * value * inverse, 0, keepdims=True)
-        for c in range(16):
-            at = slice(c * 128, (c + 1) * 128)
-            gains[c, 0:1] = total[:, at]
-            gains[c, 1:2] = other_gain[:, at]
-        gain_over.start()
-
-    def pass_on():
-        gain_over.wait_recv()
-        gain_over.wait_send()
-        gains[...] += gains_got[...]
-
-    def result():
-        value, inverse = source()
+        inverse = lax.rsqrt(jnp.mean(value * value, -1, keepdims=True) + EPSILON)
         scaled = gn[...] * gain[0:1, :]
         inner = jnp.sum(scaled * value, -1, keepdims=True)
         input_grad[...] = (
             grad_hidden[...] + inverse * scaled - inverse * inverse * inverse / width * value * inner
         )
 
-    plan.at(200, sums)
-    plan.at(201, pass_on)
-    deal16(plan, h, lambda c: gains.at[c], lambda c: gains_landed.at[c], None, take(refs, 5), 201.5, 204, both=False)
     plan.at(202, result)
-
-    def add():
-        total = gains_landed[0]
-        for c in range(1, 16):
-            total = total + gains_landed[c]
-        gains_out[...] = total
-        for w in writes:
-            w.wait()
-
-    plan.at(300, add)
+    plan.at(300, lambda: [w.wait() for w in writes])
     plan.run()
 
 
-def home(dqkv, wqkv, normed, gd, gg, gu, x, grad_hidden, gain, other_gain):
+def home(dqkv, wqkv, normed, gd, gg, gu, x, grad_hidden, gain, wq, wk, wv, wg, wu):
     rows, width = x.shape
     block, wide = gd.shape
     third = pltpu.VMEM((16, block, 384), BF)
-    tile = pltpu.VMEM((16, 8, 128), F32)
+    column = jax.ShapeDtypeStruct((block, 1), F32)
     wide32 = pltpu.VMEM((block, wide), F32)
     small = jax.ShapeDtypeStruct((block, width), F32)
     large = jax.ShapeDtypeStruct((block, wide), F32)
     outs = (
-        jax.ShapeDtypeStruct((rows, width), F32), small, small, small, jax.ShapeDtypeStruct((8, 128), F32), large, large, large
+        jax.ShapeDtypeStruct((rows, width), F32), small, small, small, column, column, large, large, large
     )
     scratch = [
         pltpu.VMEM((4, 2, 2, rows, width), BF), pltpu.VMEM(normed.shape, BF), third, third, third, third, wide32, wide32,
-        pltpu.VMEM((block, wide), BF), wide32, pltpu.VMEM((rows, width), F32), tile, tile, tile,
-        DMA, DMA((4,)), DMA((3,)), DMA,
+        pltpu.VMEM((block, wide), BF), wide32, pltpu.VMEM((rows, width), F32),
+        DMA, DMA((2,)), DMA((3,)),
     ]
-    scratch += DEAL8_SEMS + scatter_scratch(rows, width) + DEAL_SEMS * 2
+    scratch += DEAL8_SEMS + scatter_scratch(rows, width) + DEAL_SEMS
     return comm_call(
-        home_kernel, outs, [INNER] * 5 + [ANY] * 3, [INNER, INNER, ANY, INNER, INNER, ANY] + [INNER] * 4, scratch, 7, "home", 60
-    )(dqkv, wqkv, normed, gd, gg, gu, x, grad_hidden, gain, other_gain)
+        home_kernel, outs, [INNER] * 6 + [ANY] * 3, [INNER, INNER, ANY, INNER, INNER, ANY] + [INNER] * 8, scratch, 7, "home", 60
+    )(dqkv, wqkv, normed, gd, gg, gu, x, grad_hidden, gain, wq, wk, wv, wg, wu)
 
 
 def rope_tables(positions):
@@ -1138,35 +1151,31 @@
     lane = jnp.arange(128) // 64
     tile = jnp.where(lane[None] == core, jnp.tile(jnp.stack([attn_gain, mlp_gain]), (1, 2)), 0)
     tile = jnp.pad(tile, ((0, 14), (0, 0)))
-    normed, wqkv, gains, qs, ks, vs, lse, attn_low, bg, bu, bd, full_out, cot_all = front(
+    normed, wqkv, gains, qs, ks, vs, lse, attn_low, hidden, mlp_in, bg, bu, bd, full_out, cot_all = front(
         order, table, x, wq, wk, wv, wg, wu, wd, wo, cot, tile, cos, sin
     )
     again, mgain = gains[0], gains[1]
     full_out = full_out.reshape(width, width)
-    own = x.astype(F32)
-    inv_in = lax.rsqrt(jnp.mean(own * own, -1, keepdims=True) + EPSILON)
-    hidden = own + dot(attn_low, full_out)
     inv_mid = lax.rsqrt(jnp.mean(hidden * hidden, -1, keepdims=True) + EPSILON)
-    gmi, out_part, sum_g, own_u, gd = mlp((hidden * inv_mid * mgain).astype(BF), cot_all, bg, bu, bd)
+    gmi, out_part, sum_g, own_u, gd = mlp(mlp_in, cot_all, bg, bu, bd)
 
     def norm_back(grad, source, inv, gain):
         scaled = grad * gain
         inner = jnp.sum(scaled * source, -1, keepdims=True)
         return inv * scaled - inv * inv * inv / width * source * inner
 
-    mgain_part = jnp.sum(gmi * hidden * inv_mid, 0)
     grad_hidden = cot.astype(F32) + norm_back(gmi, hidden, inv_mid, mgain)
     grad_branch = grad_hidden.astype(BF)
-    grad_att = dot_nt(grad_branch, full_out).astype(BF)
     grad_qkv, out_sum, wo_grad, sum_u, gg = back(
-        order, table, grad_att, qs, ks, vs, lse, cos, sin, out_part, attn_low, grad_branch, sum_g, own_u
+        order, table, full_out, qs, ks, vs, lse, cos, sin, out_part, attn_low, grad_branch, sum_g, own_u
     )
     layer_output = (hidden + out_sum).astype(BF)
-    input_grad, gq, gk, gv, both, gd, gg, gu = home(
-        grad_qkv, wqkv, normed, gd, gg, sum_u.reshape(sum_g.shape), x, grad_hidden, gains, mgain_part[None]
-    )
-    gains = lax.dynamic_slice_in_dim(both, core * 64, 64, 1)
-    return (layer_output[None], input_grad[None], gains[0], gq, gk, gv, wo_grad, gains[1], gg, gu, gd)
+    input_grad, gq, gk, gv, gain_a, gain_m, gd, gg, gu = home(
+        grad_qkv, wqkv, normed, gd, gg, sum_u.reshape(sum_g.shape), x, grad_hidden, gains, wq, wk, wv, wg, wu
+    )
+    gain_a = gain_a[:, 0] / attn_gain.astype(F32)
+    gain_m = gain_m[:, 0] / mlp_gain.astype(F32)
+    return (layer_output[None], input_grad[None], gain_a, gq, gk, gv, wo_grad, gain_m, gg, gu, gd)
 
 
 MASKED = -1e30

time: 682 us -> 668 us (0.979)
  matrix products: 12.2 us -> 0 us
    dot_general x2 -> x0, matrix products: 12.2 us -> none  [the longest x1 7.25 us: dot_nt(): lax.dot_general(a, b, (((1,), (1,)), ((), ())), preferred_element_type=F32)]
where the time goes in v4:
time: 668 us; the launch traced here: 658 us
  Pallas kernels  633 us (95%)
  local copies, waits for them, and re-layouts  14.6 us (2%)
  other arithmetic  8.97 us (1%)
    pallas_call x1, Pallas kernels, front(): comm_call(front_kernel, outs, [ANY] + [INNER] * 9 + [ANY] * 5, [smem] * 2...  244 us
    pallas_call x1, Pallas kernels, mlp(): comm_call(mlp_kernel, outs, [INNER, ANY, INNER, INNER, ANY], [ANY] * 5, s...  143 us
    pallas_call x1, Pallas kernels, back(): comm_call(back_kernel, outs, [INNER] * 4 + [ANY], [smem] * 2 + [ANY] + [I...  132 us
    pallas_call x1, Pallas kernels, home(): comm_call(home_kernel, outs, [INNER] * 6 + [ANY] * 3, [INNER, INNER, ANY,...  114 us

profile of v4, /device:TPU:9, one launch (start us, length us, event | category | flops | bytes accessed | tf_op | source)
XLA Modules:
  0.0 657.9 jit_solution(1188462464717304609)
XLA Ops:
  0.6 0.8 copy.28
  1.4 0.1 eq.28.table
  1.7 1.0 multiply_sine_fusion
  2.7 0.1 tile.31
  2.8 0.3 copy.29
  3.1 1.0 broadcast_multiply_fusion.sin
  4.2 0.1 tile.14
  4.3 1.3 copy.30.cos
  5.6 0.6 select_reduce_fusion.order
  6.2 0.1 tile.13
  6.3 0.6 pad.4.tile
  6.9 244.3 %front.1 = (bf16[2048,2048]{1,0:T(8,128)(2,1)}, bf16[2048,384]{1,0:T(8,128)(2,1)}, f32[8,2048]{1,0:T(8,128)}, bf16[2048,128]{1,0:T(8,128)(2,1)}, bf16[2048,128]{...) custom-call(s32[32]{0:T(128)} %select_reduce_fusion.order, ...), custom_call_target="tpu_custom_call" | custom-call | tf_op jit(solution)/shard_map/front/pallas_call | solution.py:725
  251.3 142.8 %mlp.1 = (f32[128,2048]{1,0:T(8,128)}, bf16[8,128,2048]{2,1,0:T(8,128)(2,1)}, bf16[8,64,1024]{2,1,0:T(8,128)(2,1)}, bf16[16,64,1024]{2,1,0:T(8,128)(2,1)}, bf16[64,8192]{1,0:T(8,128)(2,1)}) custom-call(bf16[128,2048]{1,0:T(8,128)(2,1)} %get-tuple-element.51.src, bf16[8,128,2048]{2,1,0:T(8,128)(2,1)} %get-tuple-element.52.cot, bf16[2048,1024]{1,0:T(8,128)(2,1)} %bitcast.22, ...), custom_call_target="tpu_custom_call" | custom-call | tf_op jit(solution)/shard_map/mlp/pallas_call | solution.py:884
  394.1 1.0 slice.3
  395.1 1.5 multiply_reduce_fusion.1
  396.6 1.5 fusion.3
  398.1 132.1 %back.1 = (bf16[2048,384]{1,0:T(8,128)(2,1)}, f32[128,2048]{1,0:T(8,128)}, f32[64,2048]{1,0:T(8,128)}, bf16[4,2,64,1024]{3,2,1,0:T(8,128)(2,1)}, bf16[64,8192]{1,0:T(8,128)(2,1)}) custom-call(s32[32]{0:T(128)} %select_reduce_fusion.order, s32[32]{0:T(128)} %copy-done.12, bf16[2048,2048]{1,0:T(8,128)(2,1)} %bitcast.18, ...), custom_call_target="tpu_custom_call" | custom-call | tf_op jit(solution)/shard_map/back/pallas_call | solution.py:1002
  530.2 114.1 %home.1 = (f32[128,2048]{1,0:T(8,128)}, f32[64,2048]{1,0:T(8,128)}, f32[64,2048]{1,0:T(8,128)}, f32[64,2048]{1,0:T(8,128)}, f32[64,1]{1,0:T(8,128)}, /*index=5*/...) custom-call(bf16[2048,384]{1,0:T(8,128)(2,1)} %get-tuple-element.63.dqkv, ...), custom_call_target="tpu_custom_call" | custom-call | tf_op jit(solution)/shard_map/home/pallas_call | solution.py:1114
  644.4 0.9 reduce
  645.2 0.9 reduce.1
  646.1 0.5 convert_divide_fusion
  646.6 0.9 fusion
  647.6 1.0 copy.40
  648.5 0.8 copy.41
  649.3 0.8 copy.42
  650.1 0.8 copy.43
  650.9 0.8 copy.44
  651.7 1.3 copy.45
  653.0 1.0 copy-done.4
  654.1 1.3 copy.46
  655.4 1.0 copy-done.3
  656.4 1.3 copy.47
  (38 shorter events, 0.3 us)
Async XLA Ops:
  1.5 4.1 copy-start.12
  4.2 2.1 copy-start.13
  4.2 2.1 copy-start.14
  251.3 143.8 %copy-start = (f32[128,2048]{1,0:T(8,128)S(1)}, f32[128,2048]{1,0:T(8,128)}, u32[]{:S(2)}) copy-start(f32[128,2048]{1,0:T(8,128)} %get-tuple-element.45) | copy-start | bytes 3145732
  394.1 2.5 copy-start.1
  394.1 2.5 copy-start.2
  530.2 116.4 %copy-start.6 = (f32[128,2048]{1,0:T(8,128)S(1)}, f32[128,2048]{1,0:T(8,128)}, u32[]{:S(2)}) copy-start(f32[128,2048]{1,0:T(8,128)} %get-tuple-element.62) | copy-start | bytes 3145732
  646.1 1.4 copy-start.7
  646.6 1.9 copy-start.11
  647.6 1.8 copy-start.10
  647.6 2.6 copy-start.9
  648.5 2.4 copy-start.8
  648.5 3.2 copy-start.5
  651.7 2.3 copy-start.4
  654.1 2.3 copy-start.3

commit v5 on v4

--- a/solution.py
+++ b/solution.py
@@ -731,7 +731,7 @@
 def mlp_kernel(src, cot, bg, bu, bd, gmi, out_part, sum_g, own_u, d_home, *refs):
     refs = list(refs)
     xm, ct, wg, wu, wd, grads, act, part, stage, cols = take(refs, 10)
-    own_g, other_gu, got_gu, own_d, other_d, got_d, sum_d = take(refs, 7)
+    own_g, other_g, got_g, other_u, got_u, own_d, other_d, got_d, sum_d = take(refs, 9)
     w_sem, ct_sem, cols_sem, stage_sem, ex_sems = take(refs, 5)
     rows, width = src.shape
     hidden = wg.shape[1]
@@ -787,25 +787,24 @@
     plan.at(55, lambda: put_out(3).wait())
     scatter8(plan, h, part, gmi, take(refs, N_SCATTER8), (27, 39, 50.2, 50.3), (50.4, 58.5, 66.5, 75), 110)
 
-    def split(c, both, own, other, lanes):
+    def split(c, both, own, other):
         both = both.astype(BF).reshape(2, block, both.shape[1])
         own[c] = jnp.where(h.core == 0, both[0], both[1])
-        other[c, :, lanes] = jnp.where(h.core == 0, both[1], both[0])
+        other[c] = jnp.where(h.core == 0, both[1], both[0])
 
     def exchange(i, other, got):
-        return remote(other, got, ex_sems.at[i], ex_sems.at[2 + i], fsdp=1 - h.core)
+        return remote(other, got, ex_sems.at[i], ex_sems.at[3 + i], fsdp=1 - h.core)
 
     def load_cols(c):
         slot = lax.rem(c, 2)
         at = pl.ds(pl.multiple_of(c * 2 * block, 128), 2 * block)
         return pltpu.make_async_copy(cot.at[:, :, at], cols.at[slot], cols_sem.at[slot])
 
-    def grads_gu(first):
+    def grads_up(first, lanes, own, other):
         def one(c, carry):
             at = pl.ds(pl.multiple_of(c * 2 * block, 128), 2 * block)
             lhs = xm[:, :, at].reshape(8 * rows, 2 * block)
-            split(c, _tn(lhs, grads[:, :hidden]), own_g, other_gu, pl.ds(0, hidden))
-            split(c, _tn(lhs, grads[:, hidden:]), own_u, other_gu, pl.ds(hidden, hidden))
+            split(c, _tn(lhs, grads[:, lanes]), own, other)
             return carry
 
         lax.fori_loop(first, first + 4, one, 0)
@@ -815,24 +814,26 @@
             pl.when(c < 15)(lambda: load_cols(c + 1).start())
             load_cols(c).wait()
             lhs = cols[lax.rem(c, 2)].reshape(8 * rows, 2 * block)
-            split(c, _tn(lhs, act[...]), own_d, other_d, pl.ds(0, hidden))
+            split(c, _tn(lhs, act[...]), own_d, other_d)
             return carry
 
         lax.fori_loop(first, first + 4, one, 0)
 
     def over_y(i, own, result):
         own, result = own.reshape(4, 2, 2, *own.shape[1:]), result.reshape(4, 2, *own.shape[1:])
-        return remote(own.at[:, 1 - h.y], result, ex_sems.at[4 + i], ex_sems.at[6 + i], ctx=h.yn)
+        return remote(own.at[:, 1 - h.y], result, ex_sems.at[6 + i], ex_sems.at[8 + i], ctx=h.yn)
 
     def join(i, own, other, got, result):
         exchange(i, other, got).wait_recv()
         for c in range(16):
-            own[c] = (own[c].astype(F32) + got[c, :, 0:hidden].astype(F32)).astype(BF)
+            own[c] = (own[c].astype(F32) + got[c].astype(F32)).astype(BF)
         over_y(i, own, result).start()
 
     def join_u():
+        exchange(2, other_u, got_u).wait_recv()
         for c in range(16):
-            own_u[c] = (own_u[c].astype(F32) + got_gu[c, :, hidden:].astype(F32)).astype(BF)
+            own_u[c] = (own_u[c].astype(F32) + got_u[c].astype(F32)).astype(BF)
+        exchange(2, other_u, got_u).wait_send()
 
     def add_y(i, own, other, got, result):
         over_y(i, own, result).wait_recv()
@@ -845,16 +846,19 @@
         exchange(i, other, got).wait_send()
         over_y(i, own, result).wait_send()
 
-    d, g = (own_d, other_d, got_d, sum_d), (own_g, other_gu, got_gu, sum_g)
+    d, g = (own_d, other_d, got_d, sum_d), (own_g, other_g, got_g, sum_g)
+    lo, hi = slice(0, hidden), slice(hidden, 2 * hidden)
     plan.at(50.5, lambda: load_cols(0).start())
     for i in range(4):
         plan.at(56 + 2 * i, functools.partial(grads_d, 4 * i))
-        plan.at(68 + 3 * i, functools.partial(grads_gu, 4 * i))
+        plan.at(65 + 2 * i, functools.partial(grads_up, 4 * i, lo, own_g, other_g))
+        plan.at(75 + 2 * i, functools.partial(grads_up, 4 * i, hi, own_u, other_u))
     plan.at(64, lambda: exchange(1, other_d, got_d).start())
-    plan.at(68.5, lambda: join(1, *d))
-    plan.at(82, lambda: exchange(0, other_gu, got_gu).start())
-    plan.at(86, lambda: join(0, *g))
-    plan.at(86.5, join_u)
+    plan.at(68, lambda: join(1, *d))
+    plan.at(73, lambda: exchange(0, other_g, got_g).start())
+    plan.at(78, lambda: join(0, *g))
+    plan.at(83, lambda: exchange(2, other_u, got_u).start())
+    plan.at(87, join_u)
     plan.at(90, lambda: add_y(1, *d))
     deal8(plan, h, lambda r: sum_d.at[r], columns_of(d_home, hidden), take(refs, 3), 90.1, 200)
     plan.at(112, lambda: add_y(0, *g))
@@ -866,14 +870,14 @@
     rows, width = src.shape
     block, hidden = bg.shape[4:]
     full = pltpu.VMEM((width, hidden), BF)
-    gu, d = pltpu.VMEM((16, block, 2 * hidden), BF), pltpu.VMEM((16, block, hidden), BF)
+    d = pltpu.VMEM((16, block, hidden), BF)
     scratch = [
         pltpu.VMEM((8, rows, width), BF), pltpu.VMEM((2, 2, rows, width), BF), full, full, full,
         pltpu.VMEM((8 * rows, 2 * hidden), BF), pltpu.VMEM((8 * rows, hidden), BF),
         pltpu.VMEM((4, 2, rows, width), BF), pltpu.VMEM((2, rows, width), BF),
-        pltpu.VMEM((2, 8, rows, 2 * block), BF), d, gu, gu, d, d, d,
+        pltpu.VMEM((2, 8, rows, 2 * block), BF), *[d] * 8,
         pltpu.VMEM((8, block, hidden), BF),
-        DMA((3,)), DMA((2,)), DMA((2,)), DMA, DMA((8,)),
+        DMA((3,)), DMA((2,)), DMA((2,)), DMA, DMA((10,)),
     ]
     scratch += GATHER8_SEMS + scatter8_scratch(rows, width) + DEAL8_SEMS
     outs = (
@@ -937,7 +941,7 @@
     plan.at(0.5, project)
     deal16(plan, h, columns(ga, 128), lambda c: gh_rows.at[c], None, take(refs, 5), 0.6, 14, both=False)
     gu_sems = take(refs, 3)
-    scatter8(plan, h, out_part, out_sum, take(refs, N_SCATTER8), (0.1, 18, 35, 52), (18.8, 35.8, 52.8, 69.8), 94)
+    scatter8(plan, h, out_part, out_sum, take(refs, N_SCATTER8), (0.1, 15.6, 27, 40), (15.4, 27.1, 38.8, 50.8), 94)
     outer_home(plan, h, low, branch, own, other, got, send, recv, 2, 8)
     deal8(plan, h, lambda r: sum_g.at[r], columns_of(g_home, sum_g.shape[2]), gu_sems, 0.3, 198)
     half_u, u_sems = take(refs, 2)

time: 668 us -> 661 us (0.990)
  Pallas kernels: 633 us -> 625 us
    pallas_call x1, Pallas kernels: 132 us -> 124 us  [back(): comm_call(back_kernel, outs, [INNER] * 4 + [ANY], [smem] * 2 + [ANY] + [I...]
where the time goes in v5:
time: 661 us; the launch traced here: 650 us
  Pallas kernels  625 us (95%)
  local copies, waits for them, and re-layouts  14.6 us (2%)
  other arithmetic  8.97 us (1%)
    pallas_call x1, Pallas kernels, front(): comm_call(front_kernel, outs, [ANY] + [INNER] * 9 + [ANY] * 5, [smem] * 2...  244 us
    pallas_call x1, Pallas kernels, mlp(): comm_call(mlp_kernel, outs, [INNER, ANY, INNER, INNER, ANY], [ANY] * 5, s...  143 us
    pallas_call x1, Pallas kernels, back(): comm_call(back_kernel, outs, [INNER] * 4 + [ANY], [smem] * 2 + [ANY] + [I...  124 us
    pallas_call x1, Pallas kernels, home(): comm_call(home_kernel, outs, [INNER] * 6 + [ANY] * 3, [INNER, INNER, ANY,...  114 us

profile of v5, /device:TPU:9, one launch (start us, length us, event | category | flops | bytes accessed | tf_op | source)
XLA Modules:
  0.0 650.0 jit_solution(13899737557718451893)
XLA Ops:
  0.6 0.8 copy.28
  1.4 0.1 eq.28.table
  1.7 1.0 multiply_sine_fusion
  2.7 0.1 tile.31
  2.8 0.3 copy.29
  3.1 1.0 broadcast_multiply_fusion.sin
  4.2 0.1 tile.14
  4.3 1.3 copy.30.cos
  5.6 0.6 select_reduce_fusion.order
  6.2 0.1 tile.13
  6.3 0.6 pad.4.tile
  6.9 244.3 %front.1 = (bf16[2048,2048]{1,0:T(8,128)(2,1)}, bf16[2048,384]{1,0:T(8,128)(2,1)}, f32[8,2048]{1,0:T(8,128)}, bf16[2048,128]{1,0:T(8,128)(2,1)}, bf16[2048,128]{...) custom-call(s32[32]{0:T(128)} %select_reduce_fusion.order, ...), custom_call_target="tpu_custom_call" | custom-call | tf_op jit(solution)/shard_map/front/pallas_call | solution.py:725
  251.3 142.8 %mlp.1 = (f32[128,2048]{1,0:T(8,128)}, bf16[8,128,2048]{2,1,0:T(8,128)(2,1)}, bf16[8,64,1024]{2,1,0:T(8,128)(2,1)}, bf16[16,64,1024]{2,1,0:T(8,128)(2,1)}, bf16[64,8192]{1,0:T(8,128)(2,1)}) custom-call(bf16[128,2048]{1,0:T(8,128)(2,1)} %get-tuple-element.51.src, bf16[8,128,2048]{2,1,0:T(8,128)(2,1)} %get-tuple-element.52.cot, bf16[2048,1024]{1,0:T(8,128)(2,1)} %bitcast.22, ...), custom_call_target="tpu_custom_call" | custom-call | tf_op jit(solution)/shard_map/mlp/pallas_call | solution.py:888
  394.1 1.0 slice.3
  395.1 1.5 multiply_reduce_fusion.1
  396.6 1.5 fusion.3
  398.1 124.2 %back.1 = (bf16[2048,384]{1,0:T(8,128)(2,1)}, f32[128,2048]{1,0:T(8,128)}, f32[64,2048]{1,0:T(8,128)}, bf16[4,2,64,1024]{3,2,1,0:T(8,128)(2,1)}, bf16[64,8192]{1,0:T(8,128)(2,1)}) custom-call(s32[32]{0:T(128)} %select_reduce_fusion.order, s32[32]{0:T(128)} %copy-done.12, bf16[2048,2048]{1,0:T(8,128)(2,1)} %bitcast.18, ...), custom_call_target="tpu_custom_call" | custom-call | tf_op jit(solution)/shard_map/back/pallas_call | solution.py:1006
  522.3 114.1 %home.1 = (f32[128,2048]{1,0:T(8,128)}, f32[64,2048]{1,0:T(8,128)}, f32[64,2048]{1,0:T(8,128)}, f32[64,2048]{1,0:T(8,128)}, f32[64,1]{1,0:T(8,128)}, /*index=5*/...) custom-call(bf16[2048,384]{1,0:T(8,128)(2,1)} %get-tuple-element.63.dqkv, ...), custom_call_target="tpu_custom_call" | custom-call | tf_op jit(solution)/shard_map/home/pallas_call | solution.py:1118
  636.5 0.9 reduce
  637.3 0.9 reduce.1
  638.2 0.5 convert_divide_fusion
  638.7 0.9 fusion
  639.7 1.0 copy.40
  640.6 0.8 copy.41
  641.4 0.8 copy.42
  642.2 0.8 copy.43
  643.0 0.8 copy.44
  643.8 1.3 copy.45
  645.1 1.0 copy-done.4
  646.2 1.3 copy.46
  647.5 1.0 copy-done.3
  648.5 1.3 copy.47
  (38 shorter events, 0.3 us)
Async XLA Ops:
  1.5 4.1 copy-start.12
  4.2 2.1 copy-start.13
  4.2 2.1 copy-start.14
  251.3 143.8 %copy-start = (f32[128,2048]{1,0:T(8,128)S(1)}, f32[128,2048]{1,0:T(8,128)}, u32[]{:S(2)}) copy-start(f32[128,2048]{1,0:T(8,128)} %get-tuple-element.45) | copy-start | bytes 3145732
  394.1 2.5 copy-start.1
  394.1 2.5 copy-start.2
  522.3 116.4 %copy-start.6 = (f32[128,2048]{1,0:T(8,128)S(1)}, f32[128,2048]{1,0:T(8,128)}, u32[]{:S(2)}) copy-start(f32[128,2048]{1,0:T(8,128)} %get-tuple-element.62) | copy-start | bytes 3145732
  638.2 1.4 copy-start.7
  638.7 1.9 copy-start.11
  639.6 1.8 copy-start.10
  639.6 2.6 copy-start.9
  640.6 2.4 copy-start.8
  640.6 3.2 copy-start.5
  643.8 2.3 copy-start.4
  646.2 2.3 copy-start.3
